TPU v7x, 32 devices: a whole 2x2x4 slice. The times are simulated.
32 devices in a mesh: ctx: 8 (over z, x), head: 4 (over y, core).
Axes of the slice: x: 2, y: 2, z: 4, core: 2. Of those that a mesh axis runs over, the one named last changes fastest.
Arguments:
- query_raw: bfloat16 [16384, 2048], P(('ctx', 'head')), may hold values from -6 to 6
- key_raw: bfloat16 [16384, 2048], P(('ctx', 'head')), may hold values from -6 to 6
- values: bfloat16 [16384, 4096], P(('ctx', 'head')), may hold values from -48 to 48
- in_gate: bfloat16 [16384, 8], P(('ctx', 'head')), may hold values from -10 to 130
- forget_gate: bfloat16 [16384, 8], P(('ctx', 'head')), may hold values from -1 to 16
- query_conv: bfloat16 [4, 2048], replicated, may hold values from -3 to 3
- key_conv: bfloat16 [4, 2048], replicated, may hold values from -3 to 3
Outputs:
- hidden_out: bfloat16 [16384, 4096], P(('ctx', 'head'))
All inputs are finite; a program needn't handle non-finite values.
Results may differ from a plain program's by a relative error of at most 0.0052.
Values may be sent and summed in bfloat16 or wider, within the bound.
No kernel may reach another device: no remote copies, remote signals or barrier semaphores. Data moves between devices by JAX's collectives and lax.ppermute only.
A program may use at most 192 MiB of HBM per device.

v0:
```python
import functools

import jax
import jax.numpy as jnp
from jax import lax
from jax.experimental import pallas as pl
from jax.experimental.pallas import tpu as pltpu
from jax.sharding import PartitionSpec as P

AXES = ("ctx", "head")
HEADS = 8
CHAINS = 1
GROUP = HEADS // 2
LOCAL = GROUP // CHAINS
OWNERS = 8
DK = 256
DV = 512
WIDTH = LOCAL * DV // OWNERS
PIECES = DV // WIDTH
SPLIT = DK // WIDTH
AUX = 16
ROWS = DK + AUX
BLK = 512
TAPS = 4
TILE = 256
STEP = 128
EMPTY = -1e30
SCALE = DK**-0.5
F32 = jnp.float32
BF16 = jnp.bfloat16
NUM = BF16
NT = (((1,), (1,)), ((), ()))


def narrow(x):
    return x.astype(BF16).astype(F32)


def split3(x):
    top = narrow(x)
    middle = narrow(x - top)
    return [top, middle, x - top - middle]


def aux_rows(norms, top, decay):
    parts = []
    for norm in norms:
        high = narrow(norm)
        parts += [high, norm - high]
    parts += split3(top) + split3(decay)
    row = lax.broadcasted_iota(jnp.int32, (AUX, WIDTH), 0)
    out = jnp.zeros((AUX, WIDTH), F32)
    for index, part in enumerate(parts):
        out = jnp.where(row == index, part, out)
    return out.astype(BF16)


def read_aux(aux):
    aux = aux.astype(F32)
    norms = [aux[2 * k : 2 * k + 1] + aux[2 * k + 1 : 2 * k + 2] for k in range(SPLIT)]
    at = 2 * SPLIT
    top = aux[at : at + 1] + aux[at + 1 : at + 2] + aux[at + 2 : at + 3]
    decay = aux[at + 3 : at + 4] + aux[at + 4 : at + 5] + aux[at + 5 : at + 6]
    return norms, top, decay


def dot_norm(aux, query):
    out = None
    for k in range(SPLIT):
        part = lax.dot_general(
            aux, query[:, k * WIDTH : (k + 1) * WIDTH], NT, preferred_element_type=F32
        )
        part = part[2 * k : 2 * k + 1] + part[2 * k + 1 : 2 * k + 2]
        out = part if out is None else out + part
    return out


def column(row):
    return jnp.broadcast_to(row, (128, row.shape[1])).T


def widen(col, width):
    return jnp.concatenate([col] * (width // 128), axis=1)


def place():
    me = lax.axis_index("ctx") * lax.axis_size("head") + lax.axis_index("head")
    return me % 2, me // (2 * OWNERS)


def first_head(mine, chain):
    core, _ = place()
    return GROUP * (core if mine else 1 - core) + LOCAL * chain


def span(index, width):
    return pl.ds(pl.multiple_of(index * width, width), width)


VMEM_SPEC = pl.BlockSpec(memory_space=pltpu.VMEM)


def on_chip(kernel, operands, shapes, scratch=(), name=None, flops=0, size=1 << 20):
    many = isinstance(shapes, list)
    kept = [pltpu.with_memory_space_constraint(x, pltpu.VMEM) for x in operands]
    out = [pltpu.VMEM(shape, dtype) for shape, dtype in (shapes if many else [shapes])]
    results = pl.pallas_call(
        kernel,
        in_specs=[VMEM_SPEC] * len(kept),
        out_specs=[VMEM_SPEC] * len(out),
        out_shape=out,
        scratch_shapes=list(scratch),
        name=name,
        cost_estimate=pl.CostEstimate(flops=flops, transcendentals=0, bytes_accessed=size),
        compiler_params=pltpu.CompilerParams(vmem_limit_bytes=8 << 20),
    )(*kept)
    return results if many else results[0]


def tails_kernel(key_hbm, query_hbm, out_ref, sems):
    width = key_hbm.shape[1]
    last = pl.ds(BLK - AUX, AUX)
    for copy in start_all(
        [
            pltpu.make_async_copy(key_hbm.at[last], out_ref.at[:, 0:width], sems.at[0]),
            pltpu.make_async_copy(query_hbm.at[last], out_ref.at[:, width : 2 * width], sems.at[1]),
        ]
    ):
        copy.wait()


def tails_call(key_raw, query_raw):
    return kernel_call(
        tails_kernel,
        [("hbm", key_raw), ("hbm", query_raw)],
        [("vmem", (AUX, 2 * key_raw.shape[1]), BF16)],
        [pltpu.SemaphoreType.DMA((2,))],
        "tails",
        0,
        1 << 17,
    )[0]


def prepare_kernel(in_hbm, forget_hbm, key_hbm, tap_hbm, val_hbm, rows_ref, key_ref, tap_ref, val_ref, gate_buf, sems):
    gates_in = start_all(
        [
            pltpu.make_async_copy(in_hbm, gate_buf.at[0], sems.at[0]),
            pltpu.make_async_copy(forget_hbm, gate_buf.at[1], sems.at[1]),
        ]
    )
    loads = start_all(
        [
            pltpu.make_async_copy(key_hbm, key_ref, sems.at[2]),
            pltpu.make_async_copy(tap_hbm, tap_ref, sems.at[3]),
            pltpu.make_async_copy(val_hbm, val_ref, sems.at[4]),
        ]
    )
    for copy in gates_in:
        copy.wait()
    gate = gate_buf[0].astype(F32)
    forget = gate_buf[1].astype(F32)
    log_forget = jnp.minimum(forget, 0.0) - jnp.log1p(jnp.exp(-jnp.abs(forget)))
    lane = lax.broadcasted_iota(jnp.int32, (HEADS, BLK), 1)
    total = log_forget
    shift = 1
    while shift < BLK:
        total = total + jnp.where(lane >= shift, pltpu.roll(total, shift, 1), 0.0)
        shift *= 2
    level = gate - total
    top = level
    shift = 1
    while shift < BLK:
        top = jnp.maximum(top, jnp.where(lane >= shift, pltpu.roll(top, shift, 1), -jnp.inf))
        shift *= 2
    last_top = top[:, BLK - 1 :]
    last_total = total[:, BLK - 1 :]
    out = (
        level,
        top,
        jnp.exp(level - last_top),
        jnp.broadcast_to(last_total + last_top, (HEADS, BLK)),
        jnp.broadcast_to(last_total, (HEADS, BLK)),
    )
    for index, part in enumerate(out):
        rows_ref[index * HEADS : (index + 1) * HEADS] = part
    for copy in loads:
        copy.wait()


def prepare_call(in_gate, forget_gate, key_raw, key_conv, values):
    return kernel_call(
        prepare_kernel,
        [("hbm", in_gate.T), ("hbm", forget_gate.T), ("hbm", key_raw), ("hbm", key_conv), ("hbm", values)],
        [
            ("vmem", (5 * HEADS, BLK), F32),
            ("vmem", key_raw.shape, BF16),
            ("vmem", key_conv.shape, BF16),
            ("vmem", values.shape, BF16),
        ],
        [pltpu.VMEM((2, HEADS, BLK), BF16), pltpu.SemaphoreType.DMA((5,))],
        "prepare",
        0,
        6 << 20,
    )


def row_of(rows_ref, kind, head):
    return rows_ref[pl.ds(kind * HEADS + head, 1), :]


PADDED = pltpu.VMEM((BLK + 8, DK), F32)
HBM_SPEC = pl.BlockSpec(memory_space=pltpu.HBM)
LIMIT = 20 << 20


def kernel_call(kernel, inputs, outputs, scratch, name, flops, size):
    in_specs, operands = [], []
    for where, x in inputs:
        operands.append(pltpu.with_memory_space_constraint(x, pltpu.VMEM if where == "vmem" else pltpu.HBM))
        in_specs.append(VMEM_SPEC if where == "vmem" else HBM_SPEC)
    return pl.pallas_call(
        kernel,
        in_specs=in_specs,
        out_specs=[VMEM_SPEC if where == "vmem" else HBM_SPEC for where, _, _ in outputs],
        out_shape=[
            (pltpu.VMEM if where == "vmem" else pltpu.HBM)(shape, dtype)
            for where, shape, dtype in outputs
        ],
        scratch_shapes=scratch,
        name=name,
        cost_estimate=pl.CostEstimate(flops=flops, transcendentals=0, bytes_accessed=size),
        compiler_params=pltpu.CompilerParams(vmem_limit_bytes=LIMIT),
    )(*operands)


def conv_rows(columns, rim_columns, raw, rim_ref, tap_ref, padded):
    padded[0:8] = rim_ref[:, rim_columns].astype(F32)[8:16]
    padded[8 : 8 + BLK] = raw.astype(F32)
    taps = tap_ref[:, columns].astype(F32)
    for start in range(0, BLK, STEP):
        first = 8 - (TAPS - 1) + start
        mixed = taps[0:1] * padded[first : first + STEP]
        for tap in range(1, TAPS):
            mixed = mixed + taps[tap : tap + 1] * padded[first + tap : first + tap + STEP]
        yield start, (mixed * (0.5 * jnp.tanh(0.5 * mixed) + 0.5)).astype(BF16)


def start_all(copies):
    for copy in copies:
        copy.start()
    return copies


def state_kernel(mine, chain, raw_ref, rim_ref, tap_ref, val_ref, rows_ref, rec_ref, act_hbm, act_buf, padded, weighted, sems):
    head0 = first_head(mine, chain)
    act_out = []
    for local in range(LOCAL):
        head = head0 + local
        weight = column(row_of(rows_ref, 2, head))
        norm = jnp.zeros((1, DK), F32)
        columns = span(head, DK)
        for start, act in conv_rows(columns, columns, raw_ref[:, columns], rim_ref, tap_ref, padded.at[local % 2]):
            act_buf[local, start : start + STEP] = act
            scaled = act.astype(F32) * widen(weight[start : start + STEP], DK)
            norm = norm + jnp.sum(scaled, axis=0, keepdims=True)
            weighted[local % 2, start : start + STEP] = scaled.astype(BF16)
        act_out.append(
            pltpu.make_async_copy(act_buf.at[local], act_hbm.at[:, local * DK : (local + 1) * DK], sems.at[local])
        )
        act_out[-1].start()
        memory = lax.dot_general(
            weighted[local % 2], val_ref[:, span(head, DV)], (((0,), (0,)), ((), ())), preferred_element_type=F32
        )
        top = row_of(rows_ref, 3, head)[:, :WIDTH]
        decay = row_of(rows_ref, 4, head)[:, :WIDTH]
        aux = aux_rows([norm[:, k * WIDTH : (k + 1) * WIDTH] for k in range(SPLIT)], top, decay)
        for piece in range(PIECES):
            at = local * PIECES + piece
            rec_ref[at, 0:DK] = memory[:, piece * WIDTH : (piece + 1) * WIDTH].astype(BF16)
            rec_ref[at, DK:ROWS] = aux
    for copy in act_out:
        copy.wait()


def state_call(mine, chain, raw, rim, taps, values, rows):
    return kernel_call(
        functools.partial(state_kernel, mine, chain),
        [("vmem", raw), ("vmem", rim), ("vmem", taps), ("vmem", values), ("vmem", rows)],
        [("vmem", (OWNERS, ROWS, WIDTH), BF16), ("hbm", (BLK, LOCAL * DK), BF16)],
        [
            pltpu.VMEM((LOCAL, BLK, DK), BF16),
            pltpu.VMEM((2, BLK + 8, DK), F32),
            pltpu.VMEM((2, BLK, DK), BF16),
            pltpu.SemaphoreType.DMA((LOCAL,)),
        ],
        "state",
        LOCAL * 2 * BLK * DK * DV,
        LOCAL * 3 << 20,
    )


def merge(early, late):
    norms, top, decay = early
    later_norms, later_top, later_decay = late
    joined_top = jnp.maximum(top + later_decay, later_top)
    before = jnp.exp(top + later_decay - joined_top)
    after = jnp.exp(later_top - joined_top)
    joined = [before * a + after * b for a, b in zip(norms, later_norms)]
    return before, after, (joined, joined_top, decay + later_decay)


def join_kernel(own_ref, other_ref, out_hbm, first_hbm, out_buf, sems):
    second = place()[0] == 1
    held = pltpu.make_async_copy(own_ref, first_hbm, sems.at[LOCAL])
    passed = pltpu.make_async_copy(other_ref, first_hbm, sems.at[LOCAL])

    @pl.when(second)
    def _():
        passed.start()

    @pl.when(jnp.logical_not(second))
    def _():
        held.start()

    copies = []
    for local in range(LOCAL):
        at = local * PIECES
        norms, top, decay = read_aux(own_ref[at, DK:ROWS])
        other_norms, other_top, other_decay = read_aux(other_ref[at, DK:ROWS])
        own_log = top + jnp.where(second, 0.0, other_decay)
        other_log = other_top + jnp.where(second, decay, 0.0)
        joined_top = jnp.maximum(own_log, other_log)
        own_weight = jnp.exp(own_log - joined_top)
        other_weight = jnp.exp(other_log - joined_top)
        joined = [own_weight * a + other_weight * b for a, b in zip(norms, other_norms)]
        aux = aux_rows(joined, joined_top, decay + other_decay)
        for piece in range(PIECES):
            own = own_ref[at + piece, 0:DK].astype(F32)
            other = other_ref[at + piece, 0:DK].astype(F32)
            out_buf[at + piece, 0:DK] = (own_weight * own + other_weight * other).astype(BF16)
            out_buf[at + piece, DK:ROWS] = aux
        part = pl.ds(at, PIECES)
        copies.append(pltpu.make_async_copy(out_buf.at[part], out_hbm.at[part], sems.at[local]))
        copies[-1].start()
    for copy in copies:
        copy.wait()
    held.wait()


def join_call(own, other):
    return kernel_call(
        join_kernel,
        [("vmem", own), ("vmem", other)],
        [("hbm", own.shape, BF16)] * 2,
        [pltpu.VMEM(own.shape, BF16), pltpu.SemaphoreType.DMA((LOCAL + 1,))],
        "join",
        0,
        4 << 20,
    )


def split_kernel(enter_ref, first_ref, keep_ref, send_ref):
    second = place()[0] == 1
    for local in range(LOCAL):
        at = local * PIECES
        early = read_aux(enter_ref[at, DK:ROWS])
        before, after, joined = merge(early, read_aux(first_ref[at, DK:ROWS]))
        aux = aux_rows(*joined)
        plain = enter_ref[at, DK:ROWS]
        for piece in range(PIECES):
            chip = enter_ref[at + piece, 0:DK]
            moved = before * chip.astype(F32) + after * first_ref[at + piece, 0:DK].astype(F32)
            moved = moved.astype(BF16)
            keep_ref[at + piece, 0:DK] = jnp.where(second, moved, chip)
            send_ref[at + piece, 0:DK] = jnp.where(second, chip, moved)
            keep_ref[at + piece, DK:ROWS] = jnp.where(second, aux, plain)
            send_ref[at + piece, DK:ROWS] = jnp.where(second, plain, aux)


def split_call(enter, first):
    return kernel_call(
        split_kernel,
        [("vmem", enter), ("vmem", first)],
        [("vmem", enter.shape, BF16)] * 2,
        [],
        "split",
        0,
        4 << 20,
    )


def near_kernel(
    mine, chain, raw_hbm, rim_ref, tap_hbm, key_hbm, val_hbm, rows_ref,
    query_hbm, num_hbm, stat_ref,
    raw_buf, key_buf, val_buf, query_buf, num_buf, tap_buf, padded, sems,
):
    head0 = first_head(mine, chain)
    taps_in = pltpu.make_async_copy(tap_hbm, tap_buf, sems.at[5 * LOCAL])
    taps_in.start()
    coming, going = [], []
    for local in range(LOCAL):
        mid, wide = slice(local * DK, (local + 1) * DK), slice(local * DV, (local + 1) * DV)
        pairs = (
            (raw_hbm.at[:, span(head0 + local, DK)], raw_buf.at[local]),
            (key_hbm.at[:, mid], key_buf.at[local]),
            (val_hbm.at[:, span(head0 + local, DV)], val_buf.at[local]),
            (query_buf.at[local], query_hbm.at[:, mid]),
            (num_buf.at[local], num_hbm.at[:, wide]),
        )
        copies = [pltpu.make_async_copy(a, b, sems.at[5 * local + k]) for k, (a, b) in enumerate(pairs)]
        coming.append(start_all(copies[:3]))
        going.append(copies[3:])
    taps_in.wait()
    causal = lax.broadcasted_iota(jnp.int32, (TILE, TILE), 0) >= lax.broadcasted_iota(
        jnp.int32, (TILE, TILE), 1
    )
    ones = jnp.ones((8, TILE), BF16)
    for local in range(LOCAL):
        head = head0 + local
        coming[local][0].wait()
        columns, rim_columns = span(head, DK), span(HEADS + head, DK)
        for start, act in conv_rows(columns, rim_columns, raw_buf[local], rim_ref, tap_buf, padded.at[local % 2]):
            query_buf[local, start : start + STEP] = act
        going[local][0].start()
        coming[local][1].wait()
        coming[local][2].wait()
        peak = row_of(rows_ref, 1, head)
        level = row_of(rows_ref, 0, head)
        peak_column = column(peak)
        for t in range(0, BLK, TILE):
            query = query_buf[local, t : t + TILE]
            rows_peak = widen(peak_column[t : t + TILE], TILE)
            den = jnp.zeros((1, TILE), F32)
            num = None
            for s in range(0, t + TILE, TILE):
                scores = lax.dot_general(query, key_buf[local, s : s + TILE], NT, preferred_element_type=F32)
                exponent = level[:, s : s + TILE] - rows_peak
                if s == t:
                    exponent = jnp.where(causal, exponent, -jnp.inf)
                mixing = (scores * (SCALE * jnp.exp(exponent))).astype(BF16)
                den = den + lax.dot_general(ones, mixing, NT, preferred_element_type=F32)[0:1]
                part = jnp.dot(mixing, val_buf[local, s : s + TILE], preferred_element_type=F32)
                num = part if num is None else num + part
            num_buf[local, t : t + TILE] = num.astype(NUM)
            stat_ref[local, 0:1, t : t + TILE] = den
        going[local][1].start()
        stat_ref[local, 1:2] = peak
        stat_ref[local, 2:8] = jnp.zeros((6, BLK), F32)
    for copies in going:
        for copy in copies:
            copy.wait()


def near_call(mine, chain, raw, rim, taps, key_act, values, rows):
    return kernel_call(
        functools.partial(near_kernel, mine, chain),
        [("hbm", raw), ("vmem", rim), ("hbm", taps), ("hbm", key_act), ("hbm", values), ("vmem", rows)],
        [
            ("hbm", (BLK, LOCAL * DK), BF16),
            ("hbm", (BLK, LOCAL * DV), NUM),
            ("vmem", (LOCAL, 8, BLK), F32),
        ],
        [
            pltpu.VMEM((LOCAL, BLK, DK), BF16),
            pltpu.VMEM((LOCAL, BLK, DK), BF16),
            pltpu.VMEM((LOCAL, BLK, DV), BF16),
            pltpu.VMEM((LOCAL, BLK, DK), BF16),
            pltpu.VMEM((LOCAL, BLK, DV), NUM),
            pltpu.VMEM((TAPS, HEADS * DK), BF16),
            pltpu.VMEM((2, BLK + 8, DK), F32),
            pltpu.SemaphoreType.DMA((5 * LOCAL + 1,)),
        ],
        "near",
        LOCAL * 2 * BLK * BLK * (DK + DV),
        LOCAL * 5 << 20,
    )


def total_kernel(rule, rec_ref, out_ref):
    count = rec_ref.shape[0]
    norms, tops, decays = [], [], []
    for k in range(count):
        norm, top, decay = read_aux(rec_ref[k, DK:ROWS])
        norms.append(norm)
        tops.append(top if rule is None else jnp.where(place()[1] > rule[k], top, EMPTY))
        decays.append(decay)
    after = jnp.zeros((1, WIDTH), F32)
    logs = [None] * count
    for k in reversed(range(count)):
        logs[k] = tops[k] + after
        after = after + decays[k]
    peak = functools.reduce(jnp.maximum, logs)
    weights = [jnp.exp(log - peak) for log in logs]
    joined = [sum(w * n[part] for w, n in zip(weights, norms)) for part in range(SPLIT)]
    for start in range(0, DK, STEP):
        acc = weights[0] * rec_ref[0, start : start + STEP].astype(F32)
        for k in range(1, count):
            acc = acc + weights[k] * rec_ref[k, start : start + STEP].astype(F32)
        out_ref[start : start + STEP] = acc.astype(BF16)
    out_ref[DK:ROWS] = aux_rows(joined, peak, after)


def total_call(records, rule=None):
    return on_chip(functools.partial(total_kernel, rule), [records], ((ROWS, WIDTH), BF16), name="total")


def prefix_kernel(rec_ref, enter_ref, out_hbm, out_buf, sems):
    count = rec_ref.shape[0]
    norms, top, _ = read_aux(enter_ref[DK:ROWS])
    state = (norms, jnp.where(place()[1] > 0, top, EMPTY), jnp.zeros((1, WIDTH), F32))
    weights = []
    for k in range(count):
        out_buf[k, DK:ROWS] = aux_rows(*state)
        if k + 1 < count:
            early, late, state = merge(state, read_aux(rec_ref[k, DK:ROWS]))
            weights.append((early, late))
    for start in range(0, DK, STEP):
        run = enter_ref[start : start + STEP].astype(F32)
        for k in range(count):
            out_buf[k, start : start + STEP] = run.astype(BF16)
            if k + 1 < count:
                early, late = weights[k]
                run = early * run + late * rec_ref[k, start : start + STEP].astype(F32)
    copy = pltpu.make_async_copy(out_buf, out_hbm, sems.at[0])
    copy.start()
    copy.wait()


def prefix_call(records, entering):
    return kernel_call(
        prefix_kernel,
        [("vmem", records), ("vmem", entering)],
        [("hbm", records.shape, BF16)],
        [pltpu.VMEM(records.shape, BF16), pltpu.SemaphoreType.DMA((1,))],
        "prefix",
        0,
        2 << 20,
    )[0]


def far_kernel(mine, chain, query_ref, num_ref, stat_ref, enter_ref, *refs):
    out_ref, ready, sems = refs[-3:]
    copies = []
    for local in range(LOCAL):
        mid, wide = slice(local * DK, (local + 1) * DK), slice(local * DV, (local + 1) * DV)
        at = local * PIECES
        aux = enter_ref[at, DK:ROWS]
        _, top, _ = read_aux(aux)
        query = query_ref[:, mid]
        den = stat_ref[local, 0:1]
        near_peak = stat_ref[local, 1:2]
        far_log = top[:, 0:1]
        peak = jnp.maximum(near_peak, far_log)
        near_part = jnp.exp(near_peak - peak)
        far_part = jnp.exp(far_log - peak) * SCALE
        below = near_part * den + far_part * dot_norm(aux, query)
        scale = 1.0 / jnp.maximum(jnp.abs(below), 1.0)
        near_column = column(near_part * scale)
        far_column = column(far_part * scale)
        memory = jnp.concatenate([enter_ref[at + piece, 0:DK] for piece in range(PIECES)], axis=1)
        for t in range(0, BLK, STEP):
            far = jnp.dot(query[t : t + STEP], memory, preferred_element_type=F32)
            near_weight = widen(near_column[t : t + STEP], DV)
            far_weight = widen(far_column[t : t + STEP], DV)
            ready[local, t : t + STEP] = (near_weight * num_ref[t : t + STEP, wide].astype(F32) + far_weight * far).astype(BF16)
        head = first_head(mine, chain) + local
        copies.append(pltpu.make_async_copy(ready.at[local], out_ref.at[:, span(head, DV)], sems.at[local]))
        copies[-1].start()
    for copy in copies:
        copy.wait()


def far_call(mine, chain, query_act, num, stat, entering, out=None):
    operands = [pltpu.with_memory_space_constraint(x, pltpu.VMEM) for x in (query_act, num, stat, entering)]
    in_specs = [VMEM_SPEC] * len(operands)
    aliases = {}
    if out is not None:
        in_specs.append(pl.BlockSpec(memory_space=pltpu.HBM))
        aliases = {len(operands): 0}
        operands.append(out)
    return pl.pallas_call(
        functools.partial(far_kernel, mine, chain),
        in_specs=in_specs,
        out_specs=pl.BlockSpec(memory_space=pltpu.HBM),
        out_shape=jax.ShapeDtypeStruct((BLK, HEADS * DV), BF16),
        scratch_shapes=[pltpu.VMEM((LOCAL, BLK, DV), BF16), pltpu.SemaphoreType.DMA((LOCAL,))],
        input_output_aliases=aliases,
        compiler_params=pltpu.CompilerParams(vmem_limit_bytes=8 << 20),
        name="far",
        cost_estimate=pl.CostEstimate(
            flops=LOCAL * 2 * BLK * DK * DV, transcendentals=0, bytes_accessed=LOCAL * 5 << 20
        ),
    )(*operands)


def on_device(query_raw, key_raw, values, in_gate, forget_gate, query_conv, key_conv):
    devices = lax.axis_size(AXES)
    cube_size = 2 * OWNERS
    cubes = devices // cube_size
    line = [(i, i + 1) for i in range(devices - 1)]
    swap = [(i, i ^ 1) for i in range(devices)]
    forward = [(i, i + 1) for i in range(0, devices, 2)]
    owners = [
        [g * cube_size + 2 * k + c for k in range(OWNERS)] for g in range(cubes) for c in range(2)
    ]
    up = lambda distance: [(i, i + distance * cube_size) for i in range(devices - distance * cube_size)]
    spread = lambda x: lax.all_to_all(x, AXES, 0, 0, axis_index_groups=owners, tiled=True)
    after = lambda x, *done: lax.optimization_barrier((x,) + done)[0]

    chains = range(CHAINS)
    key_mine, key_theirs, other_mine, first = ([None] * CHAINS for _ in range(4))
    pieces, entering, enter_mine, enter_theirs = ([None] * CHAINS for _ in range(4))
    near_mine, near_theirs = ([None] * CHAINS for _ in range(2))

    rim = lax.ppermute(tails_call(key_raw, query_raw), AXES, line)
    rows, key_held, taps_held, val_held = prepare_call(in_gate, forget_gate, key_raw, key_conv, values)

    for c in chains:
        sent, key_theirs[c] = state_call(False, c, key_held, rim, taps_held, val_held, rows)
        rows = after(rows, sent)
        other_mine[c] = lax.ppermute(sent, AXES, swap)
    for c in chains:
        own, key_mine[c] = state_call(True, c, key_held, rim, taps_held, val_held, rows)
        joined, first[c] = join_call(own, other_mine[c])
        rows = after(rows, joined)
        pieces[c] = spread(joined)
    for c in chains:
        near_mine[c] = near_call(True, c, query_raw, rim, query_conv, key_mine[c], values, rows)
        rows = after(rows, near_mine[c][0])
        near_theirs[c] = near_call(False, c, query_raw, rim, query_conv, key_theirs[c], values, rows)
        pieces[c] = after(pieces[c], near_theirs[c][0])
        total = total_call(pieces[c])
        rows = after(rows, total)
        entering[c] = lax.ppermute(total, AXES, up(1))
        distance = 1
        while distance < cubes - 1:
            earlier = lax.ppermute(entering[c], AXES, up(distance))
            entering[c] = total_call(jnp.stack([earlier, entering[c]]), (distance, 0))
            distance *= 2
    for c in chains:
        before = prefix_call(pieces[c], entering[c])
        rows = after(rows, before)
        enter_mine[c] = spread(before)
    out = None
    for c in chains:
        keep, send = split_call(enter_mine[c], first[c])
        enter_theirs[c] = lax.ppermute(send, AXES, swap)
        out = far_call(True, c, *near_mine[c], keep, out)
        out = far_call(False, c, *near_theirs[c], enter_theirs[c], out)
    return out


def solution(mesh):
    split = P(AXES, None)
    in_specs = (split, split, split, split, split, P(), P())
    return jax.shard_map(on_device, mesh=mesh, in_specs=in_specs, out_specs=split, check_vma=False)
```

profile of v0, /device:TPU:0, one launch (start us, length us, event | category | flops | bytes accessed | tf_op | source)
XLA Modules:
  0.0 79.9 jit_solution(5459280300508184475)
XLA Ops:
  0.0 0.9 %tails.1 = bf16[16,4096]{1,0:T(8,128)(2,1)S(1)} custom-call(bf16[512,2048]{1,0:T(8,128)(2,1)} %key_hbm.3, bf16[512,2048]{1,0:T(8,128)(2,1)} %raw_hbm.3), custom_call_target="tpu_custom_call" | custom-call | bytes 131072 | tf_op jit(solution)/shard_map/tails/pallas_call | solution.py:221
  0.9 2.4 %collective-permute-start = (bf16[16,4096]{1,0:T(8,128)(2,1)S(1)}, bf16[16,4096]{1,0:T(8,128)(2,1)S(1)}, u32[]{:S(2)}, u32[]{:S(2)}) collective-permute-start(bf16[16,4096]{1,0:T(8,128)(2,1)S(1)} %tails.1), channel_id=1, source_target_pairs={{0,1},{1,2},{2,3},{3,4},{4,5},{5,6},{6,7},{7,8},{8,9},{9,10},{10,1... | collective-permute-start | bytes 393224 | tf_op jit(solution)/shard_map/ppermute | solution.py:615
  3.3 2.9 %prepare.1 = (f32[40,512]{1,0:T(8,128)S(1)}, bf16[512,2048]{1,0:T(8,128)(2,1)S(1)}, bf16[4,2048]{1,0:T(4,128)(2,1)S(1)}, bf16[512,4096]{1,0:T(8,128)(2,1)S(1)}) custom-call(bf16[8,512]{1,0:T(8,128)(2,1)} %bitcast.2, bf16[8,512]{1,0:T(8,128)(2,1)} %bitcast.3, bf16[512,2048]{1,0:T(8,128)(2,1)} %key_hbm.3, bf16[4,2048]{1,0:T(4,128)(2,1)} %tap_hbm.3, ...), custom_call_target="tpu_custom_call" | custom-call | bytes 6291456 | tf_op jit(solution)/shard_map/prepare/pallas_call | solution.py:221
  6.2 0.0 collective-permute-done.rim_ref
  6.2 4.2 %state.2 = (bf16[8,272,256]{2,1,0:T(8,128)(2,1)S(1)}, bf16[512,1024]{1,0:T(8,128)(2,1)}) custom-call(bf16[512,2048]{1,0:T(8,128)(2,1)S(1)} %get-tuple-element.27.raw_ref, bf16[16,4096]{1,0:T(8,128)(2,1)S(1)} %collective-permute-done.rim_ref, bf16[4,2048]{1,0:T(4,128)(2,1)S(1)} %get-tuple-element.28.tap_ref, bf16[512,4096]{1,0:T(8,128)(2,1)S(1)} %get-tuple-element.29.val_ref, ...), custom_call_target="tpu_custom_call" | custom-call | flops 536870912 | bytes 12582912 | tf_op jit(solution)/shard_map/state/pallas_call | solution.py:221
  10.5 2.7 %collective-permute-start.1 = (bf16[8,272,256]{2,1,0:T(8,128)(2,1)S(1)}, bf16[8,272,256]{2,1,0:T(8,128)(2,1)S(1)}, u32[]{:S(2)}, u32[]{:S(2)}) collective-permute-start(bf16[8,272,256]{2,1,0:T(8,128)(2,1)S(1)} %get-tuple-element.32), channel_id=1, source_target_pairs={{0,1},{1,0},{2,3},{3,2},{4,5},{5,4},{6,7},{7,6},{8,9},{9,8},{10,11... | collective-permute-start | bytes 3342344 | tf_op jit(solution)/shard_map/ppermute | solution.py:621
  13.2 4.2 %state.3 = (bf16[8,272,256]{2,1,0:T(8,128)(2,1)S(1)}, bf16[512,1024]{1,0:T(8,128)(2,1)}) custom-call(bf16[512,2048]{1,0:T(8,128)(2,1)S(1)} %get-tuple-element.27.raw_ref, bf16[16,4096]{1,0:T(8,128)(2,1)S(1)} %collective-permute-done.rim_ref, bf16[4,2048]{1,0:T(4,128)(2,1)S(1)} %get-tuple-element.28.tap_ref, bf16[512,4096]{1,0:T(8,128)(2,1)S(1)} %get-tuple-element.29.val_ref, ...), custom_call_target="tpu_custom_call" | custom-call | flops 536870912 | bytes 12582912 | tf_op jit(solution)/shard_map/state/pallas_call | solution.py:221
  17.4 0.0 collective-permute-done.1.other_ref
  17.4 1.4 %join.1 = (bf16[8,272,256]{2,1,0:T(8,128)(2,1)}, bf16[8,272,256]{2,1,0:T(8,128)(2,1)}) custom-call(bf16[8,272,256]{2,1,0:T(8,128)(2,1)S(1)} %get-tuple-element.34.own_ref, bf16[8,272,256]{2,1,0:T(8,128)(2,1)S(1)} %collective-permute-done.1.other_ref), custom_call_target="tpu_custom_call" | custom-call | bytes 4194304 | tf_op jit(solution)/shard_map/join/pallas_call | solution.py:221
  18.8 4.7 %all-to-all-start = ((bf16[8,272,256]{2,1,0:T(8,128)(2,1)}), bf16[8,272,256]{2,1,0:T(8,128)(2,1)S(1)}, u32[]{:S(2)}, u32[]{:S(2)}) async-start(bf16[8,272,256]{2,1,0:T(8,128)(2,1)} %get-tuple-element.35), calls=%async_computation | async-start | bytes 2228224 | tf_op jit(solution)/shard_map/all_to_all | solution.py:607
  23.5 7.5 %near.2 = (bf16[512,1024]{1,0:T(8,128)(2,1)}, bf16[512,2048]{1,0:T(8,128)(2,1)}, f32[4,8,512]{2,1,0:T(8,128)S(1)}) custom-call(bf16[512,2048]{1,0:T(8,128)(2,1)} %raw_hbm.3, bf16[16,4096]{1,0:T(8,128)(2,1)S(1)} %collective-permute-done.rim_ref, bf16[4,2048]{1,0:T(4,128)(2,1)} %tap_hbm.5, bf16[512,1024]{1,0:T(8,128)(2,1)} %get-tuple-element.37.key_hbm, ...), custom_call_target="tpu_custom_call" | custom-call | flops 1610612736 | bytes 20971520 | tf_op jit(solution)/shard_map/near/pallas_call | solution.py:221
  31.1 7.6 %near.3 = (bf16[512,1024]{1,0:T(8,128)(2,1)}, bf16[512,2048]{1,0:T(8,128)(2,1)}, f32[4,8,512]{2,1,0:T(8,128)S(1)}) custom-call(bf16[512,2048]{1,0:T(8,128)(2,1)} %raw_hbm.3, bf16[16,4096]{1,0:T(8,128)(2,1)S(1)} %collective-permute-done.rim_ref, bf16[4,2048]{1,0:T(4,128)(2,1)} %tap_hbm.5, bf16[512,1024]{1,0:T(8,128)(2,1)} %get-tuple-element.31.key_hbm, ...), custom_call_target="tpu_custom_call" | custom-call | flops 1610612736 | bytes 20971520 | tf_op jit(solution)/shard_map/near/pallas_call | solution.py:221
  38.7 1.5 %all-to-all-done.rec_ref = bf16[8,272,256]{2,1,0:T(8,128)(2,1)S(1)} async-done(((bf16[8,272,256]{2,1,0:T(8,128)(2,1)}), bf16[8,272,256]{2,1,0:T(8,128)(2,1)S(1)}, u32[]{:S(2)}, u32[]{:S(2)}) %all-to-all-start) | async-done | bytes 1114144 | tf_op jit(solution)/shard_map/all_to_all | solution.py:607
  40.2 0.3 total.1
  40.4 4.4 %collective-permute-start.2 = (bf16[272,256]{1,0:T(8,128)(2,1)S(1)}, bf16[272,256]{1,0:T(8,128)(2,1)S(1)}, u32[]{:S(2)}, u32[]{:S(2)}) collective-permute-start(bf16[272,256]{1,0:T(8,128)(2,1)S(1)} %total.1), channel_id=1, source_target_pairs={{0,16},{1,17},{2,18},{3,19},{4,20},{5,21},{6,22},{7,23},{8,24},{9,... | collective-permute-start | bytes 417800 | tf_op jit(solution)/shard_map/ppermute | solution.py:634
  44.8 2.9 %collective-permute-done.2.enter_ref = bf16[272,256]{1,0:T(8,128)(2,1)S(1)} collective-permute-done((bf16[272,256]{1,0:T(8,128)(2,1)S(1)}, bf16[272,256]{1,0:T(8,128)(2,1)S(1)}, u32[]{:S(2)}, u32[]{:S(2)}) %collective-permute-start.2) | collective-permute-done | bytes 139296 | tf_op jit(solution)/shard_map/ppermute | solution.py:634
  47.7 1.4 %prefix.1 = bf16[8,272,256]{2,1,0:T(8,128)(2,1)} custom-call(bf16[8,272,256]{2,1,0:T(8,128)(2,1)S(1)} %all-to-all-done.rec_ref, bf16[272,256]{1,0:T(8,128)(2,1)S(1)} %collective-permute-done.2.enter_ref), custom_call_target="tpu_custom_call" | custom-call | bytes 2097152 | tf_op jit(solution)/shard_map/prefix/pallas_call | solution.py:221
  49.1 0.0 copy-start.2
  49.2 0.0 copy-start.4
  49.2 24.0 %all_to_all.10.enter_ref = bf16[8,272,256]{2,1,0:T(8,128)(2,1)S(1)} all-to-all(bf16[8,272,256]{2,1,0:T(8,128)(2,1)} %prefix.1), channel_id=1, replica_groups={{0,2,4,6,8,10,12,14},{1,3,5,7,9,11,13,15},{16,18,20,22,24,26,28,30},{17..., dimensions={0} | all-to-all | bytes 2228224 | tf_op jit(solution)/shard_map/all_to_all | solution.py:607
  73.2 0.0 copy-done.2
  73.2 0.0 copy-start.1
  73.2 0.7 split.1
  73.8 0.1 collective-permute-start.3
  73.9 0.0 copy-done.4
  73.9 0.8 %copy-done.1 = bf16[512,2048]{1,0:T(8,128)(2,1)S(1)} copy-done((bf16[512,2048]{1,0:T(8,128)(2,1)S(1)}, bf16[512,2048]{1,0:T(8,128)(2,1)}, u32[]{:S(2)}) %copy-start.1) | copy-done | bytes 2097176
  74.7 0.0 copy-start
  74.7 2.5 %far.2.refs_0_ = bf16[512,4096]{1,0:T(8,128)(2,1)} custom-call(bf16[512,1024]{1,0:T(8,128)(2,1)S(1)} %copy-done.4, bf16[512,2048]{1,0:T(8,128)(2,1)S(1)} %copy-done.1, f32[4,8,512]{2,1,0:T(8,128)S(1)} %get-tuple-element.47.stat_ref, bf16[8,272,256]{2,1,0:T(8,128)(2,1)S(1)} %get-tuple-element.48.enter_ref), custom_call_target="tpu_custom_call" | custom-call | flops 536870912 | bytes 20971520 | tf_op jit(solution)/shard_map/far/pallas_call | solution.py:581
  77.2 0.0 collective-permute-done.3.enter_ref
  77.2 0.0 copy-done
  77.2 0.0 copy-done.3
  77.2 2.5 %far.3 = bf16[512,4096]{1,0:T(8,128)(2,1)} custom-call(bf16[512,1024]{1,0:T(8,128)(2,1)S(1)} %copy-done.3, bf16[512,2048]{1,0:T(8,128)(2,1)S(1)} %copy-done, f32[4,8,512]{2,1,0:T(8,128)S(1)} %get-tuple-element.42.stat_ref, bf16[8,272,256]{2,1,0:T(8,128)(2,1)S(1)} %collective-permute-done.3.enter_ref, ...), custom_call_target="tpu_custom_call", output_to_operand_aliasing={{}: (4, {})} | custom-call | flops 536870912 | bytes 20971520 | tf_op jit(solution)/shard_map/far/pallas_call | solution.py:581
  (1 shorter events, 0.0 us)
Async XLA Ops:
  0.9 5.3 %collective-permute-start = (bf16[16,4096]{1,0:T(8,128)(2,1)S(1)}, bf16[16,4096]{1,0:T(8,128)(2,1)S(1)}, u32[]{:S(2)}, u32[]{:S(2)}) collective-permute-start(bf16[16,4096]{1,0:T(8,128)(2,1)S(1)} %tails.1), channel_id=1, source_target_pairs={{0,1},{1,2},{2,3},{3,4},{4,5},{5,6},{6,7},{7,8},{8,9},{9,10},{10,1... | collective-permute-start | bytes 393224 | tf_op jit(solution)/shard_map/ppermute | solution.py:615
  10.5 6.9 %collective-permute-start.1 = (bf16[8,272,256]{2,1,0:T(8,128)(2,1)S(1)}, bf16[8,272,256]{2,1,0:T(8,128)(2,1)S(1)}, u32[]{:S(2)}, u32[]{:S(2)}) collective-permute-start(bf16[8,272,256]{2,1,0:T(8,128)(2,1)S(1)} %get-tuple-element.32), channel_id=1, source_target_pairs={{0,1},{1,0},{2,3},{3,2},{4,5},{5,4},{6,7},{7,6},{8,9},{9,8},{10,11... | collective-permute-start | bytes 3342344 | tf_op jit(solution)/shard_map/ppermute | solution.py:621
  18.8 21.4 %all-to-all-start = ((bf16[8,272,256]{2,1,0:T(8,128)(2,1)}), bf16[8,272,256]{2,1,0:T(8,128)(2,1)S(1)}, u32[]{:S(2)}, u32[]{:S(2)}) async-start(bf16[8,272,256]{2,1,0:T(8,128)(2,1)} %get-tuple-element.35), calls=%async_computation | async-start | bytes 2228224 | tf_op jit(solution)/shard_map/all_to_all | solution.py:607
  40.4 7.3 %collective-permute-start.2 = (bf16[272,256]{1,0:T(8,128)(2,1)S(1)}, bf16[272,256]{1,0:T(8,128)(2,1)S(1)}, u32[]{:S(2)}, u32[]{:S(2)}) collective-permute-start(bf16[272,256]{1,0:T(8,128)(2,1)S(1)} %total.1), channel_id=1, source_target_pairs={{0,16},{1,17},{2,18},{3,19},{4,20},{5,21},{6,22},{7,23},{8,24},{9,... | collective-permute-start | bytes 417800 | tf_op jit(solution)/shard_map/ppermute | solution.py:634
  49.1 24.0 %copy-start.2 = (bf16[8,272,256]{2,1,0:T(8,128)(2,1)S(1)}, bf16[8,272,256]{2,1,0:T(8,128)(2,1)}, u32[]{:S(2)}) copy-start(bf16[8,272,256]{2,1,0:T(8,128)(2,1)} %get-tuple-element.44.first_ref) | copy-start | bytes 3342340
  49.2 24.8 %copy-start.4 = (bf16[512,1024]{1,0:T(8,128)(2,1)S(1)}, bf16[512,1024]{1,0:T(8,128)(2,1)}, u32[]{:S(2)}) copy-start(bf16[512,1024]{1,0:T(8,128)(2,1)} %get-tuple-element.38.query_ref) | copy-start | bytes 3145732
  73.2 1.6 %copy-start.1 = (bf16[512,2048]{1,0:T(8,128)(2,1)S(1)}, bf16[512,2048]{1,0:T(8,128)(2,1)}, u32[]{:S(2)}) copy-start(bf16[512,2048]{1,0:T(8,128)(2,1)} %get-tuple-element.46.num_ref) | copy-start | bytes 6291460
  73.8 3.4 %collective-permute-start.3 = (bf16[8,272,256]{2,1,0:T(8,128)(2,1)S(1)}, bf16[8,272,256]{2,1,0:T(8,128)(2,1)S(1)}, u32[]{:S(2)}, u32[]{:S(2)}) collective-permute-start(bf16[8,272,256]{2,1,0:T(8,128)(2,1)S(1)} %get-tuple-element.45), channel_id=1, source_target_pairs={{0,1},{1,0},{2,3},{3,2},{4,5},{5,4},{6,7},{7,6},{8,9},{9,8},{10,11... | collective-permute-start | bytes 3342344 | tf_op jit(solution)/shard_map/ppermute | solution.py:647
  74.7 2.5 %copy-start = (bf16[512,2048]{1,0:T(8,128)(2,1)S(1)}, bf16[512,2048]{1,0:T(8,128)(2,1)}, u32[]{:S(2)}) copy-start(bf16[512,2048]{1,0:T(8,128)(2,1)} %get-tuple-element.41.num_ref) | copy-start | bytes 6291460
  74.7 2.5 %copy-start.3 = (bf16[512,1024]{1,0:T(8,128)(2,1)S(1)}, bf16[512,1024]{1,0:T(8,128)(2,1)}, u32[]{:S(2)}) copy-start(bf16[512,1024]{1,0:T(8,128)(2,1)} %get-tuple-element.40.query_ref) | copy-start | bytes 3145732
where the time goes:
time: 80.4 us; the launch traced here: 79.9 us
  Pallas kernels  36.1 us (45%)
  blocking collectives  24 us (30%)
  starting transfers between devices  14.2 us (18%)
  waiting for transfers between devices  4.41 us (5%)
  local copies, waits for them, and re-layouts  0.84 us (1%)
    pallas_call x9, Pallas kernels, kernel_call(): pl.pallas_call(kernel, in_specs=in_specs, out_specs=[VMEM_SPEC if where =...  30.9 us
    all_to_all x1, blocking collectives, on_device(): lax.all_to_all(x, AXES, 0, 0, axis_index_groups=owners, tiled=True)  24 us
    pallas_call x2, Pallas kernels, far_call(): pl.pallas_call(functools.partial(far_kernel, mine, chain), in_specs=in_sp...  4.91 us
    all_to_all x1, starting transfers between devices, on_device(): lax.all_to_all(x, AXES, 0, 0, axis_index_groups=owners, tiled=True)  4.71 us
    ppermute x1, starting transfers between devices, on_device(): entering[c] = lax.ppermute(total, AXES, up(1))  4.36 us
    ppermute x1, waiting for transfers between devices, on_device(): entering[c] = lax.ppermute(total, AXES, up(1))  2.93 us
    ppermute x1, starting transfers between devices, on_device(): other_mine[c] = lax.ppermute(sent, AXES, swap)  2.7 us
    ppermute x1, starting transfers between devices, on_device(): rim = lax.ppermute(tails_call(key_raw, query_raw), AXES, line)  2.36 us
  transfers between devices with their start and end apart: 5, of which 2 were waited for; matrix products, arithmetic and copies ran while one was open for 0% of the time, Pallas kernels for 31%

commit v1 on v0

--- a/solution.py
+++ b/solution.py
@@ -25,6 +25,9 @@
 TILE = 256
 STEP = 128
 EMPTY = -1e30
+ORDER = (7, 6, 5, 3, 4, 2, 1)
+SIDES = [(True, local) for local in range(LOCAL)] + [(False, local) for local in range(LOCAL)]
+PARTS = (SIDES[:4], SIDES[4:6], SIDES[6:])
 SCALE = DK**-0.5
 F32 = jnp.float32
 BF16 = jnp.bfloat16
@@ -85,11 +88,11 @@
 
 def place():
     me = lax.axis_index("ctx") * lax.axis_size("head") + lax.axis_index("head")
-    return me % 2, me // (2 * OWNERS)
+    return me % 2, me // (2 * OWNERS), me % (2 * OWNERS) // 2
 
 
 def first_head(mine, chain):
-    core, _ = place()
+    core = place()[0]
     return GROUP * (core if mine else 1 - core) + LOCAL * chain
 
 
@@ -251,23 +254,17 @@
     return copies
 
 
-def state_kernel(mine, chain, raw_ref, rim_ref, tap_ref, val_ref, rows_ref, rec_ref, act_hbm, act_buf, padded, weighted, sems):
+def state_kernel(mine, chain, raw_ref, rim_ref, tap_ref, val_ref, rows_ref, rec_ref, padded, weighted):
     head0 = first_head(mine, chain)
-    act_out = []
     for local in range(LOCAL):
         head = head0 + local
         weight = column(row_of(rows_ref, 2, head))
         norm = jnp.zeros((1, DK), F32)
         columns = span(head, DK)
         for start, act in conv_rows(columns, columns, raw_ref[:, columns], rim_ref, tap_ref, padded.at[local % 2]):
-            act_buf[local, start : start + STEP] = act
             scaled = act.astype(F32) * widen(weight[start : start + STEP], DK)
             norm = norm + jnp.sum(scaled, axis=0, keepdims=True)
             weighted[local % 2, start : start + STEP] = scaled.astype(BF16)
-        act_out.append(
-            pltpu.make_async_copy(act_buf.at[local], act_hbm.at[:, local * DK : (local + 1) * DK], sems.at[local])
-        )
-        act_out[-1].start()
         memory = lax.dot_general(
             weighted[local % 2], val_ref[:, span(head, DV)], (((0,), (0,)), ((), ())), preferred_element_type=F32
         )
@@ -278,25 +275,18 @@
             at = local * PIECES + piece
             rec_ref[at, 0:DK] = memory[:, piece * WIDTH : (piece + 1) * WIDTH].astype(BF16)
             rec_ref[at, DK:ROWS] = aux
-    for copy in act_out:
-        copy.wait()
 
 
 def state_call(mine, chain, raw, rim, taps, values, rows):
     return kernel_call(
         functools.partial(state_kernel, mine, chain),
         [("vmem", raw), ("vmem", rim), ("vmem", taps), ("vmem", values), ("vmem", rows)],
-        [("vmem", (OWNERS, ROWS, WIDTH), BF16), ("hbm", (BLK, LOCAL * DK), BF16)],
-        [
-            pltpu.VMEM((LOCAL, BLK, DK), BF16),
-            pltpu.VMEM((2, BLK + 8, DK), F32),
-            pltpu.VMEM((2, BLK, DK), BF16),
-            pltpu.SemaphoreType.DMA((LOCAL,)),
-        ],
+        [("vmem", (OWNERS, ROWS, WIDTH), BF16)],
+        [pltpu.VMEM((2, BLK + 8, DK), F32), pltpu.VMEM((2, BLK, DK), BF16)],
         "state",
         LOCAL * 2 * BLK * DK * DV,
         LOCAL * 3 << 20,
-    )
+    )[0]
 
 
 def merge(early, late):
@@ -309,20 +299,10 @@
     return before, after, (joined, joined_top, decay + later_decay)
 
 
-def join_kernel(own_ref, other_ref, out_hbm, first_hbm, out_buf, sems):
-    second = place()[0] == 1
-    held = pltpu.make_async_copy(own_ref, first_hbm, sems.at[LOCAL])
-    passed = pltpu.make_async_copy(other_ref, first_hbm, sems.at[LOCAL])
-
-    @pl.when(second)
-    def _():
-        passed.start()
-
-    @pl.when(jnp.logical_not(second))
-    def _():
-        held.start()
-
-    copies = []
+def join_kernel(own_ref, other_ref, *refs):
+    outs, buf = refs[:-1], refs[-1]
+    core, _, chip = place()
+    second = core == 1
     for local in range(LOCAL):
         at = local * PIECES
         norms, top, decay = read_aux(own_ref[at, DK:ROWS])
@@ -337,52 +317,53 @@
         for piece in range(PIECES):
             own = own_ref[at + piece, 0:DK].astype(F32)
             other = other_ref[at + piece, 0:DK].astype(F32)
-            out_buf[at + piece, 0:DK] = (own_weight * own + other_weight * other).astype(BF16)
-            out_buf[at + piece, DK:ROWS] = aux
-        part = pl.ds(at, PIECES)
-        copies.append(pltpu.make_async_copy(out_buf.at[part], out_hbm.at[part], sems.at[local]))
-        copies[-1].start()
-    for copy in copies:
-        copy.wait()
-    held.wait()
+            buf[at + piece, 0:DK] = (own_weight * own + other_weight * other).astype(BF16)
+            buf[at + piece, DK:ROWS] = aux
+    for mask, out_ref in enumerate(outs):
+        out_ref[...] = buf[chip ^ mask]
 
 
 def join_call(own, other):
     return kernel_call(
         join_kernel,
         [("vmem", own), ("vmem", other)],
-        [("hbm", own.shape, BF16)] * 2,
-        [pltpu.VMEM(own.shape, BF16), pltpu.SemaphoreType.DMA((LOCAL + 1,))],
+        [("vmem", own.shape[1:], BF16)] * OWNERS,
+        [pltpu.VMEM(own.shape, BF16)],
         "join",
         0,
         4 << 20,
     )
 
 
-def split_kernel(enter_ref, first_ref, keep_ref, send_ref):
-    second = place()[0] == 1
+def split_kernel(first_ref, *refs):
+    records, (keep_ref, send_ref, enter_buf) = refs[:OWNERS], refs[OWNERS:]
+    core, _, chip = place()
+    second = core == 1
+    for mask, record in enumerate(records):
+        enter_buf[chip ^ mask] = record[...]
     for local in range(LOCAL):
         at = local * PIECES
-        early = read_aux(enter_ref[at, DK:ROWS])
+        early = read_aux(enter_buf[at, DK:ROWS])
         before, after, joined = merge(early, read_aux(first_ref[at, DK:ROWS]))
         aux = aux_rows(*joined)
-        plain = enter_ref[at, DK:ROWS]
+        plain = enter_buf[at, DK:ROWS]
         for piece in range(PIECES):
-            chip = enter_ref[at + piece, 0:DK]
-            moved = before * chip.astype(F32) + after * first_ref[at + piece, 0:DK].astype(F32)
+            chip_part = enter_buf[at + piece, 0:DK]
+            moved = before * chip_part.astype(F32) + after * first_ref[at + piece, 0:DK].astype(F32)
             moved = moved.astype(BF16)
-            keep_ref[at + piece, 0:DK] = jnp.where(second, moved, chip)
-            send_ref[at + piece, 0:DK] = jnp.where(second, chip, moved)
+            keep_ref[at + piece, 0:DK] = jnp.where(second, moved, chip_part)
+            send_ref[at + piece, 0:DK] = jnp.where(second, chip_part, moved)
             keep_ref[at + piece, DK:ROWS] = jnp.where(second, aux, plain)
             send_ref[at + piece, DK:ROWS] = jnp.where(second, plain, aux)
 
 
-def split_call(enter, first):
+def split_call(records, first):
+    shape = (OWNERS, ROWS, WIDTH)
     return kernel_call(
         split_kernel,
-        [("vmem", enter), ("vmem", first)],
-        [("vmem", enter.shape, BF16)] * 2,
-        [],
+        [("vmem", first)] + [("vmem", record) for record in records],
+        [("vmem", shape, BF16)] * 2,
+        [pltpu.VMEM(shape, BF16)],
         "split",
         0,
         4 << 20,
@@ -390,99 +371,143 @@
 
 
 def near_kernel(
-    mine, chain, raw_hbm, rim_ref, tap_hbm, key_hbm, val_hbm, rows_ref,
-    query_hbm, num_hbm, stat_ref,
-    raw_buf, key_buf, val_buf, query_buf, num_buf, tap_buf, padded, sems,
+    heads, park, raw_hbm, key_hbm, rim_ref, tap_hbm, key_tap_hbm, val_hbm, rows_ref, *refs,
 ):
-    head0 = first_head(mine, chain)
-    taps_in = pltpu.make_async_copy(tap_hbm, tap_buf, sems.at[5 * LOCAL])
-    taps_in.start()
+    count = len(heads)
+    if park:
+        own_ref, other_ref = refs[:2]
+        first_hbm = refs[5]
+        refs = refs[2:5] + refs[6:]
+    (
+        query_hbm, num_hbm, stat_ref,
+        raw_buf, raw_key_buf, key_buf, val_buf, query_buf, num_buf, tap_buf, padded, sems,
+    ) = refs
+    places = [first_head(mine, 0) + local for mine, local in heads]
+    taps_in = start_all(
+        [
+            pltpu.make_async_copy(tap_hbm, tap_buf.at[0], sems.at[5 * count]),
+            pltpu.make_async_copy(key_tap_hbm, tap_buf.at[1], sems.at[5 * count + 1]),
+        ]
+    )
+    if park:
+        second = place()[0] == 1
+        held = pltpu.make_async_copy(own_ref, first_hbm, sems.at[5 * count + 2])
+        passed = pltpu.make_async_copy(other_ref, first_hbm, sems.at[5 * count + 2])
+
+        @pl.when(second)
+        def _():
+            passed.start()
+
+        @pl.when(jnp.logical_not(second))
+        def _():
+            held.start()
+
     coming, going = [], []
-    for local in range(LOCAL):
+    for local in range(count):
         mid, wide = slice(local * DK, (local + 1) * DK), slice(local * DV, (local + 1) * DV)
         pairs = (
-            (raw_hbm.at[:, span(head0 + local, DK)], raw_buf.at[local]),
-            (key_hbm.at[:, mid], key_buf.at[local]),
-            (val_hbm.at[:, span(head0 + local, DV)], val_buf.at[local]),
+            (raw_hbm.at[:, span(places[local], DK)], raw_buf.at[local]),
+            (key_hbm.at[:, span(places[local], DK)], raw_key_buf.at[local]),
+            (val_hbm.at[:, span(places[local], DV)], val_buf.at[local]),
             (query_buf.at[local], query_hbm.at[:, mid]),
             (num_buf.at[local], num_hbm.at[:, wide]),
         )
         copies = [pltpu.make_async_copy(a, b, sems.at[5 * local + k]) for k, (a, b) in enumerate(pairs)]
         coming.append(start_all(copies[:3]))
         going.append(copies[3:])
-    taps_in.wait()
+    for copy in taps_in:
+        copy.wait()
     causal = lax.broadcasted_iota(jnp.int32, (TILE, TILE), 0) >= lax.broadcasted_iota(
         jnp.int32, (TILE, TILE), 1
     )
-    ones = jnp.ones((8, TILE), BF16)
-    for local in range(LOCAL):
-        head = head0 + local
+    for local in range(count):
+        head = places[local]
         coming[local][0].wait()
         columns, rim_columns = span(head, DK), span(HEADS + head, DK)
-        for start, act in conv_rows(columns, rim_columns, raw_buf[local], rim_ref, tap_buf, padded.at[local % 2]):
+        for start, act in conv_rows(columns, rim_columns, raw_buf[local], rim_ref, tap_buf.at[0], padded.at[0]):
             query_buf[local, start : start + STEP] = act
         going[local][0].start()
         coming[local][1].wait()
+        for start, act in conv_rows(columns, columns, raw_key_buf[local], rim_ref, tap_buf.at[1], padded.at[1]):
+            key_buf[local, start : start + STEP] = act
         coming[local][2].wait()
         peak = row_of(rows_ref, 1, head)
         level = row_of(rows_ref, 0, head)
         peak_column = column(peak)
+        scores = {
+            s: lax.dot_general(query_buf[local, s:BLK], key_buf[local, s : s + TILE], NT, preferred_element_type=F32)
+            for s in range(0, BLK, TILE)
+        }
         for t in range(0, BLK, TILE):
-            query = query_buf[local, t : t + TILE]
             rows_peak = widen(peak_column[t : t + TILE], TILE)
-            den = jnp.zeros((1, TILE), F32)
-            num = None
+            parts = []
             for s in range(0, t + TILE, TILE):
-                scores = lax.dot_general(query, key_buf[local, s : s + TILE], NT, preferred_element_type=F32)
                 exponent = level[:, s : s + TILE] - rows_peak
                 if s == t:
                     exponent = jnp.where(causal, exponent, -jnp.inf)
-                mixing = (scores * (SCALE * jnp.exp(exponent))).astype(BF16)
-                den = den + lax.dot_general(ones, mixing, NT, preferred_element_type=F32)[0:1]
-                part = jnp.dot(mixing, val_buf[local, s : s + TILE], preferred_element_type=F32)
-                num = part if num is None else num + part
+                parts.append((scores[s][t - s : t - s + TILE] * (SCALE * jnp.exp(exponent))).astype(BF16))
+            mixing = jnp.concatenate(parts, axis=1)
+            num = jnp.dot(mixing, val_buf[local, 0 : t + TILE], preferred_element_type=F32)
             num_buf[local, t : t + TILE] = num.astype(NUM)
-            stat_ref[local, 0:1, t : t + TILE] = den
-        going[local][1].start()
+            added = sum(part.astype(F32) for part in parts)
+            den = jnp.sum(added[:, 0:128] + added[:, 128:TILE], axis=1, keepdims=True)
+            stat_ref[local, 0:1, t : t + TILE] = jnp.broadcast_to(den, (TILE, 128)).T[0:1]
         stat_ref[local, 1:2] = peak
         stat_ref[local, 2:8] = jnp.zeros((6, BLK), F32)
+        going[local][1].start()
     for copies in going:
         for copy in copies:
             copy.wait()
-
-
-def near_call(mine, chain, raw, rim, taps, key_act, values, rows):
-    return kernel_call(
-        functools.partial(near_kernel, mine, chain),
-        [("hbm", raw), ("vmem", rim), ("hbm", taps), ("hbm", key_act), ("hbm", values), ("vmem", rows)],
+    if park:
+        held.wait()
+
+
+def near_call(heads, query_raw, key_raw, rim, query_conv, key_conv, values, rows, parked=()):
+    count = len(heads)
+    inputs = [
+        ("hbm", query_raw), ("hbm", key_raw), ("vmem", rim), ("hbm", query_conv), ("hbm", key_conv),
+        ("hbm", values), ("vmem", rows),
+    ]
+    outputs = [
+        ("hbm", (BLK, count * DK), BF16),
+        ("hbm", (BLK, count * DV), NUM),
+        ("vmem", (count, 8, BLK), F32),
+    ]
+    if parked:
+        inputs += [("vmem", record) for record in parked]
+        outputs += [("hbm", parked[0].shape, BF16)]
+    return kernel_call(
+        functools.partial(near_kernel, heads, bool(parked)),
+        inputs,
+        outputs,
         [
-            ("hbm", (BLK, LOCAL * DK), BF16),
-            ("hbm", (BLK, LOCAL * DV), NUM),
-            ("vmem", (LOCAL, 8, BLK), F32),
-        ],
-        [
-            pltpu.VMEM((LOCAL, BLK, DK), BF16),
-            pltpu.VMEM((LOCAL, BLK, DK), BF16),
-            pltpu.VMEM((LOCAL, BLK, DV), BF16),
-            pltpu.VMEM((LOCAL, BLK, DK), BF16),
-            pltpu.VMEM((LOCAL, BLK, DV), NUM),
-            pltpu.VMEM((TAPS, HEADS * DK), BF16),
+            pltpu.VMEM((count, BLK, DK), BF16),
+            pltpu.VMEM((count, BLK, DK), BF16),
+            pltpu.VMEM((count, BLK, DK), BF16),
+            pltpu.VMEM((count, BLK, DV), BF16),
+            pltpu.VMEM((count, BLK, DK), BF16),
+            pltpu.VMEM((count, BLK, DV), NUM),
+            pltpu.VMEM((2, TAPS, HEADS * DK), BF16),
             pltpu.VMEM((2, BLK + 8, DK), F32),
-            pltpu.SemaphoreType.DMA((5 * LOCAL + 1,)),
+            pltpu.SemaphoreType.DMA((5 * count + 3,)),
         ],
         "near",
-        LOCAL * 2 * BLK * BLK * (DK + DV),
-        LOCAL * 5 << 20,
-    )
-
-
-def total_kernel(rule, rec_ref, out_ref):
-    count = rec_ref.shape[0]
+        count * 2 * BLK * BLK * (DK + DV),
+        count * 5 << 20,
+    )
+
+
+def total_kernel(rule, *refs):
+    records, (stack_ref, out_ref) = refs[:-2], refs[-2:]
+    _, cube, chip = place()
+    count = len(records)
+    for mask, record in enumerate(records):
+        stack_ref[mask if rule else chip ^ mask] = record[...]
     norms, tops, decays = [], [], []
     for k in range(count):
-        norm, top, decay = read_aux(rec_ref[k, DK:ROWS])
+        norm, top, decay = read_aux(stack_ref[k, DK:ROWS])
         norms.append(norm)
-        tops.append(top if rule is None else jnp.where(place()[1] > rule[k], top, EMPTY))
+        tops.append(jnp.where(cube > rule[k], top, EMPTY) if rule else top)
         decays.append(decay)
     after = jnp.zeros((1, WIDTH), F32)
     logs = [None] * count
@@ -493,63 +518,72 @@
     weights = [jnp.exp(log - peak) for log in logs]
     joined = [sum(w * n[part] for w, n in zip(weights, norms)) for part in range(SPLIT)]
     for start in range(0, DK, STEP):
-        acc = weights[0] * rec_ref[0, start : start + STEP].astype(F32)
+        acc = weights[0] * stack_ref[0, start : start + STEP].astype(F32)
         for k in range(1, count):
-            acc = acc + weights[k] * rec_ref[k, start : start + STEP].astype(F32)
+            acc = acc + weights[k] * stack_ref[k, start : start + STEP].astype(F32)
         out_ref[start : start + STEP] = acc.astype(BF16)
     out_ref[DK:ROWS] = aux_rows(joined, peak, after)
 
 
 def total_call(records, rule=None):
-    return on_chip(functools.partial(total_kernel, rule), [records], ((ROWS, WIDTH), BF16), name="total")
-
-
-def prefix_kernel(rec_ref, enter_ref, out_hbm, out_buf, sems):
-    count = rec_ref.shape[0]
+    return kernel_call(
+        functools.partial(total_kernel, rule),
+        [("vmem", record) for record in records],
+        [("vmem", (len(records), ROWS, WIDTH), BF16), ("vmem", (ROWS, WIDTH), BF16)],
+        [],
+        "total",
+        0,
+        1 << 20,
+    )
+
+
+def prefix_kernel(rec_ref, enter_ref, *refs):
+    outs, buf = refs[:-1], refs[-1]
+    _, cube, chip = place()
     norms, top, _ = read_aux(enter_ref[DK:ROWS])
-    state = (norms, jnp.where(place()[1] > 0, top, EMPTY), jnp.zeros((1, WIDTH), F32))
+    state = (norms, jnp.where(cube > 0, top, EMPTY), jnp.zeros((1, WIDTH), F32))
     weights = []
-    for k in range(count):
-        out_buf[k, DK:ROWS] = aux_rows(*state)
-        if k + 1 < count:
+    for k in range(OWNERS):
+        buf[k, DK:ROWS] = aux_rows(*state)
+        if k + 1 < OWNERS:
             early, late, state = merge(state, read_aux(rec_ref[k, DK:ROWS]))
             weights.append((early, late))
     for start in range(0, DK, STEP):
         run = enter_ref[start : start + STEP].astype(F32)
-        for k in range(count):
-            out_buf[k, start : start + STEP] = run.astype(BF16)
-            if k + 1 < count:
+        for k in range(OWNERS):
+            buf[k, start : start + STEP] = run.astype(BF16)
+            if k + 1 < OWNERS:
                 early, late = weights[k]
                 run = early * run + late * rec_ref[k, start : start + STEP].astype(F32)
-    copy = pltpu.make_async_copy(out_buf, out_hbm, sems.at[0])
-    copy.start()
-    copy.wait()
+    for mask, out_ref in enumerate(outs):
+        out_ref[...] = buf[chip ^ mask]
 
 
 def prefix_call(records, entering):
     return kernel_call(
         prefix_kernel,
         [("vmem", records), ("vmem", entering)],
-        [("hbm", records.shape, BF16)],
-        [pltpu.VMEM(records.shape, BF16), pltpu.SemaphoreType.DMA((1,))],
+        [("vmem", (ROWS, WIDTH), BF16)] * OWNERS,
+        [pltpu.VMEM(records.shape, BF16)],
         "prefix",
         0,
         2 << 20,
-    )[0]
-
-
-def far_kernel(mine, chain, query_ref, num_ref, stat_ref, enter_ref, *refs):
-    out_ref, ready, sems = refs[-3:]
+    )
+
+
+def far_kernel(mine, slots, sources, *refs):
+    near, enter_ref, (out_ref, ready, sems) = refs[: 3 * sources], refs[3 * sources], refs[-3:]
     copies = []
-    for local in range(LOCAL):
-        mid, wide = slice(local * DK, (local + 1) * DK), slice(local * DV, (local + 1) * DV)
+    for local, (source, slot) in enumerate(slots):
+        query_ref, num_ref, stat_ref = near[3 * source : 3 * source + 3]
+        mid, wide = slice(slot * DK, (slot + 1) * DK), slice(slot * DV, (slot + 1) * DV)
         at = local * PIECES
         aux = enter_ref[at, DK:ROWS]
-        _, top, _ = read_aux(aux)
+        _, far_log, _ = read_aux(aux)
+        far_log = far_log[:, 0:1]
         query = query_ref[:, mid]
-        den = stat_ref[local, 0:1]
-        near_peak = stat_ref[local, 1:2]
-        far_log = top[:, 0:1]
+        den = stat_ref[slot, 0:1]
+        near_peak = stat_ref[slot, 1:2]
         peak = jnp.maximum(near_peak, far_log)
         near_part = jnp.exp(near_peak - peak)
         far_part = jnp.exp(far_log - peak) * SCALE
@@ -562,16 +596,22 @@
             far = jnp.dot(query[t : t + STEP], memory, preferred_element_type=F32)
             near_weight = widen(near_column[t : t + STEP], DV)
             far_weight = widen(far_column[t : t + STEP], DV)
-            ready[local, t : t + STEP] = (near_weight * num_ref[t : t + STEP, wide].astype(F32) + far_weight * far).astype(BF16)
-        head = first_head(mine, chain) + local
+            near_rows = num_ref[t : t + STEP, wide].astype(F32)
+            ready[local, t : t + STEP] = (near_weight * near_rows + far_weight * far).astype(BF16)
+        head = first_head(mine, 0) + local
         copies.append(pltpu.make_async_copy(ready.at[local], out_ref.at[:, span(head, DV)], sems.at[local]))
         copies[-1].start()
     for copy in copies:
         copy.wait()
 
 
-def far_call(mine, chain, query_act, num, stat, entering, out=None):
-    operands = [pltpu.with_memory_space_constraint(x, pltpu.VMEM) for x in (query_act, num, stat, entering)]
+def far_call(mine, near, entering, out=None):
+    slots, operands = [], []
+    for source, (heads, results) in enumerate(near):
+        operands += results
+        slots += [(local, (source, slot)) for slot, (side, local) in enumerate(heads) if side == mine]
+    slots = [slot for _, slot in sorted(slots)]
+    operands = [pltpu.with_memory_space_constraint(x, pltpu.VMEM) for x in operands + [entering]]
     in_specs = [VMEM_SPEC] * len(operands)
     aliases = {}
     if out is not None:
@@ -579,7 +619,7 @@
         aliases = {len(operands): 0}
         operands.append(out)
     return pl.pallas_call(
-        functools.partial(far_kernel, mine, chain),
+        functools.partial(far_kernel, mine, slots, len(near)),
         in_specs=in_specs,
         out_specs=pl.BlockSpec(memory_space=pltpu.HBM),
         out_shape=jax.ShapeDtypeStruct((BLK, HEADS * DV), BF16),
@@ -599,55 +639,49 @@
     cubes = devices // cube_size
     line = [(i, i + 1) for i in range(devices - 1)]
     swap = [(i, i ^ 1) for i in range(devices)]
-    forward = [(i, i + 1) for i in range(0, devices, 2)]
-    owners = [
-        [g * cube_size + 2 * k + c for k in range(OWNERS)] for g in range(cubes) for c in range(2)
-    ]
     up = lambda distance: [(i, i + distance * cube_size) for i in range(devices - distance * cube_size)]
-    spread = lambda x: lax.all_to_all(x, AXES, 0, 0, axis_index_groups=owners, tiled=True)
     after = lambda x, *done: lax.optimization_barrier((x,) + done)[0]
 
-    chains = range(CHAINS)
-    key_mine, key_theirs, other_mine, first = ([None] * CHAINS for _ in range(4))
-    pieces, entering, enter_mine, enter_theirs = ([None] * CHAINS for _ in range(4))
-    near_mine, near_theirs = ([None] * CHAINS for _ in range(2))
+    def spread(records):
+        moved = {0: records[0]}
+        for mask in ORDER:
+            route = [(i, i ^ (2 * mask)) for i in range(devices)]
+            moved[mask] = lax.ppermute(records[mask], AXES, route)
+        return [moved[mask] for mask in range(OWNERS)]
 
     rim = lax.ppermute(tails_call(key_raw, query_raw), AXES, line)
     rows, key_held, taps_held, val_held = prepare_call(in_gate, forget_gate, key_raw, key_conv, values)
-
-    for c in chains:
-        sent, key_theirs[c] = state_call(False, c, key_held, rim, taps_held, val_held, rows)
-        rows = after(rows, sent)
-        other_mine[c] = lax.ppermute(sent, AXES, swap)
-    for c in chains:
-        own, key_mine[c] = state_call(True, c, key_held, rim, taps_held, val_held, rows)
-        joined, first[c] = join_call(own, other_mine[c])
-        rows = after(rows, joined)
-        pieces[c] = spread(joined)
-    for c in chains:
-        near_mine[c] = near_call(True, c, query_raw, rim, query_conv, key_mine[c], values, rows)
-        rows = after(rows, near_mine[c][0])
-        near_theirs[c] = near_call(False, c, query_raw, rim, query_conv, key_theirs[c], values, rows)
-        pieces[c] = after(pieces[c], near_theirs[c][0])
-        total = total_call(pieces[c])
-        rows = after(rows, total)
-        entering[c] = lax.ppermute(total, AXES, up(1))
-        distance = 1
-        while distance < cubes - 1:
-            earlier = lax.ppermute(entering[c], AXES, up(distance))
-            entering[c] = total_call(jnp.stack([earlier, entering[c]]), (distance, 0))
-            distance *= 2
-    for c in chains:
-        before = prefix_call(pieces[c], entering[c])
-        rows = after(rows, before)
-        enter_mine[c] = spread(before)
-    out = None
-    for c in chains:
-        keep, send = split_call(enter_mine[c], first[c])
-        enter_theirs[c] = lax.ppermute(send, AXES, swap)
-        out = far_call(True, c, *near_mine[c], keep, out)
-        out = far_call(False, c, *near_theirs[c], enter_theirs[c], out)
-    return out
+    near_args = (query_raw, key_raw, rim, query_conv, key_conv, values)
+
+    sent = state_call(False, 0, key_held, rim, taps_held, val_held, rows)
+    rows = after(rows, sent)
+    other = lax.ppermute(sent, AXES, swap)
+    own = state_call(True, 0, key_held, rim, taps_held, val_held, rows)
+    joined = join_call(own, other)
+    rows = after(rows, joined[0])
+    records = spread(joined)
+    *near_first, first = near_call(PARTS[0], *near_args, rows, (own, other))
+    records[0] = after(records[0], near_first[0])
+    stack, total = total_call(records)
+    rows = after(rows, total)
+    entering = lax.ppermute(total, AXES, up(1))
+    distance = 1
+    while distance < cubes - 1:
+        earlier = lax.ppermute(entering, AXES, up(distance))
+        entering = total_call([earlier, entering], (distance, 0))[1]
+        distance *= 2
+    near_second = near_call(PARTS[1], *near_args, rows)
+    before = prefix_call(after(stack, near_second[0]), entering)
+    rows = after(rows, before[0])
+    records = spread(before)
+    near_third = near_call(PARTS[2], *near_args, rows)
+    records[0] = after(records[0], near_third[0])
+    keep, send = split_call(records, first)
+    enter_theirs = lax.ppermute(send, AXES, swap)
+    near = list(zip(PARTS, ([*near_first], [*near_second], [*near_third])))
+    sides = [[part for part in near if any(side == mine for side, _ in part[0])] for mine in (True, False)]
+    out = far_call(True, sides[0], keep)
+    return far_call(False, sides[1], enter_theirs, out)
 
 
 def solution(mesh):

time: 80.4 us -> 71.1 us (0.88)
  blocking collectives: 24 us -> 0 us
  starting transfers between devices: 14.2 us -> 26.9 us
  waiting for transfers between devices: 4.41 us -> 7.56 us
  local copies, waits for them, and re-layouts: 0.84 us -> 0.03 us
    all_to_all x1 -> x0, blocking collectives: 24 us -> none  [on_device(): lax.all_to_all(x, AXES, 0, 0, axis_index_groups=owners, tiled=True)]
    ppermute x3 -> x17, starting transfers between devices: 7.13 us -> 24.6 us  [the longest x14 17.3 us: spread(): moved[mask] = lax.ppermute(records[mask], AXES, route)]
    all_to_all x1 -> x0, starting transfers between devices: 4.71 us -> none  [on_device(): lax.all_to_all(x, AXES, 0, 0, axis_index_groups=owners, tiled=True)]
    ppermute x3 -> x17, waiting for transfers between devices: 2.93 us -> 7.56 us  [the longest x14 7.33 us: spread(): moved[mask] = lax.ppermute(records[mask], AXES, route)]
    all_to_all x1 -> x0, waiting for transfers between devices: 1.47 us -> none  [on_device(): lax.all_to_all(x, AXES, 0, 0, axis_index_groups=owners, tiled=True)]
    unnamed x10 -> x14, local copies, waits for them, and re-layouts: 0.84 us -> 0.03 us
    pallas_call x3 -> x2, Pallas kernels: 5.16 us -> 4.88 us  [far_call(): pl.pallas_call(functools.partial(far_kernel, mine, slots, len(near)), in_...]
    pallas_call x9 -> x11, Pallas kernels: 30.9 us -> 30.8 us  [kernel_call(): pl.pallas_call(kernel, in_specs=in_specs, out_specs=[VMEM_SPEC if where =...]
  transfers between devices with their start and end apart: 5 -> 18, of which waited for: 2 -> 5; matrix products, arithmetic and copies ran while one was open for 0% -> 0% of each run, Pallas kernels for 31% -> 38%
where the time goes in v1:
time: 71.1 us; the launch traced here: 70.7 us
  Pallas kernels  35.7 us (50%)
  starting transfers between devices  26.9 us (38%)
  waiting for transfers between devices  7.56 us (11%)
    pallas_call x11, Pallas kernels, kernel_call(): pl.pallas_call(kernel, in_specs=in_specs, out_specs=[VMEM_SPEC if where =...  30.8 us
    ppermute x14, starting transfers between devices, spread(): moved[mask] = lax.ppermute(records[mask], AXES, route)  17.3 us
    ppermute x14, waiting for transfers between devices, spread(): moved[mask] = lax.ppermute(records[mask], AXES, route)  7.33 us
    pallas_call x2, Pallas kernels, far_call(): pl.pallas_call(functools.partial(far_kernel, mine, slots, len(near)), in_...  4.88 us
    ppermute x1, starting transfers between devices, on_device(): entering = lax.ppermute(total, AXES, up(1))  4.49 us
    ppermute x1, starting transfers between devices, on_device(): other = lax.ppermute(sent, AXES, swap)  2.68 us
    ppermute x1, starting transfers between devices, on_device(): rim = lax.ppermute(tails_call(key_raw, query_raw), AXES, line)  2.36 us
  transfers between devices with their start and end apart: 18, of which 5 were waited for; matrix products, arithmetic and copies ran while one was open for 0% of the time, Pallas kernels for 38%

profile of v1, /device:TPU:0, one launch (start us, length us, event | category | flops | bytes accessed | tf_op | source)
XLA Modules:
  0.0 70.7 jit_solution(12290792342305710438)
XLA Ops:
  0.0 0.9 %tails.1 = bf16[16,4096]{1,0:T(8,128)(2,1)S(1)} custom-call(bf16[512,2048]{1,0:T(8,128)(2,1)} %key_hbm.9, bf16[512,2048]{1,0:T(8,128)(2,1)} %raw_hbm.5), custom_call_target="tpu_custom_call" | custom-call | bytes 131072 | tf_op jit(solution)/shard_map/tails/pallas_call | solution.py:224
  0.9 2.4 %collective-permute-start = (bf16[16,4096]{1,0:T(8,128)(2,1)S(1)}, bf16[16,4096]{1,0:T(8,128)(2,1)S(1)}, u32[]{:S(2)}, u32[]{:S(2)}) collective-permute-start(bf16[16,4096]{1,0:T(8,128)(2,1)S(1)} %tails.1), channel_id=1, source_target_pairs={{0,1},{1,2},{2,3},{3,4},{4,5},{5,6},{6,7},{7,8},{8,9},{9,10},{10,1... | collective-permute-start | bytes 393224 | tf_op jit(solution)/shard_map/ppermute | solution.py:652
  3.3 2.9 %prepare.1 = (f32[40,512]{1,0:T(8,128)S(1)}, bf16[512,2048]{1,0:T(8,128)(2,1)S(1)}, bf16[4,2048]{1,0:T(4,128)(2,1)S(1)}, bf16[512,4096]{1,0:T(8,128)(2,1)S(1)}) custom-call(bf16[8,512]{1,0:T(8,128)(2,1)} %bitcast.2, bf16[8,512]{1,0:T(8,128)(2,1)} %bitcast.3, bf16[512,2048]{1,0:T(8,128)(2,1)} %key_hbm.9, bf16[4,2048]{1,0:T(4,128)(2,1)} %key_tap_hbm.5, ...), custom_call_target="tpu_custom_call" | custom-call | bytes 6291456 | tf_op jit(solution)/shard_map/prepare/pallas_call | solution.py:224
  6.2 3.0 %state.2 = bf16[8,272,256]{2,1,0:T(8,128)(2,1)S(1)} custom-call(bf16[512,2048]{1,0:T(8,128)(2,1)S(1)} %get-tuple-element.47.raw_ref, bf16[16,4096]{1,0:T(8,128)(2,1)S(1)} %collective-permute-done.rim_ref, bf16[4,2048]{1,0:T(4,128)(2,1)S(1)} %get-tuple-element.48.tap_ref, bf16[512,4096]{1,0:T(8,128)(2,1)S(1)} %get-tuple-element.49.val_ref, ...), custom_call_target="tpu_custom_call" | custom-call | flops 536870912 | bytes 12582912 | tf_op jit(solution)/shard_map/state/pallas_call | solution.py:224
  9.2 2.7 %collective-permute-start.1 = (bf16[8,272,256]{2,1,0:T(8,128)(2,1)S(1)}, bf16[8,272,256]{2,1,0:T(8,128)(2,1)S(1)}, u32[]{:S(2)}, u32[]{:S(2)}) collective-permute-start(bf16[8,272,256]{2,1,0:T(8,128)(2,1)S(1)} %state.2), channel_id=1, source_target_pairs={{0,1},{1,0},{2,3},{3,2},{4,5},{5,4},{6,7},{7,6},{8,9},{9,8},{10,11... | collective-permute-start | bytes 3342344 | tf_op jit(solution)/shard_map/ppermute | solution.py:658
  11.9 3.0 %state.3.own_ref.refs_0_ = bf16[8,272,256]{2,1,0:T(8,128)(2,1)S(1)} custom-call(bf16[512,2048]{1,0:T(8,128)(2,1)S(1)} %get-tuple-element.47.raw_ref, bf16[16,4096]{1,0:T(8,128)(2,1)S(1)} %collective-permute-done.rim_ref, bf16[4,2048]{1,0:T(4,128)(2,1)S(1)} %get-tuple-element.48.tap_ref, bf16[512,4096]{1,0:T(8,128)(2,1)S(1)} %get-tuple-element.49.val_ref, ...), custom_call_target="tpu_custom_call" | custom-call | flops 536870912 | bytes 12582912 | tf_op jit(solution)/shard_map/state/pallas_call | solution.py:224
  14.9 0.7 join.1
  15.6 1.5 %collective-permute-start.2 = (bf16[272,256]{1,0:T(8,128)(2,1)S(1)}, bf16[272,256]{1,0:T(8,128)(2,1)S(1)}, u32[]{:S(2)}, u32[]{:S(2)}) collective-permute-start(bf16[272,256]{1,0:T(8,128)(2,1)S(1)} %get-tuple-element.55), channel_id=1, source_target_pairs={{0,2},{1,3},{2,0},{3,1},{4,6},{5,7},{6,4},{7,5},{8,10},{9,11},{10,... | collective-permute-start | bytes 417800 | tf_op jit(solution)/shard_map/ppermute | solution.py:649
  17.1 1.5 %collective-permute-start.3 = (bf16[272,256]{1,0:T(8,128)(2,1)S(1)}, bf16[272,256]{1,0:T(8,128)(2,1)S(1)}, u32[]{:S(2)}, u32[]{:S(2)}) collective-permute-start(bf16[272,256]{1,0:T(8,128)(2,1)S(1)} %get-tuple-element.56), channel_id=1, source_target_pairs={{0,4},{1,5},{2,6},{3,7},{4,0},{5,1},{6,2},{7,3},{8,12},{9,13},{10,... | collective-permute-start | bytes 417800 | tf_op jit(solution)/shard_map/ppermute | solution.py:649
  18.7 0.7 collective-permute-start.4
  19.4 3.0 %collective-permute-start.5 = (bf16[272,256]{1,0:T(8,128)(2,1)S(1)}, bf16[272,256]{1,0:T(8,128)(2,1)S(1)}, u32[]{:S(2)}, u32[]{:S(2)}) collective-permute-start(bf16[272,256]{1,0:T(8,128)(2,1)S(1)} %get-tuple-element.58), channel_id=1, source_target_pairs={{0,8},{1,9},{2,10},{3,11},{4,12},{5,13},{6,14},{7,15},{8,0},{9,1},... | collective-permute-start | bytes 417800 | tf_op jit(solution)/shard_map/ppermute | solution.py:649
  22.4 2.6 %collective-permute-start.7 = (bf16[272,256]{1,0:T(8,128)(2,1)S(1)}, bf16[272,256]{1,0:T(8,128)(2,1)S(1)}, u32[]{:S(2)}, u32[]{:S(2)}) collective-permute-start(bf16[272,256]{1,0:T(8,128)(2,1)S(1)} %get-tuple-element.60), channel_id=1, source_target_pairs={{0,12},{1,13},{2,14},{3,15},{4,8},{5,9},{6,10},{7,11},{8,4},{9,5},... | collective-permute-start | bytes 417800 | tf_op jit(solution)/shard_map/ppermute | solution.py:649
  25.0 1.9 %collective-permute-start.8 = (bf16[272,256]{1,0:T(8,128)(2,1)S(1)}, bf16[272,256]{1,0:T(8,128)(2,1)S(1)}, u32[]{:S(2)}, u32[]{:S(2)}) collective-permute-start(bf16[272,256]{1,0:T(8,128)(2,1)S(1)} %get-tuple-element.61), channel_id=1, source_target_pairs={{0,14},{1,15},{2,12},{3,13},{4,10},{5,11},{6,8},{7,9},{8,6},{9,7},... | collective-permute-start | bytes 417800 | tf_op jit(solution)/shard_map/ppermute | solution.py:649
  26.9 8.5 %near.3 = (bf16[512,1024]{1,0:T(8,128)(2,1)}, bf16[512,2048]{1,0:T(8,128)(2,1)}, f32[4,8,512]{2,1,0:T(8,128)S(1)}, bf16[8,272,256]{2,1,0:T(8,128)(2,1)}) custom-call(bf16[512,2048]{1,0:T(8,128)(2,1)} %raw_hbm.5, bf16[512,2048]{1,0:T(8,128)(2,1)} %key_hbm.9, bf16[16,4096]{1,0:T(8,128)(2,1)S(1)} %collective-permute-done.rim_ref, bf16[4,2048]{1,0:T(4,128)(2,1)} %tap_hbm.7, ...), custom_call_target="tpu_custom_call" | custom-call | flops 1610612736 | bytes 20971520 | tf_op jit(solution)/shard_map/near/pallas_call | solution.py:224
  35.4 0.5 collective-permute-done.8.refs_7_
  35.9 0.4 total.1
  36.2 4.5 %collective-permute-start.9 = (bf16[272,256]{1,0:T(8,128)(2,1)S(1)}, bf16[272,256]{1,0:T(8,128)(2,1)S(1)}, u32[]{:S(2)}, u32[]{:S(2)}) collective-permute-start(bf16[272,256]{1,0:T(8,128)(2,1)S(1)} %get-tuple-element.62), channel_id=1, source_target_pairs={{0,16},{1,17},{2,18},{3,19},{4,20},{5,21},{6,22},{7,23},{8,24},{9,... | collective-permute-start | bytes 417800 | tf_op jit(solution)/shard_map/ppermute | solution.py:667
  40.7 5.0 %near.4 = (bf16[512,512]{1,0:T(8,128)(2,1)}, bf16[512,1024]{1,0:T(8,128)(2,1)}, f32[2,8,512]{2,1,0:T(8,128)S(1)}) custom-call(bf16[512,2048]{1,0:T(8,128)(2,1)} %raw_hbm.5, bf16[512,2048]{1,0:T(8,128)(2,1)} %key_hbm.9, bf16[16,4096]{1,0:T(8,128)(2,1)S(1)} %collective-permute-done.rim_ref, bf16[4,2048]{1,0:T(4,128)(2,1)} %tap_hbm.7, ...), custom_call_target="tpu_custom_call" | custom-call | flops 805306368 | bytes 10485760 | tf_op jit(solution)/shard_map/near/pallas_call | solution.py:224
  45.7 0.5 prefix.1
  46.2 0.7 %collective-permute-start.10 = (bf16[272,256]{1,0:T(8,128)(2,1)S(1)}, bf16[272,256]{1,0:T(8,128)(2,1)S(1)}, u32[]{:S(2)}, u32[]{:S(2)}) collective-permute-start(bf16[272,256]{1,0:T(8,128)(2,1)S(1)} %get-tuple-element.76), channel_id=1, source_target_pairs={{0,2},{1,3},{2,0},{3,1},{4,6},{5,7},{6,4},{7,5},{8,10},{9,11},{10,... | collective-permute-start | bytes 417800 | tf_op jit(solution)/shard_map/ppermute | solution.py:649
  46.9 1.4 %collective-permute-start.11 = (bf16[272,256]{1,0:T(8,128)(2,1)S(1)}, bf16[272,256]{1,0:T(8,128)(2,1)S(1)}, u32[]{:S(2)}, u32[]{:S(2)}) collective-permute-start(bf16[272,256]{1,0:T(8,128)(2,1)S(1)} %get-tuple-element.77), channel_id=1, source_target_pairs={{0,4},{1,5},{2,6},{3,7},{4,0},{5,1},{6,2},{7,3},{8,12},{9,13},{10,... | collective-permute-start | bytes 417800 | tf_op jit(solution)/shard_map/ppermute | solution.py:649
  48.3 1.4 %collective-permute-start.12 = (bf16[272,256]{1,0:T(8,128)(2,1)S(1)}, bf16[272,256]{1,0:T(8,128)(2,1)S(1)}, u32[]{:S(2)}, u32[]{:S(2)}) collective-permute-start(bf16[272,256]{1,0:T(8,128)(2,1)S(1)} %get-tuple-element.78), channel_id=1, source_target_pairs={{0,6},{1,7},{2,4},{3,5},{4,2},{5,3},{6,0},{7,1},{8,14},{9,15},{10,... | collective-permute-start | bytes 417800 | tf_op jit(solution)/shard_map/ppermute | solution.py:649
  49.8 0.9 %collective-permute-start.13 = (bf16[272,256]{1,0:T(8,128)(2,1)S(1)}, bf16[272,256]{1,0:T(8,128)(2,1)S(1)}, u32[]{:S(2)}, u32[]{:S(2)}) collective-permute-start(bf16[272,256]{1,0:T(8,128)(2,1)S(1)} %get-tuple-element.79), channel_id=1, source_target_pairs={{0,8},{1,9},{2,10},{3,11},{4,12},{5,13},{6,14},{7,15},{8,0},{9,1},... | collective-permute-start | bytes 417800 | tf_op jit(solution)/shard_map/ppermute | solution.py:649
  50.7 1.2 %collective-permute-start.14 = (bf16[272,256]{1,0:T(8,128)(2,1)S(1)}, bf16[272,256]{1,0:T(8,128)(2,1)S(1)}, u32[]{:S(2)}, u32[]{:S(2)}) collective-permute-start(bf16[272,256]{1,0:T(8,128)(2,1)S(1)} %get-tuple-element.80), channel_id=1, source_target_pairs={{0,10},{1,11},{2,8},{3,9},{4,14},{5,15},{6,12},{7,13},{8,2},{9,3},... | collective-permute-start | bytes 417800 | tf_op jit(solution)/shard_map/ppermute | solution.py:649
  51.9 3.9 %collective-permute-done.10.refs_1_ = bf16[272,256]{1,0:T(8,128)(2,1)S(1)} collective-permute-done((bf16[272,256]{1,0:T(8,128)(2,1)S(1)}, bf16[272,256]{1,0:T(8,128)(2,1)S(1)}, u32[]{:S(2)}, u32[]{:S(2)}) %collective-permute-start.10) | collective-permute-done | bytes 139296 | tf_op jit(solution)/shard_map/ppermute | solution.py:649
  55.8 0.4 collective-permute-start.16
  56.2 5.1 %near.5 = (bf16[512,512]{1,0:T(8,128)(2,1)}, bf16[512,1024]{1,0:T(8,128)(2,1)}, f32[2,8,512]{2,1,0:T(8,128)S(1)}) custom-call(bf16[512,2048]{1,0:T(8,128)(2,1)} %raw_hbm.5, bf16[512,2048]{1,0:T(8,128)(2,1)} %key_hbm.9, bf16[16,4096]{1,0:T(8,128)(2,1)S(1)} %collective-permute-done.rim_ref, bf16[4,2048]{1,0:T(4,128)(2,1)} %tap_hbm.7, ...), custom_call_target="tpu_custom_call" | custom-call | flops 805306368 | bytes 10485760 | tf_op jit(solution)/shard_map/near/pallas_call | solution.py:224
  61.4 0.5 collective-permute-done.15.refs_6_
  61.9 2.4 %collective-permute-done.16.refs_7_ = bf16[272,256]{1,0:T(8,128)(2,1)S(1)} collective-permute-done((bf16[272,256]{1,0:T(8,128)(2,1)S(1)}, bf16[272,256]{1,0:T(8,128)(2,1)S(1)}, u32[]{:S(2)}, u32[]{:S(2)}) %collective-permute-start.16) | collective-permute-done | bytes 139296 | tf_op jit(solution)/shard_map/ppermute | solution.py:649
  64.3 1.0 %split.1 = (bf16[8,272,256]{2,1,0:T(8,128)(2,1)S(1)}, bf16[8,272,256]{2,1,0:T(8,128)(2,1)S(1)}) custom-call(bf16[8,272,256]{2,1,0:T(8,128)(2,1)S(1)} %copy-done.1, bf16[272,256]{1,0:T(8,128)(2,1)S(1)} %get-tuple-element.75.refs_0_, bf16[272,256]{1,0:T(8,128)(2,1)S(1)} %collective-permute-done.10.refs_1_, ...), custom_call_target="tpu_custom_call" | custom-call | bytes 4194304 | tf_op jit(solution)/shard_map/split/pallas_call | solution.py:224
  65.4 2.4 %far.2.refs_7_ = bf16[512,4096]{1,0:T(8,128)(2,1)} custom-call(bf16[512,1024]{1,0:T(8,128)(2,1)S(1)} %copy-done.4, bf16[512,2048]{1,0:T(8,128)(2,1)S(1)} %copy-done, f32[4,8,512]{2,1,0:T(8,128)S(1)} %get-tuple-element.85.refs_2_, bf16[8,272,256]{2,1,0:T(8,128)(2,1)S(1)} %get-tuple-element.86.refs_3_), custom_call_target="tpu_custom_call" | custom-call | flops 536870912 | bytes 20971520 | tf_op jit(solution)/shard_map/far/pallas_call | solution.py:621
  68.1 2.4 %far.3 = bf16[512,4096]{1,0:T(8,128)(2,1)} custom-call(bf16[512,512]{1,0:T(8,128)(2,1)S(1)} %copy-done.5, bf16[512,1024]{1,0:T(8,128)(2,1)S(1)} %copy-done.2, f32[2,8,512]{2,1,0:T(8,128)S(1)} %get-tuple-element.66.refs_2_, bf16[512,512]{1,0:T(8,128)(2,1)S(1)} %copy-done.6, bf16[512,1024]{1,0:T(8,128)(2,1)S(1)} %copy-done.3, ...), custom_call_target="tpu_custom_call", output_to_operand_aliasing={{}: (7, {})} | custom-call | flops 536870912 | bytes 20971520 | tf_op jit(solution)/shard_map/far/pallas_call | solution.py:621
  (31 shorter events, 0.4 us)
Async XLA Ops:
  0.9 5.3 %collective-permute-start = (bf16[16,4096]{1,0:T(8,128)(2,1)S(1)}, bf16[16,4096]{1,0:T(8,128)(2,1)S(1)}, u32[]{:S(2)}, u32[]{:S(2)}) collective-permute-start(bf16[16,4096]{1,0:T(8,128)(2,1)S(1)} %tails.1), channel_id=1, source_target_pairs={{0,1},{1,2},{2,3},{3,4},{4,5},{5,6},{6,7},{7,8},{8,9},{9,10},{10,1... | collective-permute-start | bytes 393224 | tf_op jit(solution)/shard_map/ppermute | solution.py:652
  9.2 5.7 %collective-permute-start.1 = (bf16[8,272,256]{2,1,0:T(8,128)(2,1)S(1)}, bf16[8,272,256]{2,1,0:T(8,128)(2,1)S(1)}, u32[]{:S(2)}, u32[]{:S(2)}) collective-permute-start(bf16[8,272,256]{2,1,0:T(8,128)(2,1)S(1)} %state.2), channel_id=1, source_target_pairs={{0,1},{1,0},{2,3},{3,2},{4,5},{5,4},{6,7},{7,6},{8,9},{9,8},{10,11... | collective-permute-start | bytes 3342344 | tf_op jit(solution)/shard_map/ppermute | solution.py:658
  15.6 6.8 %collective-permute-start.2 = (bf16[272,256]{1,0:T(8,128)(2,1)S(1)}, bf16[272,256]{1,0:T(8,128)(2,1)S(1)}, u32[]{:S(2)}, u32[]{:S(2)}) collective-permute-start(bf16[272,256]{1,0:T(8,128)(2,1)S(1)} %get-tuple-element.55), channel_id=1, source_target_pairs={{0,2},{1,3},{2,0},{3,1},{4,6},{5,7},{6,4},{7,5},{8,10},{9,11},{10,... | collective-permute-start | bytes 417800 | tf_op jit(solution)/shard_map/ppermute | solution.py:649
  17.1 7.9 %collective-permute-start.3 = (bf16[272,256]{1,0:T(8,128)(2,1)S(1)}, bf16[272,256]{1,0:T(8,128)(2,1)S(1)}, u32[]{:S(2)}, u32[]{:S(2)}) collective-permute-start(bf16[272,256]{1,0:T(8,128)(2,1)S(1)} %get-tuple-element.56), channel_id=1, source_target_pairs={{0,4},{1,5},{2,6},{3,7},{4,0},{5,1},{6,2},{7,3},{8,12},{9,13},{10,... | collective-permute-start | bytes 417800 | tf_op jit(solution)/shard_map/ppermute | solution.py:649
  18.7 16.7 %collective-permute-start.4 = (bf16[272,256]{1,0:T(8,128)(2,1)S(1)}, bf16[272,256]{1,0:T(8,128)(2,1)S(1)}, u32[]{:S(2)}, u32[]{:S(2)}) collective-permute-start(bf16[272,256]{1,0:T(8,128)(2,1)S(1)} %get-tuple-element.57), channel_id=1, source_target_pairs={{0,6},{1,7},{2,4},{3,5},{4,2},{5,3},{6,0},{7,1},{8,14},{9,15},{10,... | collective-permute-start | bytes 417800 | tf_op jit(solution)/shard_map/ppermute | solution.py:649
  19.4 16.0 %collective-permute-start.5 = (bf16[272,256]{1,0:T(8,128)(2,1)S(1)}, bf16[272,256]{1,0:T(8,128)(2,1)S(1)}, u32[]{:S(2)}, u32[]{:S(2)}) collective-permute-start(bf16[272,256]{1,0:T(8,128)(2,1)S(1)} %get-tuple-element.58), channel_id=1, source_target_pairs={{0,8},{1,9},{2,10},{3,11},{4,12},{5,13},{6,14},{7,15},{8,0},{9,1},... | collective-permute-start | bytes 417800 | tf_op jit(solution)/shard_map/ppermute | solution.py:649
  22.4 13.0 %collective-permute-start.6 = (bf16[272,256]{1,0:T(8,128)(2,1)S(1)}, bf16[272,256]{1,0:T(8,128)(2,1)S(1)}, u32[]{:S(2)}, u32[]{:S(2)}) collective-permute-start(bf16[272,256]{1,0:T(8,128)(2,1)S(1)} %get-tuple-element.59), channel_id=1, source_target_pairs={{0,10},{1,11},{2,8},{3,9},{4,14},{5,15},{6,12},{7,13},{8,2},{9,3},... | collective-permute-start | bytes 417800 | tf_op jit(solution)/shard_map/ppermute | solution.py:649
  22.4 13.0 %collective-permute-start.7 = (bf16[272,256]{1,0:T(8,128)(2,1)S(1)}, bf16[272,256]{1,0:T(8,128)(2,1)S(1)}, u32[]{:S(2)}, u32[]{:S(2)}) collective-permute-start(bf16[272,256]{1,0:T(8,128)(2,1)S(1)} %get-tuple-element.60), channel_id=1, source_target_pairs={{0,12},{1,13},{2,14},{3,15},{4,8},{5,9},{6,10},{7,11},{8,4},{9,5},... | collective-permute-start | bytes 417800 | tf_op jit(solution)/shard_map/ppermute | solution.py:649
  25.0 10.9 %collective-permute-start.8 = (bf16[272,256]{1,0:T(8,128)(2,1)S(1)}, bf16[272,256]{1,0:T(8,128)(2,1)S(1)}, u32[]{:S(2)}, u32[]{:S(2)}) collective-permute-start(bf16[272,256]{1,0:T(8,128)(2,1)S(1)} %get-tuple-element.61), channel_id=1, source_target_pairs={{0,14},{1,15},{2,12},{3,13},{4,10},{5,11},{6,8},{7,9},{8,6},{9,7},... | collective-permute-start | bytes 417800 | tf_op jit(solution)/shard_map/ppermute | solution.py:649
  36.2 9.5 %collective-permute-start.9 = (bf16[272,256]{1,0:T(8,128)(2,1)S(1)}, bf16[272,256]{1,0:T(8,128)(2,1)S(1)}, u32[]{:S(2)}, u32[]{:S(2)}) collective-permute-start(bf16[272,256]{1,0:T(8,128)(2,1)S(1)} %get-tuple-element.62), channel_id=1, source_target_pairs={{0,16},{1,17},{2,18},{3,19},{4,20},{5,21},{6,22},{7,23},{8,24},{9,... | collective-permute-start | bytes 417800 | tf_op jit(solution)/shard_map/ppermute | solution.py:667
  46.2 9.6 %collective-permute-start.10 = (bf16[272,256]{1,0:T(8,128)(2,1)S(1)}, bf16[272,256]{1,0:T(8,128)(2,1)S(1)}, u32[]{:S(2)}, u32[]{:S(2)}) collective-permute-start(bf16[272,256]{1,0:T(8,128)(2,1)S(1)} %get-tuple-element.76), channel_id=1, source_target_pairs={{0,2},{1,3},{2,0},{3,1},{4,6},{5,7},{6,4},{7,5},{8,10},{9,11},{10,... | collective-permute-start | bytes 417800 | tf_op jit(solution)/shard_map/ppermute | solution.py:649
  46.9 8.9 %collective-permute-start.11 = (bf16[272,256]{1,0:T(8,128)(2,1)S(1)}, bf16[272,256]{1,0:T(8,128)(2,1)S(1)}, u32[]{:S(2)}, u32[]{:S(2)}) collective-permute-start(bf16[272,256]{1,0:T(8,128)(2,1)S(1)} %get-tuple-element.77), channel_id=1, source_target_pairs={{0,4},{1,5},{2,6},{3,7},{4,0},{5,1},{6,2},{7,3},{8,12},{9,13},{10,... | collective-permute-start | bytes 417800 | tf_op jit(solution)/shard_map/ppermute | solution.py:649
  48.3 13.0 %collective-permute-start.12 = (bf16[272,256]{1,0:T(8,128)(2,1)S(1)}, bf16[272,256]{1,0:T(8,128)(2,1)S(1)}, u32[]{:S(2)}, u32[]{:S(2)}) collective-permute-start(bf16[272,256]{1,0:T(8,128)(2,1)S(1)} %get-tuple-element.78), channel_id=1, source_target_pairs={{0,6},{1,7},{2,4},{3,5},{4,2},{5,3},{6,0},{7,1},{8,14},{9,15},{10,... | collective-permute-start | bytes 417800 | tf_op jit(solution)/shard_map/ppermute | solution.py:649
  49.8 11.6 %collective-permute-start.13 = (bf16[272,256]{1,0:T(8,128)(2,1)S(1)}, bf16[272,256]{1,0:T(8,128)(2,1)S(1)}, u32[]{:S(2)}, u32[]{:S(2)}) collective-permute-start(bf16[272,256]{1,0:T(8,128)(2,1)S(1)} %get-tuple-element.79), channel_id=1, source_target_pairs={{0,8},{1,9},{2,10},{3,11},{4,12},{5,13},{6,14},{7,15},{8,0},{9,1},... | collective-permute-start | bytes 417800 | tf_op jit(solution)/shard_map/ppermute | solution.py:649
  50.7 10.7 %collective-permute-start.14 = (bf16[272,256]{1,0:T(8,128)(2,1)S(1)}, bf16[272,256]{1,0:T(8,128)(2,1)S(1)}, u32[]{:S(2)}, u32[]{:S(2)}) collective-permute-start(bf16[272,256]{1,0:T(8,128)(2,1)S(1)} %get-tuple-element.80), channel_id=1, source_target_pairs={{0,10},{1,11},{2,8},{3,9},{4,14},{5,15},{6,12},{7,13},{8,2},{9,3},... | collective-permute-start | bytes 417800 | tf_op jit(solution)/shard_map/ppermute | solution.py:649
  55.8 6.1 %collective-permute-start.15 = (bf16[272,256]{1,0:T(8,128)(2,1)S(1)}, bf16[272,256]{1,0:T(8,128)(2,1)S(1)}, u32[]{:S(2)}, u32[]{:S(2)}) collective-permute-start(bf16[272,256]{1,0:T(8,128)(2,1)S(1)} %get-tuple-element.81), channel_id=1, source_target_pairs={{0,12},{1,13},{2,14},{3,15},{4,8},{5,9},{6,10},{7,11},{8,4},{9,5},... | collective-permute-start | bytes 417800 | tf_op jit(solution)/shard_map/ppermute | solution.py:649
  55.8 8.4 %collective-permute-start.16 = (bf16[272,256]{1,0:T(8,128)(2,1)S(1)}, bf16[272,256]{1,0:T(8,128)(2,1)S(1)}, u32[]{:S(2)}, u32[]{:S(2)}) collective-permute-start(bf16[272,256]{1,0:T(8,128)(2,1)S(1)} %get-tuple-element.82), channel_id=1, source_target_pairs={{0,14},{1,15},{2,12},{3,13},{4,10},{5,11},{6,8},{7,9},{8,6},{9,7},... | collective-permute-start | bytes 417800 | tf_op jit(solution)/shard_map/ppermute | solution.py:649
  56.2 8.1 %copy-start.1 = (bf16[8,272,256]{2,1,0:T(8,128)(2,1)S(1)}, bf16[8,272,256]{2,1,0:T(8,128)(2,1)}, u32[]{:S(2)}) copy-start(bf16[8,272,256]{2,1,0:T(8,128)(2,1)} %get-tuple-element.74.first_ref) | copy-start | bytes 3342340
  56.2 9.1 %copy-start.4 = (bf16[512,1024]{1,0:T(8,128)(2,1)S(1)}, bf16[512,1024]{1,0:T(8,128)(2,1)}, u32[]{:S(2)}) copy-start(bf16[512,1024]{1,0:T(8,128)(2,1)} %get-tuple-element.53.refs_0_) | copy-start | bytes 3145732
  61.3 4.0 %copy-start = (bf16[512,2048]{1,0:T(8,128)(2,1)S(1)}, bf16[512,2048]{1,0:T(8,128)(2,1)}, u32[]{:S(2)}) copy-start(bf16[512,2048]{1,0:T(8,128)(2,1)} %get-tuple-element.84.refs_1_) | copy-start | bytes 6291460
  65.2 2.8 %collective-permute-start.17 = (bf16[8,272,256]{2,1,0:T(8,128)(2,1)S(1)}, bf16[8,272,256]{2,1,0:T(8,128)(2,1)S(1)}, u32[]{:S(2)}, u32[]{:S(2)}) collective-permute-start(bf16[8,272,256]{2,1,0:T(8,128)(2,1)S(1)} %get-tuple-element.83), channel_id=1, source_target_pairs={{0,1},{1,0},{2,3},{3,2},{4,5},{5,4},{6,7},{7,6},{8,9},{9,8},{10,11... | collective-permute-start | bytes 3342344 | tf_op jit(solution)/shard_map/ppermute | solution.py:680
  65.3 2.7 %copy-start.2 = (bf16[512,1024]{1,0:T(8,128)(2,1)S(1)}, bf16[512,1024]{1,0:T(8,128)(2,1)}, u32[]{:S(2)}) copy-start(bf16[512,1024]{1,0:T(8,128)(2,1)} %get-tuple-element.65.refs_1_) | copy-start | bytes 3145732
  65.3 2.7 %copy-start.3 = (bf16[512,1024]{1,0:T(8,128)(2,1)S(1)}, bf16[512,1024]{1,0:T(8,128)(2,1)}, u32[]{:S(2)}) copy-start(bf16[512,1024]{1,0:T(8,128)(2,1)} %get-tuple-element.72.refs_4_) | copy-start | bytes 3145732
  65.3 2.7 %copy-start.5 = (bf16[512,512]{1,0:T(8,128)(2,1)S(1)}, bf16[512,512]{1,0:T(8,128)(2,1)}, u32[]{:S(2)}) copy-start(bf16[512,512]{1,0:T(8,128)(2,1)} %get-tuple-element.64.refs_0_) | copy-start | bytes 1572868
  65.4 2.7 %copy-start.6 = (bf16[512,512]{1,0:T(8,128)(2,1)S(1)}, bf16[512,512]{1,0:T(8,128)(2,1)}, u32[]{:S(2)}) copy-start(bf16[512,512]{1,0:T(8,128)(2,1)} %get-tuple-element.71.refs_3_) | copy-start | bytes 1572868

commit v2 on v1

--- a/solution.py
+++ b/solution.py
@@ -18,7 +18,9 @@
 WIDTH = LOCAL * DV // OWNERS
 PIECES = DV // WIDTH
 SPLIT = DK // WIDTH
-AUX = 16
+AUX = 8
+RIM = 8
+EARLY = 16
 ROWS = DK + AUX
 BLK = 512
 TAPS = 4
@@ -27,7 +29,7 @@
 EMPTY = -1e30
 ORDER = (7, 6, 5, 3, 4, 2, 1)
 SIDES = [(True, local) for local in range(LOCAL)] + [(False, local) for local in range(LOCAL)]
-PARTS = (SIDES[:4], SIDES[4:6], SIDES[6:])
+PARTS = (SIDES[:5], SIDES[5:6], SIDES[6:])
 SCALE = DK**-0.5
 F32 = jnp.float32
 BF16 = jnp.bfloat16
@@ -122,7 +124,7 @@
 
 def tails_kernel(key_hbm, query_hbm, out_ref, sems):
     width = key_hbm.shape[1]
-    last = pl.ds(BLK - AUX, AUX)
+    last = pl.ds(BLK - RIM, RIM)
     for copy in start_all(
         [
             pltpu.make_async_copy(key_hbm.at[last], out_ref.at[:, 0:width], sems.at[0]),
@@ -136,7 +138,7 @@
     return kernel_call(
         tails_kernel,
         [("hbm", key_raw), ("hbm", query_raw)],
-        [("vmem", (AUX, 2 * key_raw.shape[1]), BF16)],
+        [("vmem", (RIM, 2 * key_raw.shape[1]), BF16)],
         [pltpu.SemaphoreType.DMA((2,))],
         "tails",
         0,
@@ -237,7 +239,7 @@
 
 
 def conv_rows(columns, rim_columns, raw, rim_ref, tap_ref, padded):
-    padded[0:8] = rim_ref[:, rim_columns].astype(F32)[8:16]
+    padded[0:8] = rim_ref[:, rim_columns].astype(F32)
     padded[8 : 8 + BLK] = raw.astype(F32)
     taps = tap_ref[:, columns].astype(F32)
     for start in range(0, BLK, STEP):
@@ -254,38 +256,109 @@
     return copies
 
 
-def state_kernel(mine, chain, raw_ref, rim_ref, tap_ref, val_ref, rows_ref, rec_ref, padded, weighted):
-    head0 = first_head(mine, chain)
+def write_record(rec_ref, local, memory, norm, top, decay):
+    aux = aux_rows([norm[:, k * WIDTH : (k + 1) * WIDTH] for k in range(SPLIT)], top, decay)
+    for piece in range(PIECES):
+        at = local * PIECES + piece
+        rec_ref[at, 0:DK] = memory[:, piece * WIDTH : (piece + 1) * WIDTH].astype(BF16)
+        rec_ref[at, DK:ROWS] = aux
+
+
+def outer(weighted, values):
+    return lax.dot_general(weighted, values, (((0,), (0,)), ((), ())), preferred_element_type=F32)
+
+
+def state_kernel(raw_ref, rim_ref, tap_ref, val_ref, rows_ref, rec_ref, act_ref, padded, weighted):
     for local in range(LOCAL):
-        head = head0 + local
+        head = first_head(True, 0) + local
         weight = column(row_of(rows_ref, 2, head))
         norm = jnp.zeros((1, DK), F32)
         columns = span(head, DK)
         for start, act in conv_rows(columns, columns, raw_ref[:, columns], rim_ref, tap_ref, padded.at[local % 2]):
+            act_ref[start : start + STEP, local * DK : (local + 1) * DK] = act
             scaled = act.astype(F32) * widen(weight[start : start + STEP], DK)
             norm = norm + jnp.sum(scaled, axis=0, keepdims=True)
             weighted[local % 2, start : start + STEP] = scaled.astype(BF16)
-        memory = lax.dot_general(
-            weighted[local % 2], val_ref[:, span(head, DV)], (((0,), (0,)), ((), ())), preferred_element_type=F32
-        )
+        memory = outer(weighted[local % 2], val_ref[:, span(head, DV)])
         top = row_of(rows_ref, 3, head)[:, :WIDTH]
         decay = row_of(rows_ref, 4, head)[:, :WIDTH]
-        aux = aux_rows([norm[:, k * WIDTH : (k + 1) * WIDTH] for k in range(SPLIT)], top, decay)
-        for piece in range(PIECES):
-            at = local * PIECES + piece
-            rec_ref[at, 0:DK] = memory[:, piece * WIDTH : (piece + 1) * WIDTH].astype(BF16)
-            rec_ref[at, DK:ROWS] = aux
-
-
-def state_call(mine, chain, raw, rim, taps, values, rows):
-    return kernel_call(
-        functools.partial(state_kernel, mine, chain),
+        write_record(rec_ref, local, memory, norm, top, decay)
+
+
+def state_call(raw, rim, taps, values, rows):
+    return kernel_call(
+        state_kernel,
         [("vmem", raw), ("vmem", rim), ("vmem", taps), ("vmem", values), ("vmem", rows)],
-        [("vmem", (OWNERS, ROWS, WIDTH), BF16)],
+        [("vmem", (OWNERS, ROWS, WIDTH), BF16), ("vmem", (BLK, LOCAL * DK), BF16)],
         [pltpu.VMEM((2, BLK + 8, DK), F32), pltpu.VMEM((2, BLK, DK), BF16)],
         "state",
         LOCAL * 2 * BLK * DK * DV,
         LOCAL * 3 << 20,
+    )
+
+
+def late_state_kernel(raw_ref, tap_ref, val_ref, rows_ref, memory_ref, norm_ref, no_rim, padded, weighted):
+    no_rim[...] = jnp.zeros((RIM, HEADS * DK), BF16)
+    lanes = lax.broadcasted_iota(jnp.int32, (1, BLK), 1)
+    for local in range(LOCAL):
+        head = first_head(False, 0) + local
+        weight = column(jnp.where(lanes >= EARLY, row_of(rows_ref, 2, head), 0.0))
+        norm = jnp.zeros((1, DK), F32)
+        columns = span(head, DK)
+        for start, act in conv_rows(columns, columns, raw_ref[:, columns], no_rim, tap_ref, padded.at[local % 2]):
+            scaled = act.astype(F32) * widen(weight[start : start + STEP], DK)
+            norm = norm + jnp.sum(scaled, axis=0, keepdims=True)
+            weighted[local % 2, start : start + STEP] = scaled.astype(BF16)
+        memory_ref[local] = outer(weighted[local % 2], val_ref[:, span(head, DV)])
+        norm_ref[local] = jnp.broadcast_to(norm, (8, DK))
+
+
+def late_state_call(raw, taps, values, rows):
+    return kernel_call(
+        late_state_kernel,
+        [("vmem", raw), ("vmem", taps), ("vmem", values), ("vmem", rows)],
+        [("vmem", (LOCAL, DK, DV), F32), ("vmem", (LOCAL, 8, DK), F32)],
+        [
+            pltpu.VMEM((RIM, HEADS * DK), BF16),
+            pltpu.VMEM((2, BLK + 8, DK), F32),
+            pltpu.VMEM((2, BLK, DK), BF16),
+        ],
+        "late_state",
+        LOCAL * 2 * BLK * DK * DV,
+        LOCAL * 3 << 20,
+    )
+
+
+def early_state_kernel(raw_ref, rim_ref, tap_ref, val_ref, rows_ref, memory_ref, norm_ref, rec_ref, padded):
+    for local in range(LOCAL):
+        head = first_head(False, 0) + local
+        columns = span(head, DK)
+        weight = column(row_of(rows_ref, 2, head)[:, 0:128])[0:EARLY]
+        padded[local, 0:8] = rim_ref[:, columns].astype(F32)
+        padded[local, 8 : 8 + EARLY] = raw_ref[0:EARLY, columns].astype(F32)
+        taps = tap_ref[:, columns].astype(F32)
+        first = 8 - (TAPS - 1)
+        mixed = taps[0:1] * padded[local, first : first + EARLY]
+        for tap in range(1, TAPS):
+            mixed = mixed + taps[tap : tap + 1] * padded[local, first + tap : first + tap + EARLY]
+        act = (mixed * (0.5 * jnp.tanh(0.5 * mixed) + 0.5)).astype(BF16)
+        scaled = act.astype(F32) * widen(weight, DK)
+        norm = norm_ref[local, 0:1] + jnp.sum(scaled, axis=0, keepdims=True)
+        memory = memory_ref[local] + outer(scaled.astype(BF16), val_ref[0:EARLY, span(head, DV)])
+        top = row_of(rows_ref, 3, head)[:, :WIDTH]
+        decay = row_of(rows_ref, 4, head)[:, :WIDTH]
+        write_record(rec_ref, local, memory, norm, top, decay)
+
+
+def early_state_call(raw, rim, taps, values, rows, memory, norm):
+    return kernel_call(
+        early_state_kernel,
+        [("vmem", x) for x in (raw, rim, taps, values, rows, memory, norm)],
+        [("vmem", (OWNERS, ROWS, WIDTH), BF16)],
+        [pltpu.VMEM((LOCAL, 8 + EARLY, DK), F32)],
+        "early_state",
+        1 << 20,
+        4 << 20,
     )[0]
 
 
@@ -375,9 +448,9 @@
 ):
     count = len(heads)
     if park:
-        own_ref, other_ref = refs[:2]
-        first_hbm = refs[5]
-        refs = refs[2:5] + refs[6:]
+        own_ref, other_ref, act_ref = refs[:3]
+        first_hbm = refs[6]
+        refs = refs[3:6] + refs[7:]
     (
         query_hbm, num_hbm, stat_ref,
         raw_buf, raw_key_buf, key_buf, val_buf, query_buf, num_buf, tap_buf, padded, sems,
@@ -413,7 +486,8 @@
             (num_buf.at[local], num_hbm.at[:, wide]),
         )
         copies = [pltpu.make_async_copy(a, b, sems.at[5 * local + k]) for k, (a, b) in enumerate(pairs)]
-        coming.append(start_all(copies[:3]))
+        held_key = park and heads[local][0]
+        coming.append(start_all(copies[:1] + copies[2:3] if held_key else copies[:3]))
         going.append(copies[3:])
     for copy in taps_in:
         copy.wait()
@@ -427,15 +501,19 @@
         for start, act in conv_rows(columns, rim_columns, raw_buf[local], rim_ref, tap_buf.at[0], padded.at[0]):
             query_buf[local, start : start + STEP] = act
         going[local][0].start()
-        coming[local][1].wait()
-        for start, act in conv_rows(columns, columns, raw_key_buf[local], rim_ref, tap_buf.at[1], padded.at[1]):
-            key_buf[local, start : start + STEP] = act
-        coming[local][2].wait()
+        if park and heads[local][0]:
+            key_act = act_ref.at[:, (local * DK) : (local + 1) * DK]
+        else:
+            coming[local][1].wait()
+            for start, act in conv_rows(columns, columns, raw_key_buf[local], rim_ref, tap_buf.at[1], padded.at[1]):
+                key_buf[local, start : start + STEP] = act
+            key_act = key_buf.at[local]
+        coming[local][-1].wait()
         peak = row_of(rows_ref, 1, head)
         level = row_of(rows_ref, 0, head)
         peak_column = column(peak)
         scores = {
-            s: lax.dot_general(query_buf[local, s:BLK], key_buf[local, s : s + TILE], NT, preferred_element_type=F32)
+            s: lax.dot_general(query_buf[local, s:BLK], key_act[s : s + TILE], NT, preferred_element_type=F32)
             for s in range(0, BLK, TILE)
         }
         for t in range(0, BLK, TILE):
@@ -653,14 +731,15 @@
     rows, key_held, taps_held, val_held = prepare_call(in_gate, forget_gate, key_raw, key_conv, values)
     near_args = (query_raw, key_raw, rim, query_conv, key_conv, values)
 
-    sent = state_call(False, 0, key_held, rim, taps_held, val_held, rows)
+    late = late_state_call(key_held, taps_held, val_held, rows)
+    sent = early_state_call(key_held, rim, taps_held, val_held, rows, *late)
     rows = after(rows, sent)
     other = lax.ppermute(sent, AXES, swap)
-    own = state_call(True, 0, key_held, rim, taps_held, val_held, rows)
+    own, key_act = state_call(key_held, rim, taps_held, val_held, rows)
     joined = join_call(own, other)
     rows = after(rows, joined[0])
     records = spread(joined)
-    *near_first, first = near_call(PARTS[0], *near_args, rows, (own, other))
+    *near_first, first = near_call(PARTS[0], *near_args, rows, (own, other, key_act))
     records[0] = after(records[0], near_first[0])
     stack, total = total_call(records)
     rows = after(rows, total)

time: 71.1 us -> 68.1 us (0.958)
  waiting for transfers between devices: 7.56 us -> 3.72 us
  starting transfers between devices: 26.9 us -> 28.6 us
  Pallas kernels: 35.7 us -> 34.7 us
    ppermute x14, waiting for transfers between devices: 7.33 us -> 3.67 us  [spread(): moved[mask] = lax.ppermute(records[mask], AXES, route)]
    ppermute x14, starting transfers between devices: 17.3 us -> 19 us  [spread(): moved[mask] = lax.ppermute(records[mask], AXES, route)]
    pallas_call x11 -> x12, Pallas kernels: 30.8 us -> 29.9 us  [kernel_call(): pl.pallas_call(kernel, in_specs=in_specs, out_specs=[VMEM_SPEC if where =...]
  transfers between devices with their start and end apart: 18 -> 18, of which waited for: 5 -> 2; matrix products, arithmetic and copies ran while one was open for 0% -> 0% of each run, Pallas kernels for 38% -> 42%
where the time goes in v2:
time: 68.1 us; the launch traced here: 67.7 us
  Pallas kernels  34.7 us (51%)
  starting transfers between devices  28.6 us (42%)
  waiting for transfers between devices  3.72 us (5%)
    pallas_call x12, Pallas kernels, kernel_call(): pl.pallas_call(kernel, in_specs=in_specs, out_specs=[VMEM_SPEC if where =...  29.9 us
    ppermute x14, starting transfers between devices, spread(): moved[mask] = lax.ppermute(records[mask], AXES, route)  19 us
    pallas_call x2, Pallas kernels, far_call(): pl.pallas_call(functools.partial(far_kernel, mine, slots, len(near)), in_...  4.84 us
    ppermute x1, starting transfers between devices, on_device(): entering = lax.ppermute(total, AXES, up(1))  4.5 us
    ppermute x14, waiting for transfers between devices, spread(): moved[mask] = lax.ppermute(records[mask], AXES, route)  3.67 us
    ppermute x1, starting transfers between devices, on_device(): other = lax.ppermute(sent, AXES, swap)  2.71 us
    ppermute x1, starting transfers between devices, on_device(): rim = lax.ppermute(tails_call(key_raw, query_raw), AXES, line)  2.36 us
  transfers between devices with their start and end apart: 18, of which 2 were waited for; matrix products, arithmetic and copies ran while one was open for 0% of the time, Pallas kernels for 42%

profile of v2, /device:TPU:0, one launch (start us, length us, event | category | flops | bytes accessed | tf_op | source)
XLA Modules:
  0.0 67.7 jit_solution(14831178622501433134)
XLA Ops:
  0.0 0.8 %tails.1 = bf16[8,4096]{1,0:T(8,128)(2,1)S(1)} custom-call(bf16[512,2048]{1,0:T(8,128)(2,1)} %key_hbm.9, bf16[512,2048]{1,0:T(8,128)(2,1)} %raw_hbm.5), custom_call_target="tpu_custom_call" | custom-call | bytes 131072 | tf_op jit(solution)/shard_map/tails/pallas_call | solution.py:226
  0.8 2.4 %collective-permute-start = (bf16[8,4096]{1,0:T(8,128)(2,1)S(1)}, bf16[8,4096]{1,0:T(8,128)(2,1)S(1)}, u32[]{:S(2)}, u32[]{:S(2)}) collective-permute-start(bf16[8,4096]{1,0:T(8,128)(2,1)S(1)} %tails.1), channel_id=1, source_target_pairs={{0,1},{1,2},{2,3},{3,4},{4,5},{5,6},{6,7},{7,8},{8,9},{9,10},{10,1... | collective-permute-start | bytes 196616 | tf_op jit(solution)/shard_map/ppermute | solution.py:730
  3.2 2.9 %prepare.1 = (f32[40,512]{1,0:T(8,128)S(1)}, bf16[512,2048]{1,0:T(8,128)(2,1)S(1)}, bf16[4,2048]{1,0:T(4,128)(2,1)S(1)}, bf16[512,4096]{1,0:T(8,128)(2,1)S(1)}) custom-call(bf16[8,512]{1,0:T(8,128)(2,1)} %bitcast.2, bf16[8,512]{1,0:T(8,128)(2,1)} %bitcast.3, bf16[512,2048]{1,0:T(8,128)(2,1)} %key_hbm.9, bf16[4,2048]{1,0:T(4,128)(2,1)} %key_tap_hbm.5, ...), custom_call_target="tpu_custom_call" | custom-call | bytes 6291456 | tf_op jit(solution)/shard_map/prepare/pallas_call | solution.py:226
  6.1 2.9 %late_state.1 = (f32[4,256,512]{2,1,0:T(8,128)S(1)}, f32[4,8,256]{2,1,0:T(8,128)S(1)}) custom-call(bf16[512,2048]{1,0:T(8,128)(2,1)S(1)} %get-tuple-element.51.raw_ref, bf16[4,2048]{1,0:T(4,128)(2,1)S(1)} %get-tuple-element.52.tap_ref, bf16[512,4096]{1,0:T(8,128)(2,1)S(1)} %get-tuple-element.53.val_ref, f32[40,512]{1,0:T(8,128)S(1)} %get-tuple-element.80.rows_ref), custom_call_target="tpu_custom_call" | custom-call | flops 536870912 | bytes 12582912 | tf_op jit(solution)/shard_map/late_state/pallas_call | solution.py:226
  9.0 0.8 %early_state.1 = bf16[8,264,256]{2,1,0:T(8,128)(2,1)S(1)} custom-call(bf16[512,2048]{1,0:T(8,128)(2,1)S(1)} %get-tuple-element.51.raw_ref, bf16[8,4096]{1,0:T(8,128)(2,1)S(1)} %collective-permute-done.rim_ref, bf16[4,2048]{1,0:T(4,128)(2,1)S(1)} %get-tuple-element.52.tap_ref, bf16[512,4096]{1,0:T(8,128)(2,1)S(1)} %get-tuple-element.53.val_ref, ...), custom_call_target="tpu_custom_call" | custom-call | flops 1048576 | bytes 4194304 | tf_op jit(solution)/shard_map/early_state/pallas_call | solution.py:226
  9.8 2.7 %collective-permute-start.1 = (bf16[8,264,256]{2,1,0:T(8,128)(2,1)S(1)}, bf16[8,264,256]{2,1,0:T(8,128)(2,1)S(1)}, u32[]{:S(2)}, u32[]{:S(2)}) collective-permute-start(bf16[8,264,256]{2,1,0:T(8,128)(2,1)S(1)} %early_state.1), channel_id=1, source_target_pairs={{0,1},{1,0},{2,3},{3,2},{4,5},{5,4},{6,7},{7,6},{8,9},{9,8},{10,11... | collective-permute-start | bytes 3244040 | tf_op jit(solution)/shard_map/ppermute | solution.py:737
  12.5 3.3 %state.1 = (bf16[8,264,256]{2,1,0:T(8,128)(2,1)S(1)}, bf16[512,1024]{1,0:T(8,128)(2,1)S(1)}) custom-call(bf16[512,2048]{1,0:T(8,128)(2,1)S(1)} %get-tuple-element.51.raw_ref, bf16[8,4096]{1,0:T(8,128)(2,1)S(1)} %collective-permute-done.rim_ref, bf16[4,2048]{1,0:T(4,128)(2,1)S(1)} %get-tuple-element.52.tap_ref, ...), custom_call_target="tpu_custom_call" | custom-call | flops 536870912 | bytes 12582912 | tf_op jit(solution)/shard_map/state/pallas_call | solution.py:226
  15.9 0.7 %join.1 = (bf16[264,256]{1,0:T(8,128)(2,1)S(1)}, bf16[264,256]{1,0:T(8,128)(2,1)S(1)}, bf16[264,256]{1,0:T(8,128)(2,1)S(1)}, bf16[264,256]{1,0:T(8,128)(2,1)S(1)...) custom-call(bf16[8,264,256]{2,1,0:T(8,128)(2,1)S(1)} %get-tuple-elem, ...), custom_call_target="tpu_custom_call" | custom-call | bytes 4194304 | tf_op jit(solution)/shard_map/join/pallas_call | solution.py:226
  16.6 1.5 %collective-permute-start.2 = (bf16[264,256]{1,0:T(8,128)(2,1)S(1)}, bf16[264,256]{1,0:T(8,128)(2,1)S(1)}, u32[]{:S(2)}, u32[]{:S(2)}) collective-permute-start(bf16[264,256]{1,0:T(8,128)(2,1)S(1)} %get-tuple-element.65), channel_id=1, source_target_pairs={{0,2},{1,3},{2,0},{3,1},{4,6},{5,7},{6,4},{7,5},{8,10},{9,11},{10,... | collective-permute-start | bytes 405512 | tf_op jit(solution)/shard_map/ppermute | solution.py:727
  18.1 1.5 %collective-permute-start.3 = (bf16[264,256]{1,0:T(8,128)(2,1)S(1)}, bf16[264,256]{1,0:T(8,128)(2,1)S(1)}, u32[]{:S(2)}, u32[]{:S(2)}) collective-permute-start(bf16[264,256]{1,0:T(8,128)(2,1)S(1)} %get-tuple-element.66), channel_id=1, source_target_pairs={{0,4},{1,5},{2,6},{3,7},{4,0},{5,1},{6,2},{7,3},{8,12},{9,13},{10,... | collective-permute-start | bytes 405512 | tf_op jit(solution)/shard_map/ppermute | solution.py:727
  19.6 0.5 collective-permute-start.4
  20.1 1.6 %collective-permute-start.5 = (bf16[264,256]{1,0:T(8,128)(2,1)S(1)}, bf16[264,256]{1,0:T(8,128)(2,1)S(1)}, u32[]{:S(2)}, u32[]{:S(2)}) collective-permute-start(bf16[264,256]{1,0:T(8,128)(2,1)S(1)} %get-tuple-element.68), channel_id=1, source_target_pairs={{0,8},{1,9},{2,10},{3,11},{4,12},{5,13},{6,14},{7,15},{8,0},{9,1},... | collective-permute-start | bytes 405512 | tf_op jit(solution)/shard_map/ppermute | solution.py:727
  21.7 1.3 %collective-permute-start.6 = (bf16[264,256]{1,0:T(8,128)(2,1)S(1)}, bf16[264,256]{1,0:T(8,128)(2,1)S(1)}, u32[]{:S(2)}, u32[]{:S(2)}) collective-permute-start(bf16[264,256]{1,0:T(8,128)(2,1)S(1)} %get-tuple-element.69), channel_id=1, source_target_pairs={{0,10},{1,11},{2,8},{3,9},{4,14},{5,15},{6,12},{7,13},{8,2},{9,3},... | collective-permute-start | bytes 405512 | tf_op jit(solution)/shard_map/ppermute | solution.py:727
  23.1 2.6 %collective-permute-start.7 = (bf16[264,256]{1,0:T(8,128)(2,1)S(1)}, bf16[264,256]{1,0:T(8,128)(2,1)S(1)}, u32[]{:S(2)}, u32[]{:S(2)}) collective-permute-start(bf16[264,256]{1,0:T(8,128)(2,1)S(1)} %get-tuple-element.70), channel_id=1, source_target_pairs={{0,12},{1,13},{2,14},{3,15},{4,8},{5,9},{6,10},{7,11},{8,4},{9,5},... | collective-permute-start | bytes 405512 | tf_op jit(solution)/shard_map/ppermute | solution.py:727
  25.6 1.5 %collective-permute-start.8 = (bf16[264,256]{1,0:T(8,128)(2,1)S(1)}, bf16[264,256]{1,0:T(8,128)(2,1)S(1)}, u32[]{:S(2)}, u32[]{:S(2)}) collective-permute-start(bf16[264,256]{1,0:T(8,128)(2,1)S(1)} %get-tuple-element.71), channel_id=1, source_target_pairs={{0,14},{1,15},{2,12},{3,13},{4,10},{5,11},{6,8},{7,9},{8,6},{9,7},... | collective-permute-start | bytes 405512 | tf_op jit(solution)/shard_map/ppermute | solution.py:727
  27.1 8.1 %near.3 = (bf16[512,1280]{1,0:T(8,128)(2,1)}, bf16[512,2560]{1,0:T(8,128)(2,1)}, f32[5,8,512]{2,1,0:T(8,128)S(1)}, bf16[8,264,256]{2,1,0:T(8,128)(2,1)}) custom-call(bf16[512,2048]{1,0:T(8,128)(2,1)} %raw_hbm.5, bf16[512,2048]{1,0:T(8,128)(2,1)} %key_hbm.9, bf16[8,4096]{1,0:T(8,128)(2,1)S(1)} %collective-permute-done.rim_ref, bf16[4,2048]{1,0:T(4,128)(2,1)} %tap_hbm.7, ...), custom_call_target="tpu_custom_call" | custom-call | flops 2013265920 | bytes 26214400 | tf_op jit(solution)/shard_map/near/pallas_call | solution.py:226
  35.4 0.4 total.1
  35.8 4.5 %collective-permute-start.9 = (bf16[264,256]{1,0:T(8,128)(2,1)S(1)}, bf16[264,256]{1,0:T(8,128)(2,1)S(1)}, u32[]{:S(2)}, u32[]{:S(2)}) collective-permute-start(bf16[264,256]{1,0:T(8,128)(2,1)S(1)} %get-tuple-element.72), channel_id=1, source_target_pairs={{0,16},{1,17},{2,18},{3,19},{4,20},{5,21},{6,22},{7,23},{8,24},{9,... | collective-permute-start | bytes 405512 | tf_op jit(solution)/shard_map/ppermute | solution.py:746
  40.3 3.4 %near.4 = (bf16[512,256]{1,0:T(8,128)(2,1)}, bf16[512,512]{1,0:T(8,128)(2,1)}, f32[1,8,512]{2,1,0:T(8,128)S(1)}) custom-call(bf16[512,2048]{1,0:T(8,128)(2,1)} %raw_hbm.5, bf16[512,2048]{1,0:T(8,128)(2,1)} %key_hbm.9, bf16[8,4096]{1,0:T(8,128)(2,1)S(1)} %collective-permute-done.rim_ref, bf16[4,2048]{1,0:T(4,128)(2,1)} %tap_hbm.7, ...), custom_call_target="tpu_custom_call" | custom-call | flops 402653184 | bytes 5242880 | tf_op jit(solution)/shard_map/near/pallas_call | solution.py:226
  43.7 0.5 prefix.1
  44.1 0.6 collective-permute-start.10
  44.7 1.4 %collective-permute-start.11 = (bf16[264,256]{1,0:T(8,128)(2,1)S(1)}, bf16[264,256]{1,0:T(8,128)(2,1)S(1)}, u32[]{:S(2)}, u32[]{:S(2)}) collective-permute-start(bf16[264,256]{1,0:T(8,128)(2,1)S(1)} %get-tuple-element.87), channel_id=1, source_target_pairs={{0,4},{1,5},{2,6},{3,7},{4,0},{5,1},{6,2},{7,3},{8,12},{9,13},{10,... | collective-permute-start | bytes 405512 | tf_op jit(solution)/shard_map/ppermute | solution.py:727
  46.1 1.6 %collective-permute-start.12 = (bf16[264,256]{1,0:T(8,128)(2,1)S(1)}, bf16[264,256]{1,0:T(8,128)(2,1)S(1)}, u32[]{:S(2)}, u32[]{:S(2)}) collective-permute-start(bf16[264,256]{1,0:T(8,128)(2,1)S(1)} %get-tuple-element.88), channel_id=1, source_target_pairs={{0,6},{1,7},{2,4},{3,5},{4,2},{5,3},{6,0},{7,1},{8,14},{9,15},{10,... | collective-permute-start | bytes 405512 | tf_op jit(solution)/shard_map/ppermute | solution.py:727
  47.7 1.5 %collective-permute-start.13 = (bf16[264,256]{1,0:T(8,128)(2,1)S(1)}, bf16[264,256]{1,0:T(8,128)(2,1)S(1)}, u32[]{:S(2)}, u32[]{:S(2)}) collective-permute-start(bf16[264,256]{1,0:T(8,128)(2,1)S(1)} %get-tuple-element.89), channel_id=1, source_target_pairs={{0,8},{1,9},{2,10},{3,11},{4,12},{5,13},{6,14},{7,15},{8,0},{9,1},... | collective-permute-start | bytes 405512 | tf_op jit(solution)/shard_map/ppermute | solution.py:727
  49.2 0.5 collective-permute-start.14
  49.7 3.6 %collective-permute-done.10.refs_1_ = bf16[264,256]{1,0:T(8,128)(2,1)S(1)} collective-permute-done((bf16[264,256]{1,0:T(8,128)(2,1)S(1)}, bf16[264,256]{1,0:T(8,128)(2,1)S(1)}, u32[]{:S(2)}, u32[]{:S(2)}) %collective-permute-start.10) | collective-permute-done | bytes 135200 | tf_op jit(solution)/shard_map/ppermute | solution.py:727
  53.3 2.9 %collective-permute-start.16 = (bf16[264,256]{1,0:T(8,128)(2,1)S(1)}, bf16[264,256]{1,0:T(8,128)(2,1)S(1)}, u32[]{:S(2)}, u32[]{:S(2)}) collective-permute-start(bf16[264,256]{1,0:T(8,128)(2,1)S(1)} %get-tuple-element.92), channel_id=1, source_target_pairs={{0,14},{1,15},{2,12},{3,13},{4,10},{5,11},{6,8},{7,9},{8,6},{9,7},... | collective-permute-start | bytes 405512 | tf_op jit(solution)/shard_map/ppermute | solution.py:727
  56.2 5.1 %near.5 = (bf16[512,512]{1,0:T(8,128)(2,1)}, bf16[512,1024]{1,0:T(8,128)(2,1)}, f32[2,8,512]{2,1,0:T(8,128)S(1)}) custom-call(bf16[512,2048]{1,0:T(8,128)(2,1)} %raw_hbm.5, bf16[512,2048]{1,0:T(8,128)(2,1)} %key_hbm.9, bf16[8,4096]{1,0:T(8,128)(2,1)S(1)} %collective-permute-done.rim_ref, bf16[4,2048]{1,0:T(4,128)(2,1)} %tap_hbm.7, ...), custom_call_target="tpu_custom_call" | custom-call | flops 805306368 | bytes 10485760 | tf_op jit(solution)/shard_map/near/pallas_call | solution.py:226
  61.3 0.9 %split.1 = (bf16[8,264,256]{2,1,0:T(8,128)(2,1)S(1)}, bf16[8,264,256]{2,1,0:T(8,128)(2,1)S(1)}) custom-call(bf16[8,264,256]{2,1,0:T(8,128)(2,1)S(1)} %copy-done.2, bf16[264,256]{1,0:T(8,128)(2,1)S(1)} %get-tuple-element.85.refs_0_, bf16[264,256]{1,0:T(8,128)(2,1)S(1)} %collective-permute-done.10.refs_1_, ...), custom_call_target="tpu_custom_call" | custom-call | bytes 4194304 | tf_op jit(solution)/shard_map/split/pallas_call | solution.py:226
  62.4 0.2 copy-done.1
  62.6 2.4 %far.2.refs_10_ = bf16[512,4096]{1,0:T(8,128)(2,1)} custom-call(bf16[512,1280]{1,0:T(8,128)(2,1)S(1)} %copy-done.1, bf16[512,2560]{1,0:T(8,128)(2,1)S(1)} %copy-done, f32[5,8,512]{2,1,0:T(8,128)S(1)} %get-tuple-element.63.refs_2_, bf16[8,264,256]{2,1,0:T(8,128)(2,1)S(1)} %get-tuple-element.94.refs_3_), custom_call_target="tpu_custom_call" | custom-call | flops 536870912 | bytes 20971520 | tf_op jit(solution)/shard_map/far/pallas_call | solution.py:699
  65.1 2.4 %far.3 = bf16[512,4096]{1,0:T(8,128)(2,1)} custom-call(bf16[512,1280]{1,0:T(8,128)(2,1)S(1)} %copy-done.1, bf16[512,2560]{1,0:T(8,128)(2,1)S(1)} %copy-done, f32[5,8,512]{2,1,0:T(8,128)S(1)} %get-tuple-element.63.refs_2_, bf16[512,256]{1,0:T(8,128)(2,1)S(1)} %copy-done.6, bf16[512,512]{1,0:T(8,128)(2,1)S(1)} %copy-done.4, ...), custom_call_target="tpu_custom_call", output_to_operand_aliasing={{}: (10, {})} | custom-call | flops 536870912 | bytes 20971520 | tf_op jit(solution)/shard_map/far/pallas_call | solution.py:699
  (32 shorter events, 0.3 us)
Async XLA Ops:
  0.8 8.2 %collective-permute-start = (bf16[8,4096]{1,0:T(8,128)(2,1)S(1)}, bf16[8,4096]{1,0:T(8,128)(2,1)S(1)}, u32[]{:S(2)}, u32[]{:S(2)}) collective-permute-start(bf16[8,4096]{1,0:T(8,128)(2,1)S(1)} %tails.1), channel_id=1, source_target_pairs={{0,1},{1,2},{2,3},{3,4},{4,5},{5,6},{6,7},{7,8},{8,9},{9,10},{10,1... | collective-permute-start | bytes 196616 | tf_op jit(solution)/shard_map/ppermute | solution.py:730
  9.8 6.1 %collective-permute-start.1 = (bf16[8,264,256]{2,1,0:T(8,128)(2,1)S(1)}, bf16[8,264,256]{2,1,0:T(8,128)(2,1)S(1)}, u32[]{:S(2)}, u32[]{:S(2)}) collective-permute-start(bf16[8,264,256]{2,1,0:T(8,128)(2,1)S(1)} %early_state.1), channel_id=1, source_target_pairs={{0,1},{1,0},{2,3},{3,2},{4,5},{5,4},{6,7},{7,6},{8,9},{9,8},{10,11... | collective-permute-start | bytes 3244040 | tf_op jit(solution)/shard_map/ppermute | solution.py:737
  16.6 6.5 %collective-permute-start.2 = (bf16[264,256]{1,0:T(8,128)(2,1)S(1)}, bf16[264,256]{1,0:T(8,128)(2,1)S(1)}, u32[]{:S(2)}, u32[]{:S(2)}) collective-permute-start(bf16[264,256]{1,0:T(8,128)(2,1)S(1)} %get-tuple-element.65), channel_id=1, source_target_pairs={{0,2},{1,3},{2,0},{3,1},{4,6},{5,7},{6,4},{7,5},{8,10},{9,11},{10,... | collective-permute-start | bytes 405512 | tf_op jit(solution)/shard_map/ppermute | solution.py:727
  18.1 7.5 %collective-permute-start.3 = (bf16[264,256]{1,0:T(8,128)(2,1)S(1)}, bf16[264,256]{1,0:T(8,128)(2,1)S(1)}, u32[]{:S(2)}, u32[]{:S(2)}) collective-permute-start(bf16[264,256]{1,0:T(8,128)(2,1)S(1)} %get-tuple-element.66), channel_id=1, source_target_pairs={{0,4},{1,5},{2,6},{3,7},{4,0},{5,1},{6,2},{7,3},{8,12},{9,13},{10,... | collective-permute-start | bytes 405512 | tf_op jit(solution)/shard_map/ppermute | solution.py:727
  19.6 15.6 %collective-permute-start.4 = (bf16[264,256]{1,0:T(8,128)(2,1)S(1)}, bf16[264,256]{1,0:T(8,128)(2,1)S(1)}, u32[]{:S(2)}, u32[]{:S(2)}) collective-permute-start(bf16[264,256]{1,0:T(8,128)(2,1)S(1)} %get-tuple-element.67), channel_id=1, source_target_pairs={{0,6},{1,7},{2,4},{3,5},{4,2},{5,3},{6,0},{7,1},{8,14},{9,15},{10,... | collective-permute-start | bytes 405512 | tf_op jit(solution)/shard_map/ppermute | solution.py:727
  20.1 15.1 %collective-permute-start.5 = (bf16[264,256]{1,0:T(8,128)(2,1)S(1)}, bf16[264,256]{1,0:T(8,128)(2,1)S(1)}, u32[]{:S(2)}, u32[]{:S(2)}) collective-permute-start(bf16[264,256]{1,0:T(8,128)(2,1)S(1)} %get-tuple-element.68), channel_id=1, source_target_pairs={{0,8},{1,9},{2,10},{3,11},{4,12},{5,13},{6,14},{7,15},{8,0},{9,1},... | collective-permute-start | bytes 405512 | tf_op jit(solution)/shard_map/ppermute | solution.py:727
  21.7 13.5 %collective-permute-start.6 = (bf16[264,256]{1,0:T(8,128)(2,1)S(1)}, bf16[264,256]{1,0:T(8,128)(2,1)S(1)}, u32[]{:S(2)}, u32[]{:S(2)}) collective-permute-start(bf16[264,256]{1,0:T(8,128)(2,1)S(1)} %get-tuple-element.69), channel_id=1, source_target_pairs={{0,10},{1,11},{2,8},{3,9},{4,14},{5,15},{6,12},{7,13},{8,2},{9,3},... | collective-permute-start | bytes 405512 | tf_op jit(solution)/shard_map/ppermute | solution.py:727
  23.1 12.2 %collective-permute-start.7 = (bf16[264,256]{1,0:T(8,128)(2,1)S(1)}, bf16[264,256]{1,0:T(8,128)(2,1)S(1)}, u32[]{:S(2)}, u32[]{:S(2)}) collective-permute-start(bf16[264,256]{1,0:T(8,128)(2,1)S(1)} %get-tuple-element.70), channel_id=1, source_target_pairs={{0,12},{1,13},{2,14},{3,15},{4,8},{5,9},{6,10},{7,11},{8,4},{9,5},... | collective-permute-start | bytes 405512 | tf_op jit(solution)/shard_map/ppermute | solution.py:727
  25.6 9.8 %collective-permute-start.8 = (bf16[264,256]{1,0:T(8,128)(2,1)S(1)}, bf16[264,256]{1,0:T(8,128)(2,1)S(1)}, u32[]{:S(2)}, u32[]{:S(2)}) collective-permute-start(bf16[264,256]{1,0:T(8,128)(2,1)S(1)} %get-tuple-element.71), channel_id=1, source_target_pairs={{0,14},{1,15},{2,12},{3,13},{4,10},{5,11},{6,8},{7,9},{8,6},{9,7},... | collective-permute-start | bytes 405512 | tf_op jit(solution)/shard_map/ppermute | solution.py:727
  35.8 7.9 %collective-permute-start.9 = (bf16[264,256]{1,0:T(8,128)(2,1)S(1)}, bf16[264,256]{1,0:T(8,128)(2,1)S(1)}, u32[]{:S(2)}, u32[]{:S(2)}) collective-permute-start(bf16[264,256]{1,0:T(8,128)(2,1)S(1)} %get-tuple-element.72), channel_id=1, source_target_pairs={{0,16},{1,17},{2,18},{3,19},{4,20},{5,21},{6,22},{7,23},{8,24},{9,... | collective-permute-start | bytes 405512 | tf_op jit(solution)/shard_map/ppermute | solution.py:746
  44.1 9.1 %collective-permute-start.10 = (bf16[264,256]{1,0:T(8,128)(2,1)S(1)}, bf16[264,256]{1,0:T(8,128)(2,1)S(1)}, u32[]{:S(2)}, u32[]{:S(2)}) collective-permute-start(bf16[264,256]{1,0:T(8,128)(2,1)S(1)} %get-tuple-element.86), channel_id=1, source_target_pairs={{0,2},{1,3},{2,0},{3,1},{4,6},{5,7},{6,4},{7,5},{8,10},{9,11},{10,... | collective-permute-start | bytes 405512 | tf_op jit(solution)/shard_map/ppermute | solution.py:727
  44.7 8.5 %collective-permute-start.11 = (bf16[264,256]{1,0:T(8,128)(2,1)S(1)}, bf16[264,256]{1,0:T(8,128)(2,1)S(1)}, u32[]{:S(2)}, u32[]{:S(2)}) collective-permute-start(bf16[264,256]{1,0:T(8,128)(2,1)S(1)} %get-tuple-element.87), channel_id=1, source_target_pairs={{0,4},{1,5},{2,6},{3,7},{4,0},{5,1},{6,2},{7,3},{8,12},{9,13},{10,... | collective-permute-start | bytes 405512 | tf_op jit(solution)/shard_map/ppermute | solution.py:727
  46.1 15.2 %collective-permute-start.12 = (bf16[264,256]{1,0:T(8,128)(2,1)S(1)}, bf16[264,256]{1,0:T(8,128)(2,1)S(1)}, u32[]{:S(2)}, u32[]{:S(2)}) collective-permute-start(bf16[264,256]{1,0:T(8,128)(2,1)S(1)} %get-tuple-element.88), channel_id=1, source_target_pairs={{0,6},{1,7},{2,4},{3,5},{4,2},{5,3},{6,0},{7,1},{8,14},{9,15},{10,... | collective-permute-start | bytes 405512 | tf_op jit(solution)/shard_map/ppermute | solution.py:727
  47.7 13.6 %collective-permute-start.13 = (bf16[264,256]{1,0:T(8,128)(2,1)S(1)}, bf16[264,256]{1,0:T(8,128)(2,1)S(1)}, u32[]{:S(2)}, u32[]{:S(2)}) collective-permute-start(bf16[264,256]{1,0:T(8,128)(2,1)S(1)} %get-tuple-element.89), channel_id=1, source_target_pairs={{0,8},{1,9},{2,10},{3,11},{4,12},{5,13},{6,14},{7,15},{8,0},{9,1},... | collective-permute-start | bytes 405512 | tf_op jit(solution)/shard_map/ppermute | solution.py:727
  49.2 12.1 %collective-permute-start.14 = (bf16[264,256]{1,0:T(8,128)(2,1)S(1)}, bf16[264,256]{1,0:T(8,128)(2,1)S(1)}, u32[]{:S(2)}, u32[]{:S(2)}) collective-permute-start(bf16[264,256]{1,0:T(8,128)(2,1)S(1)} %get-tuple-element.90), channel_id=1, source_target_pairs={{0,10},{1,11},{2,8},{3,9},{4,14},{5,15},{6,12},{7,13},{8,2},{9,3},... | collective-permute-start | bytes 405512 | tf_op jit(solution)/shard_map/ppermute | solution.py:727
  53.2 8.1 %collective-permute-start.15 = (bf16[264,256]{1,0:T(8,128)(2,1)S(1)}, bf16[264,256]{1,0:T(8,128)(2,1)S(1)}, u32[]{:S(2)}, u32[]{:S(2)}) collective-permute-start(bf16[264,256]{1,0:T(8,128)(2,1)S(1)} %get-tuple-element.91), channel_id=1, source_target_pairs={{0,12},{1,13},{2,14},{3,15},{4,8},{5,9},{6,10},{7,11},{8,4},{9,5},... | collective-permute-start | bytes 405512 | tf_op jit(solution)/shard_map/ppermute | solution.py:727
  53.3 8.1 %collective-permute-start.16 = (bf16[264,256]{1,0:T(8,128)(2,1)S(1)}, bf16[264,256]{1,0:T(8,128)(2,1)S(1)}, u32[]{:S(2)}, u32[]{:S(2)}) collective-permute-start(bf16[264,256]{1,0:T(8,128)(2,1)S(1)} %get-tuple-element.92), channel_id=1, source_target_pairs={{0,14},{1,15},{2,12},{3,13},{4,10},{5,11},{6,8},{7,9},{8,6},{9,7},... | collective-permute-start | bytes 405512 | tf_op jit(solution)/shard_map/ppermute | solution.py:727
  56.2 5.2 %copy-start.2 = (bf16[8,264,256]{2,1,0:T(8,128)(2,1)S(1)}, bf16[8,264,256]{2,1,0:T(8,128)(2,1)}, u32[]{:S(2)}) copy-start(bf16[8,264,256]{2,1,0:T(8,128)(2,1)} %get-tuple-element.84.first_ref) | copy-start | bytes 3244036
  56.2 6.2 %copy-start = (bf16[512,2560]{1,0:T(8,128)(2,1)S(1)}, bf16[512,2560]{1,0:T(8,128)(2,1)}, u32[]{:S(2)}) copy-start(bf16[512,2560]{1,0:T(8,128)(2,1)} %get-tuple-element.62.refs_1_) | copy-start | bytes 7864324
  61.3 1.3 %copy-start.1 = (bf16[512,1280]{1,0:T(8,128)(2,1)S(1)}, bf16[512,1280]{1,0:T(8,128)(2,1)}, u32[]{:S(2)}) copy-start(bf16[512,1280]{1,0:T(8,128)(2,1)} %get-tuple-element.61.refs_0_) | copy-start | bytes 3932164
  62.3 2.8 %collective-permute-start.17 = (bf16[8,264,256]{2,1,0:T(8,128)(2,1)S(1)}, bf16[8,264,256]{2,1,0:T(8,128)(2,1)S(1)}, u32[]{:S(2)}, u32[]{:S(2)}) collective-permute-start(bf16[8,264,256]{2,1,0:T(8,128)(2,1)S(1)} %get-tuple-element.93), channel_id=1, source_target_pairs={{0,1},{1,0},{2,3},{3,2},{4,5},{5,4},{6,7},{7,6},{8,9},{9,8},{10,11... | collective-permute-start | bytes 3244040 | tf_op jit(solution)/shard_map/ppermute | solution.py:759
  62.6 2.5 %copy-start.3 = (bf16[512,1024]{1,0:T(8,128)(2,1)S(1)}, bf16[512,1024]{1,0:T(8,128)(2,1)}, u32[]{:S(2)}) copy-start(bf16[512,1024]{1,0:T(8,128)(2,1)} %get-tuple-element.82.refs_7_) | copy-start | bytes 3145732
  62.6 2.5 %copy-start.4 = (bf16[512,512]{1,0:T(8,128)(2,1)S(1)}, bf16[512,512]{1,0:T(8,128)(2,1)}, u32[]{:S(2)}) copy-start(bf16[512,512]{1,0:T(8,128)(2,1)} %get-tuple-element.75.refs_4_) | copy-start | bytes 1572868
  62.6 2.5 %copy-start.5 = (bf16[512,512]{1,0:T(8,128)(2,1)S(1)}, bf16[512,512]{1,0:T(8,128)(2,1)}, u32[]{:S(2)}) copy-start(bf16[512,512]{1,0:T(8,128)(2,1)} %get-tuple-element.81.refs_6_) | copy-start | bytes 1572868
  62.6 2.5 %copy-start.6 = (bf16[512,256]{1,0:T(8,128)(2,1)S(1)}, bf16[512,256]{1,0:T(8,128)(2,1)}, u32[]{:S(2)}) copy-start(bf16[512,256]{1,0:T(8,128)(2,1)} %get-tuple-element.74.refs_3_) | copy-start | bytes 786436

commit v3 on v2

--- a/solution.py
+++ b/solution.py
@@ -105,23 +105,6 @@
 VMEM_SPEC = pl.BlockSpec(memory_space=pltpu.VMEM)
 
 
-def on_chip(kernel, operands, shapes, scratch=(), name=None, flops=0, size=1 << 20):
-    many = isinstance(shapes, list)
-    kept = [pltpu.with_memory_space_constraint(x, pltpu.VMEM) for x in operands]
-    out = [pltpu.VMEM(shape, dtype) for shape, dtype in (shapes if many else [shapes])]
-    results = pl.pallas_call(
-        kernel,
-        in_specs=[VMEM_SPEC] * len(kept),
-        out_specs=[VMEM_SPEC] * len(out),
-        out_shape=out,
-        scratch_shapes=list(scratch),
-        name=name,
-        cost_estimate=pl.CostEstimate(flops=flops, transcendentals=0, bytes_accessed=size),
-        compiler_params=pltpu.CompilerParams(vmem_limit_bytes=8 << 20),
-    )(*kept)
-    return results if many else results[0]
-
-
 def tails_kernel(key_hbm, query_hbm, out_ref, sems):
     width = key_hbm.shape[1]
     last = pl.ds(BLK - RIM, RIM)
@@ -213,7 +196,6 @@
     return rows_ref[pl.ds(kind * HEADS + head, 1), :]
 
 
-PADDED = pltpu.VMEM((BLK + 8, DK), F32)
 HBM_SPEC = pl.BlockSpec(memory_space=pltpu.HBM)
 LIMIT = 20 << 20
 
@@ -238,16 +220,18 @@
     )(*operands)
 
 
-def conv_rows(columns, rim_columns, raw, rim_ref, tap_ref, padded):
-    padded[0:8] = rim_ref[:, rim_columns].astype(F32)
-    padded[8 : 8 + BLK] = raw.astype(F32)
-    taps = tap_ref[:, columns].astype(F32)
+def conv_rows(columns, rim_columns, raw, rim_ref, tap_ref):
+    taps = 0.5 * tap_ref[:, columns].astype(F32)
+    earlier = rim_ref[:, rim_columns].astype(F32)
     for start in range(0, BLK, STEP):
-        first = 8 - (TAPS - 1) + start
-        mixed = taps[0:1] * padded[first : first + STEP]
+        here = raw[start : start + STEP].astype(F32)
+        wide = jnp.concatenate([earlier, here], axis=0)
+        first = 8 - (TAPS - 1)
+        mixed = taps[0:1] * wide[first : first + STEP]
         for tap in range(1, TAPS):
-            mixed = mixed + taps[tap : tap + 1] * padded[first + tap : first + tap + STEP]
-        yield start, (mixed * (0.5 * jnp.tanh(0.5 * mixed) + 0.5)).astype(BF16)
+            mixed = mixed + taps[tap : tap + 1] * wide[first + tap : first + tap + STEP]
+        earlier = here[STEP - 8 :]
+        yield start, (mixed * (jnp.tanh(mixed) + 1.0)).astype(BF16)
 
 
 def start_all(copies):
@@ -268,13 +252,13 @@
     return lax.dot_general(weighted, values, (((0,), (0,)), ((), ())), preferred_element_type=F32)
 
 
-def state_kernel(raw_ref, rim_ref, tap_ref, val_ref, rows_ref, rec_ref, act_ref, padded, weighted):
+def state_kernel(raw_ref, rim_ref, tap_ref, val_ref, rows_ref, rec_ref, act_ref, weighted):
     for local in range(LOCAL):
         head = first_head(True, 0) + local
         weight = column(row_of(rows_ref, 2, head))
         norm = jnp.zeros((1, DK), F32)
         columns = span(head, DK)
-        for start, act in conv_rows(columns, columns, raw_ref[:, columns], rim_ref, tap_ref, padded.at[local % 2]):
+        for start, act in conv_rows(columns, columns, raw_ref[:, columns], rim_ref, tap_ref):
             act_ref[start : start + STEP, local * DK : (local + 1) * DK] = act
             scaled = act.astype(F32) * widen(weight[start : start + STEP], DK)
             norm = norm + jnp.sum(scaled, axis=0, keepdims=True)
@@ -290,14 +274,14 @@
         state_kernel,
         [("vmem", raw), ("vmem", rim), ("vmem", taps), ("vmem", values), ("vmem", rows)],
         [("vmem", (OWNERS, ROWS, WIDTH), BF16), ("vmem", (BLK, LOCAL * DK), BF16)],
-        [pltpu.VMEM((2, BLK + 8, DK), F32), pltpu.VMEM((2, BLK, DK), BF16)],
+        [pltpu.VMEM((2, BLK, DK), BF16)],
         "state",
         LOCAL * 2 * BLK * DK * DV,
         LOCAL * 3 << 20,
     )
 
 
-def late_state_kernel(raw_ref, tap_ref, val_ref, rows_ref, memory_ref, norm_ref, no_rim, padded, weighted):
+def late_state_kernel(raw_ref, tap_ref, val_ref, rows_ref, memory_ref, norm_ref, no_rim, weighted):
     no_rim[...] = jnp.zeros((RIM, HEADS * DK), BF16)
     lanes = lax.broadcasted_iota(jnp.int32, (1, BLK), 1)
     for local in range(LOCAL):
@@ -305,7 +289,7 @@
         weight = column(jnp.where(lanes >= EARLY, row_of(rows_ref, 2, head), 0.0))
         norm = jnp.zeros((1, DK), F32)
         columns = span(head, DK)
-        for start, act in conv_rows(columns, columns, raw_ref[:, columns], no_rim, tap_ref, padded.at[local % 2]):
+        for start, act in conv_rows(columns, columns, raw_ref[:, columns], no_rim, tap_ref):
             scaled = act.astype(F32) * widen(weight[start : start + STEP], DK)
             norm = norm + jnp.sum(scaled, axis=0, keepdims=True)
             weighted[local % 2, start : start + STEP] = scaled.astype(BF16)
@@ -320,7 +304,6 @@
         [("vmem", (LOCAL, DK, DV), F32), ("vmem", (LOCAL, 8, DK), F32)],
         [
             pltpu.VMEM((RIM, HEADS * DK), BF16),
-            pltpu.VMEM((2, BLK + 8, DK), F32),
             pltpu.VMEM((2, BLK, DK), BF16),
         ],
         "late_state",
@@ -336,12 +319,12 @@
         weight = column(row_of(rows_ref, 2, head)[:, 0:128])[0:EARLY]
         padded[local, 0:8] = rim_ref[:, columns].astype(F32)
         padded[local, 8 : 8 + EARLY] = raw_ref[0:EARLY, columns].astype(F32)
-        taps = tap_ref[:, columns].astype(F32)
+        taps = 0.5 * tap_ref[:, columns].astype(F32)
         first = 8 - (TAPS - 1)
         mixed = taps[0:1] * padded[local, first : first + EARLY]
         for tap in range(1, TAPS):
             mixed = mixed + taps[tap : tap + 1] * padded[local, first + tap : first + tap + EARLY]
-        act = (mixed * (0.5 * jnp.tanh(0.5 * mixed) + 0.5)).astype(BF16)
+        act = (mixed * (jnp.tanh(mixed) + 1.0)).astype(BF16)
         scaled = act.astype(F32) * widen(weight, DK)
         norm = norm_ref[local, 0:1] + jnp.sum(scaled, axis=0, keepdims=True)
         memory = memory_ref[local] + outer(scaled.astype(BF16), val_ref[0:EARLY, span(head, DV)])
@@ -453,7 +436,7 @@
         refs = refs[3:6] + refs[7:]
     (
         query_hbm, num_hbm, stat_ref,
-        raw_buf, raw_key_buf, key_buf, val_buf, query_buf, num_buf, tap_buf, padded, sems,
+        raw_buf, raw_key_buf, key_buf, val_buf, query_buf, num_buf, tap_buf, sems,
     ) = refs
     places = [first_head(mine, 0) + local for mine, local in heads]
     taps_in = start_all(
@@ -498,14 +481,14 @@
         head = places[local]
         coming[local][0].wait()
         columns, rim_columns = span(head, DK), span(HEADS + head, DK)
-        for start, act in conv_rows(columns, rim_columns, raw_buf[local], rim_ref, tap_buf.at[0], padded.at[0]):
+        for start, act in conv_rows(columns, rim_columns, raw_buf[local], rim_ref, tap_buf.at[0]):
             query_buf[local, start : start + STEP] = act
         going[local][0].start()
         if park and heads[local][0]:
             key_act = act_ref.at[:, (local * DK) : (local + 1) * DK]
         else:
             coming[local][1].wait()
-            for start, act in conv_rows(columns, columns, raw_key_buf[local], rim_ref, tap_buf.at[1], padded.at[1]):
+            for start, act in conv_rows(columns, columns, raw_key_buf[local], rim_ref, tap_buf.at[1]):
                 key_buf[local, start : start + STEP] = act
             key_act = key_buf.at[local]
         coming[local][-1].wait()
@@ -566,7 +549,6 @@
             pltpu.VMEM((count, BLK, DK), BF16),
             pltpu.VMEM((count, BLK, DV), NUM),
             pltpu.VMEM((2, TAPS, HEADS * DK), BF16),
-            pltpu.VMEM((2, BLK + 8, DK), F32),
             pltpu.SemaphoreType.DMA((5 * count + 3,)),
         ],
         "near",
@@ -670,12 +652,12 @@
         near_column = column(near_part * scale)
         far_column = column(far_part * scale)
         memory = jnp.concatenate([enter_ref[at + piece, 0:DK] for piece in range(PIECES)], axis=1)
-        for t in range(0, BLK, STEP):
-            far = jnp.dot(query[t : t + STEP], memory, preferred_element_type=F32)
-            near_weight = widen(near_column[t : t + STEP], DV)
-            far_weight = widen(far_column[t : t + STEP], DV)
-            near_rows = num_ref[t : t + STEP, wide].astype(F32)
-            ready[local, t : t + STEP] = (near_weight * near_rows + far_weight * far).astype(BF16)
+        for t in range(0, BLK, TILE):
+            far = jnp.dot(query[t : t + TILE], memory, preferred_element_type=F32)
+            near_weight = widen(near_column[t : t + TILE], DV)
+            far_weight = widen(far_column[t : t + TILE], DV)
+            near_rows = num_ref[t : t + TILE, wide].astype(F32)
+            ready[local, t : t + TILE] = (near_weight * near_rows + far_weight * far).astype(BF16)
         head = first_head(mine, 0) + local
         copies.append(pltpu.make_async_copy(ready.at[local], out_ref.at[:, span(head, DV)], sems.at[local]))
         copies[-1].start()

time: 68.1 us -> 67.2 us (0.987)
  Pallas kernels: 34.7 us -> 33.2 us
    pallas_call x12, Pallas kernels: 29.9 us -> 28.6 us  [kernel_call(): pl.pallas_call(kernel, in_specs=in_specs, out_specs=[VMEM_SPEC if where =...]
  transfers between devices with their start and end apart: 18 -> 18, of which waited for: 2 -> 3; matrix products, arithmetic and copies ran while one was open for 0% -> 0% of each run, Pallas kernels for 42% -> 40%
where the time goes in v3:
time: 67.2 us; the launch traced here: 66.7 us
  Pallas kernels  33.2 us (49%)
  starting transfers between devices  28.7 us (43%)
  waiting for transfers between devices  4.24 us (6%)
    pallas_call x12, Pallas kernels, kernel_call(): pl.pallas_call(kernel, in_specs=in_specs, out_specs=[VMEM_SPEC if where =...  28.6 us
    ppermute x14, starting transfers between devices, spread(): moved[mask] = lax.ppermute(records[mask], AXES, route)  19.1 us
    pallas_call x2, Pallas kernels, far_call(): pl.pallas_call(functools.partial(far_kernel, mine, slots, len(near)), in_...  4.62 us
    ppermute x1, starting transfers between devices, on_device(): entering = lax.ppermute(total, AXES, up(1))  4.5 us
    ppermute x14, waiting for transfers between devices, spread(): moved[mask] = lax.ppermute(records[mask], AXES, route)  4.08 us
    ppermute x1, starting transfers between devices, on_device(): other = lax.ppermute(sent, AXES, swap)  2.7 us
    ppermute x1, starting transfers between devices, on_device(): rim = lax.ppermute(tails_call(key_raw, query_raw), AXES, line)  2.36 us
  transfers between devices with their start and end apart: 18, of which 3 were waited for; matrix products, arithmetic and copies ran while one was open for 0% of the time, Pallas kernels for 40%

profile of v3, /device:TPU:0, one launch (start us, length us, event | category | flops | bytes accessed | tf_op | source)
XLA Modules:
  0.0 66.7 jit_solution(13883905903285682209)
XLA Ops:
  0.0 0.8 %tails.1 = bf16[8,4096]{1,0:T(8,128)(2,1)S(1)} custom-call(bf16[512,2048]{1,0:T(8,128)(2,1)} %key_hbm.9, bf16[512,2048]{1,0:T(8,128)(2,1)} %raw_hbm.5), custom_call_target="tpu_custom_call" | custom-call | bytes 131072 | tf_op jit(solution)/shard_map/tails/pallas_call | solution.py:208
  0.8 2.4 %collective-permute-start = (bf16[8,4096]{1,0:T(8,128)(2,1)S(1)}, bf16[8,4096]{1,0:T(8,128)(2,1)S(1)}, u32[]{:S(2)}, u32[]{:S(2)}) collective-permute-start(bf16[8,4096]{1,0:T(8,128)(2,1)S(1)} %tails.1), channel_id=1, source_target_pairs={{0,1},{1,2},{2,3},{3,4},{4,5},{5,6},{6,7},{7,8},{8,9},{9,10},{10,1... | collective-permute-start | bytes 196616 | tf_op jit(solution)/shard_map/ppermute | solution.py:712
  3.2 2.9 %prepare.1 = (f32[40,512]{1,0:T(8,128)S(1)}, bf16[512,2048]{1,0:T(8,128)(2,1)S(1)}, bf16[4,2048]{1,0:T(4,128)(2,1)S(1)}, bf16[512,4096]{1,0:T(8,128)(2,1)S(1)}) custom-call(bf16[8,512]{1,0:T(8,128)(2,1)} %bitcast.2, bf16[8,512]{1,0:T(8,128)(2,1)} %bitcast.3, bf16[512,2048]{1,0:T(8,128)(2,1)} %key_hbm.9, bf16[4,2048]{1,0:T(4,128)(2,1)} %key_tap_hbm.5, ...), custom_call_target="tpu_custom_call" | custom-call | bytes 6291456 | tf_op jit(solution)/shard_map/prepare/pallas_call | solution.py:208
  6.1 2.8 %late_state.1 = (f32[4,256,512]{2,1,0:T(8,128)S(1)}, f32[4,8,256]{2,1,0:T(8,128)S(1)}) custom-call(bf16[512,2048]{1,0:T(8,128)(2,1)S(1)} %get-tuple-element.51.raw_ref, bf16[4,2048]{1,0:T(4,128)(2,1)S(1)} %get-tuple-element.52.tap_ref, bf16[512,4096]{1,0:T(8,128)(2,1)S(1)} %get-tuple-element.53.val_ref, f32[40,512]{1,0:T(8,128)S(1)} %get-tuple-element.80.rows_ref), custom_call_target="tpu_custom_call" | custom-call | flops 536870912 | bytes 12582912 | tf_op jit(solution)/shard_map/late_state/pallas_call | solution.py:208
  8.9 0.8 %early_state.1 = bf16[8,264,256]{2,1,0:T(8,128)(2,1)S(1)} custom-call(bf16[512,2048]{1,0:T(8,128)(2,1)S(1)} %get-tuple-element.51.raw_ref, bf16[8,4096]{1,0:T(8,128)(2,1)S(1)} %collective-permute-done.rim_ref, bf16[4,2048]{1,0:T(4,128)(2,1)S(1)} %get-tuple-element.52.tap_ref, bf16[512,4096]{1,0:T(8,128)(2,1)S(1)} %get-tuple-element.53.val_ref, ...), custom_call_target="tpu_custom_call" | custom-call | flops 1048576 | bytes 4194304 | tf_op jit(solution)/shard_map/early_state/pallas_call | solution.py:208
  9.7 2.7 %collective-permute-start.1 = (bf16[8,264,256]{2,1,0:T(8,128)(2,1)S(1)}, bf16[8,264,256]{2,1,0:T(8,128)(2,1)S(1)}, u32[]{:S(2)}, u32[]{:S(2)}) collective-permute-start(bf16[8,264,256]{2,1,0:T(8,128)(2,1)S(1)} %early_state.1), channel_id=1, source_target_pairs={{0,1},{1,0},{2,3},{3,2},{4,5},{5,4},{6,7},{7,6},{8,9},{9,8},{10,11... | collective-permute-start | bytes 3244040 | tf_op jit(solution)/shard_map/ppermute | solution.py:719
  12.4 3.2 %state.1 = (bf16[8,264,256]{2,1,0:T(8,128)(2,1)S(1)}, bf16[512,1024]{1,0:T(8,128)(2,1)S(1)}) custom-call(bf16[512,2048]{1,0:T(8,128)(2,1)S(1)} %get-tuple-element.51.raw_ref, bf16[8,4096]{1,0:T(8,128)(2,1)S(1)} %collective-permute-done.rim_ref, bf16[4,2048]{1,0:T(4,128)(2,1)S(1)} %get-tuple-element.52.tap_ref, ...), custom_call_target="tpu_custom_call" | custom-call | flops 536870912 | bytes 12582912 | tf_op jit(solution)/shard_map/state/pallas_call | solution.py:208
  15.5 0.7 %join.1 = (bf16[264,256]{1,0:T(8,128)(2,1)S(1)}, bf16[264,256]{1,0:T(8,128)(2,1)S(1)}, bf16[264,256]{1,0:T(8,128)(2,1)S(1)}, bf16[264,256]{1,0:T(8,128)(2,1)S(1)...) custom-call(bf16[8,264,256]{2,1,0:T(8,128)(2,1)S(1)} %get-tuple-elem, ...), custom_call_target="tpu_custom_call" | custom-call | bytes 4194304 | tf_op jit(solution)/shard_map/join/pallas_call | solution.py:208
  16.2 1.5 %collective-permute-start.2 = (bf16[264,256]{1,0:T(8,128)(2,1)S(1)}, bf16[264,256]{1,0:T(8,128)(2,1)S(1)}, u32[]{:S(2)}, u32[]{:S(2)}) collective-permute-start(bf16[264,256]{1,0:T(8,128)(2,1)S(1)} %get-tuple-element.65), channel_id=1, source_target_pairs={{0,2},{1,3},{2,0},{3,1},{4,6},{5,7},{6,4},{7,5},{8,10},{9,11},{10,... | collective-permute-start | bytes 405512 | tf_op jit(solution)/shard_map/ppermute | solution.py:709
  17.7 1.6 %collective-permute-start.3 = (bf16[264,256]{1,0:T(8,128)(2,1)S(1)}, bf16[264,256]{1,0:T(8,128)(2,1)S(1)}, u32[]{:S(2)}, u32[]{:S(2)}) collective-permute-start(bf16[264,256]{1,0:T(8,128)(2,1)S(1)} %get-tuple-element.66), channel_id=1, source_target_pairs={{0,4},{1,5},{2,6},{3,7},{4,0},{5,1},{6,2},{7,3},{8,12},{9,13},{10,... | collective-permute-start | bytes 405512 | tf_op jit(solution)/shard_map/ppermute | solution.py:709
  19.3 0.5 collective-permute-start.4
  19.8 1.6 %collective-permute-start.5 = (bf16[264,256]{1,0:T(8,128)(2,1)S(1)}, bf16[264,256]{1,0:T(8,128)(2,1)S(1)}, u32[]{:S(2)}, u32[]{:S(2)}) collective-permute-start(bf16[264,256]{1,0:T(8,128)(2,1)S(1)} %get-tuple-element.68), channel_id=1, source_target_pairs={{0,8},{1,9},{2,10},{3,11},{4,12},{5,13},{6,14},{7,15},{8,0},{9,1},... | collective-permute-start | bytes 405512 | tf_op jit(solution)/shard_map/ppermute | solution.py:709
  21.4 1.3 %collective-permute-start.6 = (bf16[264,256]{1,0:T(8,128)(2,1)S(1)}, bf16[264,256]{1,0:T(8,128)(2,1)S(1)}, u32[]{:S(2)}, u32[]{:S(2)}) collective-permute-start(bf16[264,256]{1,0:T(8,128)(2,1)S(1)} %get-tuple-element.69), channel_id=1, source_target_pairs={{0,10},{1,11},{2,8},{3,9},{4,14},{5,15},{6,12},{7,13},{8,2},{9,3},... | collective-permute-start | bytes 405512 | tf_op jit(solution)/shard_map/ppermute | solution.py:709
  22.7 2.6 %collective-permute-start.7 = (bf16[264,256]{1,0:T(8,128)(2,1)S(1)}, bf16[264,256]{1,0:T(8,128)(2,1)S(1)}, u32[]{:S(2)}, u32[]{:S(2)}) collective-permute-start(bf16[264,256]{1,0:T(8,128)(2,1)S(1)} %get-tuple-element.70), channel_id=1, source_target_pairs={{0,12},{1,13},{2,14},{3,15},{4,8},{5,9},{6,10},{7,11},{8,4},{9,5},... | collective-permute-start | bytes 405512 | tf_op jit(solution)/shard_map/ppermute | solution.py:709
  25.3 1.5 %collective-permute-start.8 = (bf16[264,256]{1,0:T(8,128)(2,1)S(1)}, bf16[264,256]{1,0:T(8,128)(2,1)S(1)}, u32[]{:S(2)}, u32[]{:S(2)}) collective-permute-start(bf16[264,256]{1,0:T(8,128)(2,1)S(1)} %get-tuple-element.71), channel_id=1, source_target_pairs={{0,14},{1,15},{2,12},{3,13},{4,10},{5,11},{6,8},{7,9},{8,6},{9,7},... | collective-permute-start | bytes 405512 | tf_op jit(solution)/shard_map/ppermute | solution.py:709
  26.8 7.6 %near.3 = (bf16[512,1280]{1,0:T(8,128)(2,1)}, bf16[512,2560]{1,0:T(8,128)(2,1)}, f32[5,8,512]{2,1,0:T(8,128)S(1)}, bf16[8,264,256]{2,1,0:T(8,128)(2,1)}) custom-call(bf16[512,2048]{1,0:T(8,128)(2,1)} %raw_hbm.5, bf16[512,2048]{1,0:T(8,128)(2,1)} %key_hbm.9, bf16[8,4096]{1,0:T(8,128)(2,1)S(1)} %collective-permute-done.rim_ref, bf16[4,2048]{1,0:T(4,128)(2,1)} %tap_hbm.7, ...), custom_call_target="tpu_custom_call" | custom-call | flops 2013265920 | bytes 26214400 | tf_op jit(solution)/shard_map/near/pallas_call | solution.py:208
  34.4 0.6 collective-permute-done.8.refs_7_
  35.0 0.4 total.1
  35.4 4.5 %collective-permute-start.9 = (bf16[264,256]{1,0:T(8,128)(2,1)S(1)}, bf16[264,256]{1,0:T(8,128)(2,1)S(1)}, u32[]{:S(2)}, u32[]{:S(2)}) collective-permute-start(bf16[264,256]{1,0:T(8,128)(2,1)S(1)} %get-tuple-element.72), channel_id=1, source_target_pairs={{0,16},{1,17},{2,18},{3,19},{4,20},{5,21},{6,22},{7,23},{8,24},{9,... | collective-permute-start | bytes 405512 | tf_op jit(solution)/shard_map/ppermute | solution.py:728
  39.9 3.2 %near.4 = (bf16[512,256]{1,0:T(8,128)(2,1)}, bf16[512,512]{1,0:T(8,128)(2,1)}, f32[1,8,512]{2,1,0:T(8,128)S(1)}) custom-call(bf16[512,2048]{1,0:T(8,128)(2,1)} %raw_hbm.5, bf16[512,2048]{1,0:T(8,128)(2,1)} %key_hbm.9, bf16[8,4096]{1,0:T(8,128)(2,1)S(1)} %collective-permute-done.rim_ref, bf16[4,2048]{1,0:T(4,128)(2,1)} %tap_hbm.7, ...), custom_call_target="tpu_custom_call" | custom-call | flops 402653184 | bytes 5242880 | tf_op jit(solution)/shard_map/near/pallas_call | solution.py:208
  43.2 0.5 prefix.1
  43.6 0.6 collective-permute-start.10
  44.2 1.1 %collective-permute-start.11 = (bf16[264,256]{1,0:T(8,128)(2,1)S(1)}, bf16[264,256]{1,0:T(8,128)(2,1)S(1)}, u32[]{:S(2)}, u32[]{:S(2)}) collective-permute-start(bf16[264,256]{1,0:T(8,128)(2,1)S(1)} %get-tuple-element.87), channel_id=1, source_target_pairs={{0,4},{1,5},{2,6},{3,7},{4,0},{5,1},{6,2},{7,3},{8,12},{9,13},{10,... | collective-permute-start | bytes 405512 | tf_op jit(solution)/shard_map/ppermute | solution.py:709
  45.4 1.8 %collective-permute-start.12 = (bf16[264,256]{1,0:T(8,128)(2,1)S(1)}, bf16[264,256]{1,0:T(8,128)(2,1)S(1)}, u32[]{:S(2)}, u32[]{:S(2)}) collective-permute-start(bf16[264,256]{1,0:T(8,128)(2,1)S(1)} %get-tuple-element.88), channel_id=1, source_target_pairs={{0,6},{1,7},{2,4},{3,5},{4,2},{5,3},{6,0},{7,1},{8,14},{9,15},{10,... | collective-permute-start | bytes 405512 | tf_op jit(solution)/shard_map/ppermute | solution.py:709
  47.2 1.4 %collective-permute-start.13 = (bf16[264,256]{1,0:T(8,128)(2,1)S(1)}, bf16[264,256]{1,0:T(8,128)(2,1)S(1)}, u32[]{:S(2)}, u32[]{:S(2)}) collective-permute-start(bf16[264,256]{1,0:T(8,128)(2,1)S(1)} %get-tuple-element.89), channel_id=1, source_target_pairs={{0,8},{1,9},{2,10},{3,11},{4,12},{5,13},{6,14},{7,15},{8,0},{9,1},... | collective-permute-start | bytes 405512 | tf_op jit(solution)/shard_map/ppermute | solution.py:709
  48.6 0.7 %collective-permute-start.14 = (bf16[264,256]{1,0:T(8,128)(2,1)S(1)}, bf16[264,256]{1,0:T(8,128)(2,1)S(1)}, u32[]{:S(2)}, u32[]{:S(2)}) collective-permute-start(bf16[264,256]{1,0:T(8,128)(2,1)S(1)} %get-tuple-element.90), channel_id=1, source_target_pairs={{0,10},{1,11},{2,8},{3,9},{4,14},{5,15},{6,12},{7,13},{8,2},{9,3},... | collective-permute-start | bytes 405512 | tf_op jit(solution)/shard_map/ppermute | solution.py:709
  49.3 3.5 %collective-permute-done.10.refs_1_ = bf16[264,256]{1,0:T(8,128)(2,1)S(1)} collective-permute-done((bf16[264,256]{1,0:T(8,128)(2,1)S(1)}, bf16[264,256]{1,0:T(8,128)(2,1)S(1)}, u32[]{:S(2)}, u32[]{:S(2)}) %collective-permute-start.10) | collective-permute-done | bytes 135200 | tf_op jit(solution)/shard_map/ppermute | solution.py:709
  52.8 2.9 %collective-permute-start.16 = (bf16[264,256]{1,0:T(8,128)(2,1)S(1)}, bf16[264,256]{1,0:T(8,128)(2,1)S(1)}, u32[]{:S(2)}, u32[]{:S(2)}) collective-permute-start(bf16[264,256]{1,0:T(8,128)(2,1)S(1)} %get-tuple-element.92), channel_id=1, source_target_pairs={{0,14},{1,15},{2,12},{3,13},{4,10},{5,11},{6,8},{7,9},{8,6},{9,7},... | collective-permute-start | bytes 405512 | tf_op jit(solution)/shard_map/ppermute | solution.py:709
  55.7 4.8 %near.5 = (bf16[512,512]{1,0:T(8,128)(2,1)}, bf16[512,1024]{1,0:T(8,128)(2,1)}, f32[2,8,512]{2,1,0:T(8,128)S(1)}) custom-call(bf16[512,2048]{1,0:T(8,128)(2,1)} %raw_hbm.5, bf16[512,2048]{1,0:T(8,128)(2,1)} %key_hbm.9, bf16[8,4096]{1,0:T(8,128)(2,1)S(1)} %collective-permute-done.rim_ref, bf16[4,2048]{1,0:T(4,128)(2,1)} %tap_hbm.7, ...), custom_call_target="tpu_custom_call" | custom-call | flops 805306368 | bytes 10485760 | tf_op jit(solution)/shard_map/near/pallas_call | solution.py:208
  60.5 0.9 %split.1 = (bf16[8,264,256]{2,1,0:T(8,128)(2,1)S(1)}, bf16[8,264,256]{2,1,0:T(8,128)(2,1)S(1)}) custom-call(bf16[8,264,256]{2,1,0:T(8,128)(2,1)S(1)} %copy-done.2, bf16[264,256]{1,0:T(8,128)(2,1)S(1)} %get-tuple-element.85.refs_0_, bf16[264,256]{1,0:T(8,128)(2,1)S(1)} %collective-permute-done.10.refs_1_, ...), custom_call_target="tpu_custom_call" | custom-call | bytes 4194304 | tf_op jit(solution)/shard_map/split/pallas_call | solution.py:208
  61.8 2.3 %far.2.refs_10_ = bf16[512,4096]{1,0:T(8,128)(2,1)} custom-call(bf16[512,1280]{1,0:T(8,128)(2,1)S(1)} %copy-done.1, bf16[512,2560]{1,0:T(8,128)(2,1)S(1)} %copy-done, f32[5,8,512]{2,1,0:T(8,128)S(1)} %get-tuple-element.63.refs_2_, bf16[8,264,256]{2,1,0:T(8,128)(2,1)S(1)} %get-tuple-element.94.refs_3_), custom_call_target="tpu_custom_call" | custom-call | flops 536870912 | bytes 20971520 | tf_op jit(solution)/shard_map/far/pallas_call | solution.py:681
  64.3 2.3 %far.3 = bf16[512,4096]{1,0:T(8,128)(2,1)} custom-call(bf16[512,1280]{1,0:T(8,128)(2,1)S(1)} %copy-done.1, bf16[512,2560]{1,0:T(8,128)(2,1)S(1)} %copy-done, f32[5,8,512]{2,1,0:T(8,128)S(1)} %get-tuple-element.63.refs_2_, bf16[512,256]{1,0:T(8,128)(2,1)S(1)} %copy-done.6, bf16[512,512]{1,0:T(8,128)(2,1)S(1)} %copy-done.4, ...), custom_call_target="tpu_custom_call", output_to_operand_aliasing={{}: (10, {})} | custom-call | flops 536870912 | bytes 20971520 | tf_op jit(solution)/shard_map/far/pallas_call | solution.py:681
  (32 shorter events, 0.5 us)
Async XLA Ops:
  0.8 8.1 %collective-permute-start = (bf16[8,4096]{1,0:T(8,128)(2,1)S(1)}, bf16[8,4096]{1,0:T(8,128)(2,1)S(1)}, u32[]{:S(2)}, u32[]{:S(2)}) collective-permute-start(bf16[8,4096]{1,0:T(8,128)(2,1)S(1)} %tails.1), channel_id=1, source_target_pairs={{0,1},{1,2},{2,3},{3,4},{4,5},{5,6},{6,7},{7,8},{8,9},{9,10},{10,1... | collective-permute-start | bytes 196616 | tf_op jit(solution)/shard_map/ppermute | solution.py:712
  9.7 5.9 %collective-permute-start.1 = (bf16[8,264,256]{2,1,0:T(8,128)(2,1)S(1)}, bf16[8,264,256]{2,1,0:T(8,128)(2,1)S(1)}, u32[]{:S(2)}, u32[]{:S(2)}) collective-permute-start(bf16[8,264,256]{2,1,0:T(8,128)(2,1)S(1)} %early_state.1), channel_id=1, source_target_pairs={{0,1},{1,0},{2,3},{3,2},{4,5},{5,4},{6,7},{7,6},{8,9},{9,8},{10,11... | collective-permute-start | bytes 3244040 | tf_op jit(solution)/shard_map/ppermute | solution.py:719
  16.2 6.4 %collective-permute-start.2 = (bf16[264,256]{1,0:T(8,128)(2,1)S(1)}, bf16[264,256]{1,0:T(8,128)(2,1)S(1)}, u32[]{:S(2)}, u32[]{:S(2)}) collective-permute-start(bf16[264,256]{1,0:T(8,128)(2,1)S(1)} %get-tuple-element.65), channel_id=1, source_target_pairs={{0,2},{1,3},{2,0},{3,1},{4,6},{5,7},{6,4},{7,5},{8,10},{9,11},{10,... | collective-permute-start | bytes 405512 | tf_op jit(solution)/shard_map/ppermute | solution.py:709
  17.7 7.5 %collective-permute-start.3 = (bf16[264,256]{1,0:T(8,128)(2,1)S(1)}, bf16[264,256]{1,0:T(8,128)(2,1)S(1)}, u32[]{:S(2)}, u32[]{:S(2)}) collective-permute-start(bf16[264,256]{1,0:T(8,128)(2,1)S(1)} %get-tuple-element.66), channel_id=1, source_target_pairs={{0,4},{1,5},{2,6},{3,7},{4,0},{5,1},{6,2},{7,3},{8,12},{9,13},{10,... | collective-permute-start | bytes 405512 | tf_op jit(solution)/shard_map/ppermute | solution.py:709
  19.3 15.1 %collective-permute-start.4 = (bf16[264,256]{1,0:T(8,128)(2,1)S(1)}, bf16[264,256]{1,0:T(8,128)(2,1)S(1)}, u32[]{:S(2)}, u32[]{:S(2)}) collective-permute-start(bf16[264,256]{1,0:T(8,128)(2,1)S(1)} %get-tuple-element.67), channel_id=1, source_target_pairs={{0,6},{1,7},{2,4},{3,5},{4,2},{5,3},{6,0},{7,1},{8,14},{9,15},{10,... | collective-permute-start | bytes 405512 | tf_op jit(solution)/shard_map/ppermute | solution.py:709
  19.8 14.6 %collective-permute-start.5 = (bf16[264,256]{1,0:T(8,128)(2,1)S(1)}, bf16[264,256]{1,0:T(8,128)(2,1)S(1)}, u32[]{:S(2)}, u32[]{:S(2)}) collective-permute-start(bf16[264,256]{1,0:T(8,128)(2,1)S(1)} %get-tuple-element.68), channel_id=1, source_target_pairs={{0,8},{1,9},{2,10},{3,11},{4,12},{5,13},{6,14},{7,15},{8,0},{9,1},... | collective-permute-start | bytes 405512 | tf_op jit(solution)/shard_map/ppermute | solution.py:709
  21.4 13.0 %collective-permute-start.6 = (bf16[264,256]{1,0:T(8,128)(2,1)S(1)}, bf16[264,256]{1,0:T(8,128)(2,1)S(1)}, u32[]{:S(2)}, u32[]{:S(2)}) collective-permute-start(bf16[264,256]{1,0:T(8,128)(2,1)S(1)} %get-tuple-element.69), channel_id=1, source_target_pairs={{0,10},{1,11},{2,8},{3,9},{4,14},{5,15},{6,12},{7,13},{8,2},{9,3},... | collective-permute-start | bytes 405512 | tf_op jit(solution)/shard_map/ppermute | solution.py:709
  22.7 11.7 %collective-permute-start.7 = (bf16[264,256]{1,0:T(8,128)(2,1)S(1)}, bf16[264,256]{1,0:T(8,128)(2,1)S(1)}, u32[]{:S(2)}, u32[]{:S(2)}) collective-permute-start(bf16[264,256]{1,0:T(8,128)(2,1)S(1)} %get-tuple-element.70), channel_id=1, source_target_pairs={{0,12},{1,13},{2,14},{3,15},{4,8},{5,9},{6,10},{7,11},{8,4},{9,5},... | collective-permute-start | bytes 405512 | tf_op jit(solution)/shard_map/ppermute | solution.py:709
  25.3 9.8 %collective-permute-start.8 = (bf16[264,256]{1,0:T(8,128)(2,1)S(1)}, bf16[264,256]{1,0:T(8,128)(2,1)S(1)}, u32[]{:S(2)}, u32[]{:S(2)}) collective-permute-start(bf16[264,256]{1,0:T(8,128)(2,1)S(1)} %get-tuple-element.71), channel_id=1, source_target_pairs={{0,14},{1,15},{2,12},{3,13},{4,10},{5,11},{6,8},{7,9},{8,6},{9,7},... | collective-permute-start | bytes 405512 | tf_op jit(solution)/shard_map/ppermute | solution.py:709
  35.4 7.7 %collective-permute-start.9 = (bf16[264,256]{1,0:T(8,128)(2,1)S(1)}, bf16[264,256]{1,0:T(8,128)(2,1)S(1)}, u32[]{:S(2)}, u32[]{:S(2)}) collective-permute-start(bf16[264,256]{1,0:T(8,128)(2,1)S(1)} %get-tuple-element.72), channel_id=1, source_target_pairs={{0,16},{1,17},{2,18},{3,19},{4,20},{5,21},{6,22},{7,23},{8,24},{9,... | collective-permute-start | bytes 405512 | tf_op jit(solution)/shard_map/ppermute | solution.py:728
  43.6 9.2 %collective-permute-start.10 = (bf16[264,256]{1,0:T(8,128)(2,1)S(1)}, bf16[264,256]{1,0:T(8,128)(2,1)S(1)}, u32[]{:S(2)}, u32[]{:S(2)}) collective-permute-start(bf16[264,256]{1,0:T(8,128)(2,1)S(1)} %get-tuple-element.86), channel_id=1, source_target_pairs={{0,2},{1,3},{2,0},{3,1},{4,6},{5,7},{6,4},{7,5},{8,10},{9,11},{10,... | collective-permute-start | bytes 405512 | tf_op jit(solution)/shard_map/ppermute | solution.py:709
  44.2 8.6 %collective-permute-start.11 = (bf16[264,256]{1,0:T(8,128)(2,1)S(1)}, bf16[264,256]{1,0:T(8,128)(2,1)S(1)}, u32[]{:S(2)}, u32[]{:S(2)}) collective-permute-start(bf16[264,256]{1,0:T(8,128)(2,1)S(1)} %get-tuple-element.87), channel_id=1, source_target_pairs={{0,4},{1,5},{2,6},{3,7},{4,0},{5,1},{6,2},{7,3},{8,12},{9,13},{10,... | collective-permute-start | bytes 405512 | tf_op jit(solution)/shard_map/ppermute | solution.py:709
  45.4 15.1 %collective-permute-start.12 = (bf16[264,256]{1,0:T(8,128)(2,1)S(1)}, bf16[264,256]{1,0:T(8,128)(2,1)S(1)}, u32[]{:S(2)}, u32[]{:S(2)}) collective-permute-start(bf16[264,256]{1,0:T(8,128)(2,1)S(1)} %get-tuple-element.88), channel_id=1, source_target_pairs={{0,6},{1,7},{2,4},{3,5},{4,2},{5,3},{6,0},{7,1},{8,14},{9,15},{10,... | collective-permute-start | bytes 405512 | tf_op jit(solution)/shard_map/ppermute | solution.py:709
  47.2 13.3 %collective-permute-start.13 = (bf16[264,256]{1,0:T(8,128)(2,1)S(1)}, bf16[264,256]{1,0:T(8,128)(2,1)S(1)}, u32[]{:S(2)}, u32[]{:S(2)}) collective-permute-start(bf16[264,256]{1,0:T(8,128)(2,1)S(1)} %get-tuple-element.89), channel_id=1, source_target_pairs={{0,8},{1,9},{2,10},{3,11},{4,12},{5,13},{6,14},{7,15},{8,0},{9,1},... | collective-permute-start | bytes 405512 | tf_op jit(solution)/shard_map/ppermute | solution.py:709
  48.6 11.9 %collective-permute-start.14 = (bf16[264,256]{1,0:T(8,128)(2,1)S(1)}, bf16[264,256]{1,0:T(8,128)(2,1)S(1)}, u32[]{:S(2)}, u32[]{:S(2)}) collective-permute-start(bf16[264,256]{1,0:T(8,128)(2,1)S(1)} %get-tuple-element.90), channel_id=1, source_target_pairs={{0,10},{1,11},{2,8},{3,9},{4,14},{5,15},{6,12},{7,13},{8,2},{9,3},... | collective-permute-start | bytes 405512 | tf_op jit(solution)/shard_map/ppermute | solution.py:709
  52.8 7.7 %collective-permute-start.15 = (bf16[264,256]{1,0:T(8,128)(2,1)S(1)}, bf16[264,256]{1,0:T(8,128)(2,1)S(1)}, u32[]{:S(2)}, u32[]{:S(2)}) collective-permute-start(bf16[264,256]{1,0:T(8,128)(2,1)S(1)} %get-tuple-element.91), channel_id=1, source_target_pairs={{0,12},{1,13},{2,14},{3,15},{4,8},{5,9},{6,10},{7,11},{8,4},{9,5},... | collective-permute-start | bytes 405512 | tf_op jit(solution)/shard_map/ppermute | solution.py:709
  52.8 7.7 %collective-permute-start.16 = (bf16[264,256]{1,0:T(8,128)(2,1)S(1)}, bf16[264,256]{1,0:T(8,128)(2,1)S(1)}, u32[]{:S(2)}, u32[]{:S(2)}) collective-permute-start(bf16[264,256]{1,0:T(8,128)(2,1)S(1)} %get-tuple-element.92), channel_id=1, source_target_pairs={{0,14},{1,15},{2,12},{3,13},{4,10},{5,11},{6,8},{7,9},{8,6},{9,7},... | collective-permute-start | bytes 405512 | tf_op jit(solution)/shard_map/ppermute | solution.py:709
  55.7 4.9 %copy-start.2 = (bf16[8,264,256]{2,1,0:T(8,128)(2,1)S(1)}, bf16[8,264,256]{2,1,0:T(8,128)(2,1)}, u32[]{:S(2)}) copy-start(bf16[8,264,256]{2,1,0:T(8,128)(2,1)} %get-tuple-element.84.first_ref) | copy-start | bytes 3244036
  55.7 5.9 %copy-start = (bf16[512,2560]{1,0:T(8,128)(2,1)S(1)}, bf16[512,2560]{1,0:T(8,128)(2,1)}, u32[]{:S(2)}) copy-start(bf16[512,2560]{1,0:T(8,128)(2,1)} %get-tuple-element.62.refs_1_) | copy-start | bytes 7864324
  60.5 1.3 %copy-start.1 = (bf16[512,1280]{1,0:T(8,128)(2,1)S(1)}, bf16[512,1280]{1,0:T(8,128)(2,1)}, u32[]{:S(2)}) copy-start(bf16[512,1280]{1,0:T(8,128)(2,1)} %get-tuple-element.61.refs_0_) | copy-start | bytes 3932164
  61.5 2.8 %collective-permute-start.17 = (bf16[8,264,256]{2,1,0:T(8,128)(2,1)S(1)}, bf16[8,264,256]{2,1,0:T(8,128)(2,1)S(1)}, u32[]{:S(2)}, u32[]{:S(2)}) collective-permute-start(bf16[8,264,256]{2,1,0:T(8,128)(2,1)S(1)} %get-tuple-element.93), channel_id=1, source_target_pairs={{0,1},{1,0},{2,3},{3,2},{4,5},{5,4},{6,7},{7,6},{8,9},{9,8},{10,11... | collective-permute-start | bytes 3244040 | tf_op jit(solution)/shard_map/ppermute | solution.py:741
  61.8 2.5 %copy-start.3 = (bf16[512,1024]{1,0:T(8,128)(2,1)S(1)}, bf16[512,1024]{1,0:T(8,128)(2,1)}, u32[]{:S(2)}) copy-start(bf16[512,1024]{1,0:T(8,128)(2,1)} %get-tuple-element.82.refs_7_) | copy-start | bytes 3145732
  61.8 2.5 %copy-start.4 = (bf16[512,512]{1,0:T(8,128)(2,1)S(1)}, bf16[512,512]{1,0:T(8,128)(2,1)}, u32[]{:S(2)}) copy-start(bf16[512,512]{1,0:T(8,128)(2,1)} %get-tuple-element.75.refs_4_) | copy-start | bytes 1572868
  61.8 2.5 %copy-start.5 = (bf16[512,512]{1,0:T(8,128)(2,1)S(1)}, bf16[512,512]{1,0:T(8,128)(2,1)}, u32[]{:S(2)}) copy-start(bf16[512,512]{1,0:T(8,128)(2,1)} %get-tuple-element.81.refs_6_) | copy-start | bytes 1572868
  61.8 2.5 %copy-start.6 = (bf16[512,256]{1,0:T(8,128)(2,1)S(1)}, bf16[512,256]{1,0:T(8,128)(2,1)}, u32[]{:S(2)}) copy-start(bf16[512,256]{1,0:T(8,128)(2,1)} %get-tuple-element.74.refs_3_) | copy-start | bytes 786436

commit v4 on v3

--- a/solution.py
+++ b/solution.py
@@ -27,7 +27,7 @@
 TILE = 256
 STEP = 128
 EMPTY = -1e30
-ORDER = (7, 6, 5, 3, 4, 2, 1)
+ORDER = (1, 7, 2, 6, 4, 5, 3)
 SIDES = [(True, local) for local in range(LOCAL)] + [(False, local) for local in range(LOCAL)]
 PARTS = (SIDES[:5], SIDES[5:6], SIDES[6:])
 SCALE = DK**-0.5
@@ -392,25 +392,22 @@
 
 
 def split_kernel(first_ref, *refs):
-    records, (keep_ref, send_ref, enter_buf) = refs[:OWNERS], refs[OWNERS:]
+    records, (keep_ref, send_ref) = refs[:OWNERS], refs[OWNERS:]
     core, _, chip = place()
     second = core == 1
     for mask, record in enumerate(records):
-        enter_buf[chip ^ mask] = record[...]
-    for local in range(LOCAL):
-        at = local * PIECES
-        early = read_aux(enter_buf[at, DK:ROWS])
-        before, after, joined = merge(early, read_aux(first_ref[at, DK:ROWS]))
+        at = chip ^ mask
+        before, after, joined = merge(read_aux(record[DK:ROWS]), read_aux(first_ref[at, DK:ROWS]))
         aux = aux_rows(*joined)
-        plain = enter_buf[at, DK:ROWS]
-        for piece in range(PIECES):
-            chip_part = enter_buf[at + piece, 0:DK]
-            moved = before * chip_part.astype(F32) + after * first_ref[at + piece, 0:DK].astype(F32)
-            moved = moved.astype(BF16)
-            keep_ref[at + piece, 0:DK] = jnp.where(second, moved, chip_part)
-            send_ref[at + piece, 0:DK] = jnp.where(second, chip_part, moved)
-            keep_ref[at + piece, DK:ROWS] = jnp.where(second, aux, plain)
-            send_ref[at + piece, DK:ROWS] = jnp.where(second, plain, aux)
+        plain = record[DK:ROWS]
+        keep_ref[at, DK:ROWS] = jnp.where(second, aux, plain)
+        send_ref[at, DK:ROWS] = jnp.where(second, plain, aux)
+        for start in range(0, DK, STEP):
+            chip_part = record[start : start + STEP]
+            first_part = first_ref[at, start : start + STEP]
+            moved = (before * chip_part.astype(F32) + after * first_part.astype(F32)).astype(BF16)
+            keep_ref[at, start : start + STEP] = jnp.where(second, moved, chip_part)
+            send_ref[at, start : start + STEP] = jnp.where(second, chip_part, moved)
 
 
 def split_call(records, first):
@@ -419,7 +416,7 @@
         split_kernel,
         [("vmem", first)] + [("vmem", record) for record in records],
         [("vmem", shape, BF16)] * 2,
-        [pltpu.VMEM(shape, BF16)],
+        [],
         "split",
         0,
         4 << 20,

time: 67.2 us -> 67.1 us (level)
  transfers between devices with their start and end apart: 18 -> 18, of which waited for: 3 -> 2; matrix products, arithmetic and copies ran while one was open for 0% -> 0% of each run, Pallas kernels for 40% -> 40%
where the time goes in v4:
time: 67.1 us; the launch traced here: 66.6 us
  Pallas kernels  33 us (49%)
  starting transfers between devices  28.7 us (43%)
  waiting for transfers between devices  4.09 us (6%)
    pallas_call x12, Pallas kernels, kernel_call(): pl.pallas_call(kernel, in_specs=in_specs, out_specs=[VMEM_SPEC if where =...  28.3 us
    ppermute x14, starting transfers between devices, spread(): moved[mask] = lax.ppermute(records[mask], AXES, route)  19.1 us
    pallas_call x2, Pallas kernels, far_call(): pl.pallas_call(functools.partial(far_kernel, mine, slots, len(near)), in_...  4.63 us
    ppermute x1, starting transfers between devices, on_device(): entering = lax.ppermute(total, AXES, up(1))  4.5 us
    ppermute x14, waiting for transfers between devices, spread(): moved[mask] = lax.ppermute(records[mask], AXES, route)  4.08 us
    ppermute x1, starting transfers between devices, on_device(): other = lax.ppermute(sent, AXES, swap)  2.7 us
    ppermute x1, starting transfers between devices, on_device(): rim = lax.ppermute(tails_call(key_raw, query_raw), AXES, line)  2.36 us
  transfers between devices with their start and end apart: 18, of which 2 were waited for; matrix products, arithmetic and copies ran while one was open for 0% of the time, Pallas kernels for 40%

profile of v4, /device:TPU:0, one launch (start us, length us, event | category | flops | bytes accessed | tf_op | source)
XLA Modules:
  0.0 66.6 jit_solution(11212165539017217262)
XLA Ops:
  0.0 0.8 %tails.1 = bf16[8,4096]{1,0:T(8,128)(2,1)S(1)} custom-call(bf16[512,2048]{1,0:T(8,128)(2,1)} %key_hbm.9, bf16[512,2048]{1,0:T(8,128)(2,1)} %raw_hbm.5), custom_call_target="tpu_custom_call" | custom-call | bytes 131072 | tf_op jit(solution)/shard_map/tails/pallas_call | solution.py:208
  0.8 2.4 %collective-permute-start = (bf16[8,4096]{1,0:T(8,128)(2,1)S(1)}, bf16[8,4096]{1,0:T(8,128)(2,1)S(1)}, u32[]{:S(2)}, u32[]{:S(2)}) collective-permute-start(bf16[8,4096]{1,0:T(8,128)(2,1)S(1)} %tails.1), channel_id=1, source_target_pairs={{0,1},{1,2},{2,3},{3,4},{4,5},{5,6},{6,7},{7,8},{8,9},{9,10},{10,1... | collective-permute-start | bytes 196616 | tf_op jit(solution)/shard_map/ppermute | solution.py:709
  3.2 2.9 %prepare.1 = (f32[40,512]{1,0:T(8,128)S(1)}, bf16[512,2048]{1,0:T(8,128)(2,1)S(1)}, bf16[4,2048]{1,0:T(4,128)(2,1)S(1)}, bf16[512,4096]{1,0:T(8,128)(2,1)S(1)}) custom-call(bf16[8,512]{1,0:T(8,128)(2,1)} %bitcast.2, bf16[8,512]{1,0:T(8,128)(2,1)} %bitcast.3, bf16[512,2048]{1,0:T(8,128)(2,1)} %key_hbm.9, bf16[4,2048]{1,0:T(4,128)(2,1)} %key_tap_hbm.5, ...), custom_call_target="tpu_custom_call" | custom-call | bytes 6291456 | tf_op jit(solution)/shard_map/prepare/pallas_call | solution.py:208
  6.1 2.8 %late_state.1 = (f32[4,256,512]{2,1,0:T(8,128)S(1)}, f32[4,8,256]{2,1,0:T(8,128)S(1)}) custom-call(bf16[512,2048]{1,0:T(8,128)(2,1)S(1)} %get-tuple-element.51.raw_ref, bf16[4,2048]{1,0:T(4,128)(2,1)S(1)} %get-tuple-element.52.tap_ref, bf16[512,4096]{1,0:T(8,128)(2,1)S(1)} %get-tuple-element.53.val_ref, f32[40,512]{1,0:T(8,128)S(1)} %get-tuple-element.80.rows_ref), custom_call_target="tpu_custom_call" | custom-call | flops 536870912 | bytes 12582912 | tf_op jit(solution)/shard_map/late_state/pallas_call | solution.py:208
  8.9 0.8 %early_state.1 = bf16[8,264,256]{2,1,0:T(8,128)(2,1)S(1)} custom-call(bf16[512,2048]{1,0:T(8,128)(2,1)S(1)} %get-tuple-element.51.raw_ref, bf16[8,4096]{1,0:T(8,128)(2,1)S(1)} %collective-permute-done.rim_ref, bf16[4,2048]{1,0:T(4,128)(2,1)S(1)} %get-tuple-element.52.tap_ref, bf16[512,4096]{1,0:T(8,128)(2,1)S(1)} %get-tuple-element.53.val_ref, ...), custom_call_target="tpu_custom_call" | custom-call | flops 1048576 | bytes 4194304 | tf_op jit(solution)/shard_map/early_state/pallas_call | solution.py:208
  9.7 2.7 %collective-permute-start.1 = (bf16[8,264,256]{2,1,0:T(8,128)(2,1)S(1)}, bf16[8,264,256]{2,1,0:T(8,128)(2,1)S(1)}, u32[]{:S(2)}, u32[]{:S(2)}) collective-permute-start(bf16[8,264,256]{2,1,0:T(8,128)(2,1)S(1)} %early_state.1), channel_id=1, source_target_pairs={{0,1},{1,0},{2,3},{3,2},{4,5},{5,4},{6,7},{7,6},{8,9},{9,8},{10,11... | collective-permute-start | bytes 3244040 | tf_op jit(solution)/shard_map/ppermute | solution.py:716
  12.4 3.2 %state.1 = (bf16[8,264,256]{2,1,0:T(8,128)(2,1)S(1)}, bf16[512,1024]{1,0:T(8,128)(2,1)S(1)}) custom-call(bf16[512,2048]{1,0:T(8,128)(2,1)S(1)} %get-tuple-element.51.raw_ref, bf16[8,4096]{1,0:T(8,128)(2,1)S(1)} %collective-permute-done.rim_ref, bf16[4,2048]{1,0:T(4,128)(2,1)S(1)} %get-tuple-element.52.tap_ref, ...), custom_call_target="tpu_custom_call" | custom-call | flops 536870912 | bytes 12582912 | tf_op jit(solution)/shard_map/state/pallas_call | solution.py:208
  15.5 0.7 %join.1 = (bf16[264,256]{1,0:T(8,128)(2,1)S(1)}, bf16[264,256]{1,0:T(8,128)(2,1)S(1)}, bf16[264,256]{1,0:T(8,128)(2,1)S(1)}, bf16[264,256]{1,0:T(8,128)(2,1)S(1)...) custom-call(bf16[8,264,256]{2,1,0:T(8,128)(2,1)S(1)} %get-tuple-elem, ...), custom_call_target="tpu_custom_call" | custom-call | bytes 4194304 | tf_op jit(solution)/shard_map/join/pallas_call | solution.py:208
  16.2 1.5 %collective-permute-start.2 = (bf16[264,256]{1,0:T(8,128)(2,1)S(1)}, bf16[264,256]{1,0:T(8,128)(2,1)S(1)}, u32[]{:S(2)}, u32[]{:S(2)}) collective-permute-start(bf16[264,256]{1,0:T(8,128)(2,1)S(1)} %get-tuple-element.65), channel_id=1, source_target_pairs={{0,2},{1,3},{2,0},{3,1},{4,6},{5,7},{6,4},{7,5},{8,10},{9,11},{10,... | collective-permute-start | bytes 405512 | tf_op jit(solution)/shard_map/ppermute | solution.py:706
  17.7 1.6 %collective-permute-start.3 = (bf16[264,256]{1,0:T(8,128)(2,1)S(1)}, bf16[264,256]{1,0:T(8,128)(2,1)S(1)}, u32[]{:S(2)}, u32[]{:S(2)}) collective-permute-start(bf16[264,256]{1,0:T(8,128)(2,1)S(1)} %get-tuple-element.66), channel_id=1, source_target_pairs={{0,4},{1,5},{2,6},{3,7},{4,0},{5,1},{6,2},{7,3},{8,12},{9,13},{10,... | collective-permute-start | bytes 405512 | tf_op jit(solution)/shard_map/ppermute | solution.py:706
  19.3 0.5 collective-permute-start.4
  19.8 1.6 %collective-permute-start.5 = (bf16[264,256]{1,0:T(8,128)(2,1)S(1)}, bf16[264,256]{1,0:T(8,128)(2,1)S(1)}, u32[]{:S(2)}, u32[]{:S(2)}) collective-permute-start(bf16[264,256]{1,0:T(8,128)(2,1)S(1)} %get-tuple-element.68), channel_id=1, source_target_pairs={{0,8},{1,9},{2,10},{3,11},{4,12},{5,13},{6,14},{7,15},{8,0},{9,1},... | collective-permute-start | bytes 405512 | tf_op jit(solution)/shard_map/ppermute | solution.py:706
  21.4 1.3 %collective-permute-start.6 = (bf16[264,256]{1,0:T(8,128)(2,1)S(1)}, bf16[264,256]{1,0:T(8,128)(2,1)S(1)}, u32[]{:S(2)}, u32[]{:S(2)}) collective-permute-start(bf16[264,256]{1,0:T(8,128)(2,1)S(1)} %get-tuple-element.69), channel_id=1, source_target_pairs={{0,10},{1,11},{2,8},{3,9},{4,14},{5,15},{6,12},{7,13},{8,2},{9,3},... | collective-permute-start | bytes 405512 | tf_op jit(solution)/shard_map/ppermute | solution.py:706
  22.7 2.6 %collective-permute-start.7 = (bf16[264,256]{1,0:T(8,128)(2,1)S(1)}, bf16[264,256]{1,0:T(8,128)(2,1)S(1)}, u32[]{:S(2)}, u32[]{:S(2)}) collective-permute-start(bf16[264,256]{1,0:T(8,128)(2,1)S(1)} %get-tuple-element.70), channel_id=1, source_target_pairs={{0,12},{1,13},{2,14},{3,15},{4,8},{5,9},{6,10},{7,11},{8,4},{9,5},... | collective-permute-start | bytes 405512 | tf_op jit(solution)/shard_map/ppermute | solution.py:706
  25.3 1.5 %collective-permute-start.8 = (bf16[264,256]{1,0:T(8,128)(2,1)S(1)}, bf16[264,256]{1,0:T(8,128)(2,1)S(1)}, u32[]{:S(2)}, u32[]{:S(2)}) collective-permute-start(bf16[264,256]{1,0:T(8,128)(2,1)S(1)} %get-tuple-element.71), channel_id=1, source_target_pairs={{0,14},{1,15},{2,12},{3,13},{4,10},{5,11},{6,8},{7,9},{8,6},{9,7},... | collective-permute-start | bytes 405512 | tf_op jit(solution)/shard_map/ppermute | solution.py:706
  26.8 7.6 %near.3 = (bf16[512,1280]{1,0:T(8,128)(2,1)}, bf16[512,2560]{1,0:T(8,128)(2,1)}, f32[5,8,512]{2,1,0:T(8,128)S(1)}, bf16[8,264,256]{2,1,0:T(8,128)(2,1)}) custom-call(bf16[512,2048]{1,0:T(8,128)(2,1)} %raw_hbm.5, bf16[512,2048]{1,0:T(8,128)(2,1)} %key_hbm.9, bf16[8,4096]{1,0:T(8,128)(2,1)S(1)} %collective-permute-done.rim_ref, bf16[4,2048]{1,0:T(4,128)(2,1)} %tap_hbm.7, ...), custom_call_target="tpu_custom_call" | custom-call | flops 2013265920 | bytes 26214400 | tf_op jit(solution)/shard_map/near/pallas_call | solution.py:208
  34.4 0.6 collective-permute-done.8.refs_7_
  35.4 4.5 %collective-permute-start.9 = (bf16[264,256]{1,0:T(8,128)(2,1)S(1)}, bf16[264,256]{1,0:T(8,128)(2,1)S(1)}, u32[]{:S(2)}, u32[]{:S(2)}) collective-permute-start(bf16[264,256]{1,0:T(8,128)(2,1)S(1)} %get-tuple-element.72), channel_id=1, source_target_pairs={{0,16},{1,17},{2,18},{3,19},{4,20},{5,21},{6,22},{7,23},{8,24},{9,... | collective-permute-start | bytes 405512 | tf_op jit(solution)/shard_map/ppermute | solution.py:725
  39.9 3.2 %near.4 = (bf16[512,256]{1,0:T(8,128)(2,1)}, bf16[512,512]{1,0:T(8,128)(2,1)}, f32[1,8,512]{2,1,0:T(8,128)S(1)}) custom-call(bf16[512,2048]{1,0:T(8,128)(2,1)} %raw_hbm.5, bf16[512,2048]{1,0:T(8,128)(2,1)} %key_hbm.9, bf16[8,4096]{1,0:T(8,128)(2,1)S(1)} %collective-permute-done.rim_ref, bf16[4,2048]{1,0:T(4,128)(2,1)} %tap_hbm.7, ...), custom_call_target="tpu_custom_call" | custom-call | flops 402653184 | bytes 5242880 | tf_op jit(solution)/shard_map/near/pallas_call | solution.py:208
  43.2 0.5 prefix.1
  43.6 0.6 collective-permute-start.10
  44.2 1.1 %collective-permute-start.11 = (bf16[264,256]{1,0:T(8,128)(2,1)S(1)}, bf16[264,256]{1,0:T(8,128)(2,1)S(1)}, u32[]{:S(2)}, u32[]{:S(2)}) collective-permute-start(bf16[264,256]{1,0:T(8,128)(2,1)S(1)} %get-tuple-element.87), channel_id=1, source_target_pairs={{0,4},{1,5},{2,6},{3,7},{4,0},{5,1},{6,2},{7,3},{8,12},{9,13},{10,... | collective-permute-start | bytes 405512 | tf_op jit(solution)/shard_map/ppermute | solution.py:706
  45.4 1.8 %collective-permute-start.12 = (bf16[264,256]{1,0:T(8,128)(2,1)S(1)}, bf16[264,256]{1,0:T(8,128)(2,1)S(1)}, u32[]{:S(2)}, u32[]{:S(2)}) collective-permute-start(bf16[264,256]{1,0:T(8,128)(2,1)S(1)} %get-tuple-element.88), channel_id=1, source_target_pairs={{0,6},{1,7},{2,4},{3,5},{4,2},{5,3},{6,0},{7,1},{8,14},{9,15},{10,... | collective-permute-start | bytes 405512 | tf_op jit(solution)/shard_map/ppermute | solution.py:706
  47.2 1.4 %collective-permute-start.13 = (bf16[264,256]{1,0:T(8,128)(2,1)S(1)}, bf16[264,256]{1,0:T(8,128)(2,1)S(1)}, u32[]{:S(2)}, u32[]{:S(2)}) collective-permute-start(bf16[264,256]{1,0:T(8,128)(2,1)S(1)} %get-tuple-element.89), channel_id=1, source_target_pairs={{0,8},{1,9},{2,10},{3,11},{4,12},{5,13},{6,14},{7,15},{8,0},{9,1},... | collective-permute-start | bytes 405512 | tf_op jit(solution)/shard_map/ppermute | solution.py:706
  48.6 0.7 %collective-permute-start.14 = (bf16[264,256]{1,0:T(8,128)(2,1)S(1)}, bf16[264,256]{1,0:T(8,128)(2,1)S(1)}, u32[]{:S(2)}, u32[]{:S(2)}) collective-permute-start(bf16[264,256]{1,0:T(8,128)(2,1)S(1)} %get-tuple-element.90), channel_id=1, source_target_pairs={{0,10},{1,11},{2,8},{3,9},{4,14},{5,15},{6,12},{7,13},{8,2},{9,3},... | collective-permute-start | bytes 405512 | tf_op jit(solution)/shard_map/ppermute | solution.py:706
  49.3 3.5 %collective-permute-done.10.refs_1_ = bf16[264,256]{1,0:T(8,128)(2,1)S(1)} collective-permute-done((bf16[264,256]{1,0:T(8,128)(2,1)S(1)}, bf16[264,256]{1,0:T(8,128)(2,1)S(1)}, u32[]{:S(2)}, u32[]{:S(2)}) %collective-permute-start.10) | collective-permute-done | bytes 135200 | tf_op jit(solution)/shard_map/ppermute | solution.py:706
  52.8 2.9 %collective-permute-start.16 = (bf16[264,256]{1,0:T(8,128)(2,1)S(1)}, bf16[264,256]{1,0:T(8,128)(2,1)S(1)}, u32[]{:S(2)}, u32[]{:S(2)}) collective-permute-start(bf16[264,256]{1,0:T(8,128)(2,1)S(1)} %get-tuple-element.92), channel_id=1, source_target_pairs={{0,14},{1,15},{2,12},{3,13},{4,10},{5,11},{6,8},{7,9},{8,6},{9,7},... | collective-permute-start | bytes 405512 | tf_op jit(solution)/shard_map/ppermute | solution.py:706
  55.7 4.8 %near.5 = (bf16[512,512]{1,0:T(8,128)(2,1)}, bf16[512,1024]{1,0:T(8,128)(2,1)}, f32[2,8,512]{2,1,0:T(8,128)S(1)}) custom-call(bf16[512,2048]{1,0:T(8,128)(2,1)} %raw_hbm.5, bf16[512,2048]{1,0:T(8,128)(2,1)} %key_hbm.9, bf16[8,4096]{1,0:T(8,128)(2,1)S(1)} %collective-permute-done.rim_ref, bf16[4,2048]{1,0:T(4,128)(2,1)} %tap_hbm.7, ...), custom_call_target="tpu_custom_call" | custom-call | flops 805306368 | bytes 10485760 | tf_op jit(solution)/shard_map/near/pallas_call | solution.py:208
  60.5 0.7 %split.1 = (bf16[8,264,256]{2,1,0:T(8,128)(2,1)S(1)}, bf16[8,264,256]{2,1,0:T(8,128)(2,1)S(1)}) custom-call(bf16[8,264,256]{2,1,0:T(8,128)(2,1)S(1)} %copy-done.2, bf16[264,256]{1,0:T(8,128)(2,1)S(1)} %get-tuple-element.85.refs_0_, bf16[264,256]{1,0:T(8,128)(2,1)S(1)} %collective-permute-done.10.refs_1_, ...), custom_call_target="tpu_custom_call" | custom-call | bytes 4194304 | tf_op jit(solution)/shard_map/split/pallas_call | solution.py:208
  61.3 0.4 copy-done.1
  61.8 2.3 %far.2.refs_10_ = bf16[512,4096]{1,0:T(8,128)(2,1)} custom-call(bf16[512,1280]{1,0:T(8,128)(2,1)S(1)} %copy-done.1, bf16[512,2560]{1,0:T(8,128)(2,1)S(1)} %copy-done, f32[5,8,512]{2,1,0:T(8,128)S(1)} %get-tuple-element.63.refs_2_, bf16[8,264,256]{2,1,0:T(8,128)(2,1)S(1)} %get-tuple-element.94.refs_3_), custom_call_target="tpu_custom_call" | custom-call | flops 536870912 | bytes 20971520 | tf_op jit(solution)/shard_map/far/pallas_call | solution.py:678
  64.2 2.3 %far.3 = bf16[512,4096]{1,0:T(8,128)(2,1)} custom-call(bf16[512,1280]{1,0:T(8,128)(2,1)S(1)} %copy-done.1, bf16[512,2560]{1,0:T(8,128)(2,1)S(1)} %copy-done, f32[5,8,512]{2,1,0:T(8,128)S(1)} %get-tuple-element.63.refs_2_, bf16[512,256]{1,0:T(8,128)(2,1)S(1)} %copy-done.6, bf16[512,512]{1,0:T(8,128)(2,1)S(1)} %copy-done.4, ...), custom_call_target="tpu_custom_call", output_to_operand_aliasing={{}: (10, {})} | custom-call | flops 536870912 | bytes 20971520 | tf_op jit(solution)/shard_map/far/pallas_call | solution.py:678
  (32 shorter events, 0.5 us)
Async XLA Ops:
  0.8 8.1 %collective-permute-start = (bf16[8,4096]{1,0:T(8,128)(2,1)S(1)}, bf16[8,4096]{1,0:T(8,128)(2,1)S(1)}, u32[]{:S(2)}, u32[]{:S(2)}) collective-permute-start(bf16[8,4096]{1,0:T(8,128)(2,1)S(1)} %tails.1), channel_id=1, source_target_pairs={{0,1},{1,2},{2,3},{3,4},{4,5},{5,6},{6,7},{7,8},{8,9},{9,10},{10,1... | collective-permute-start | bytes 196616 | tf_op jit(solution)/shard_map/ppermute | solution.py:709
  9.7 5.9 %collective-permute-start.1 = (bf16[8,264,256]{2,1,0:T(8,128)(2,1)S(1)}, bf16[8,264,256]{2,1,0:T(8,128)(2,1)S(1)}, u32[]{:S(2)}, u32[]{:S(2)}) collective-permute-start(bf16[8,264,256]{2,1,0:T(8,128)(2,1)S(1)} %early_state.1), channel_id=1, source_target_pairs={{0,1},{1,0},{2,3},{3,2},{4,5},{5,4},{6,7},{7,6},{8,9},{9,8},{10,11... | collective-permute-start | bytes 3244040 | tf_op jit(solution)/shard_map/ppermute | solution.py:716
  16.2 6.4 %collective-permute-start.2 = (bf16[264,256]{1,0:T(8,128)(2,1)S(1)}, bf16[264,256]{1,0:T(8,128)(2,1)S(1)}, u32[]{:S(2)}, u32[]{:S(2)}) collective-permute-start(bf16[264,256]{1,0:T(8,128)(2,1)S(1)} %get-tuple-element.65), channel_id=1, source_target_pairs={{0,2},{1,3},{2,0},{3,1},{4,6},{5,7},{6,4},{7,5},{8,10},{9,11},{10,... | collective-permute-start | bytes 405512 | tf_op jit(solution)/shard_map/ppermute | solution.py:706
  17.7 7.5 %collective-permute-start.3 = (bf16[264,256]{1,0:T(8,128)(2,1)S(1)}, bf16[264,256]{1,0:T(8,128)(2,1)S(1)}, u32[]{:S(2)}, u32[]{:S(2)}) collective-permute-start(bf16[264,256]{1,0:T(8,128)(2,1)S(1)} %get-tuple-element.66), channel_id=1, source_target_pairs={{0,4},{1,5},{2,6},{3,7},{4,0},{5,1},{6,2},{7,3},{8,12},{9,13},{10,... | collective-permute-start | bytes 405512 | tf_op jit(solution)/shard_map/ppermute | solution.py:706
  19.3 15.1 %collective-permute-start.4 = (bf16[264,256]{1,0:T(8,128)(2,1)S(1)}, bf16[264,256]{1,0:T(8,128)(2,1)S(1)}, u32[]{:S(2)}, u32[]{:S(2)}) collective-permute-start(bf16[264,256]{1,0:T(8,128)(2,1)S(1)} %get-tuple-element.67), channel_id=1, source_target_pairs={{0,6},{1,7},{2,4},{3,5},{4,2},{5,3},{6,0},{7,1},{8,14},{9,15},{10,... | collective-permute-start | bytes 405512 | tf_op jit(solution)/shard_map/ppermute | solution.py:706
  19.8 14.6 %collective-permute-start.5 = (bf16[264,256]{1,0:T(8,128)(2,1)S(1)}, bf16[264,256]{1,0:T(8,128)(2,1)S(1)}, u32[]{:S(2)}, u32[]{:S(2)}) collective-permute-start(bf16[264,256]{1,0:T(8,128)(2,1)S(1)} %get-tuple-element.68), channel_id=1, source_target_pairs={{0,8},{1,9},{2,10},{3,11},{4,12},{5,13},{6,14},{7,15},{8,0},{9,1},... | collective-permute-start | bytes 405512 | tf_op jit(solution)/shard_map/ppermute | solution.py:706
  21.4 13.0 %collective-permute-start.6 = (bf16[264,256]{1,0:T(8,128)(2,1)S(1)}, bf16[264,256]{1,0:T(8,128)(2,1)S(1)}, u32[]{:S(2)}, u32[]{:S(2)}) collective-permute-start(bf16[264,256]{1,0:T(8,128)(2,1)S(1)} %get-tuple-element.69), channel_id=1, source_target_pairs={{0,10},{1,11},{2,8},{3,9},{4,14},{5,15},{6,12},{7,13},{8,2},{9,3},... | collective-permute-start | bytes 405512 | tf_op jit(solution)/shard_map/ppermute | solution.py:706
  22.7 11.7 %collective-permute-start.7 = (bf16[264,256]{1,0:T(8,128)(2,1)S(1)}, bf16[264,256]{1,0:T(8,128)(2,1)S(1)}, u32[]{:S(2)}, u32[]{:S(2)}) collective-permute-start(bf16[264,256]{1,0:T(8,128)(2,1)S(1)} %get-tuple-element.70), channel_id=1, source_target_pairs={{0,12},{1,13},{2,14},{3,15},{4,8},{5,9},{6,10},{7,11},{8,4},{9,5},... | collective-permute-start | bytes 405512 | tf_op jit(solution)/shard_map/ppermute | solution.py:706
  25.3 9.8 %collective-permute-start.8 = (bf16[264,256]{1,0:T(8,128)(2,1)S(1)}, bf16[264,256]{1,0:T(8,128)(2,1)S(1)}, u32[]{:S(2)}, u32[]{:S(2)}) collective-permute-start(bf16[264,256]{1,0:T(8,128)(2,1)S(1)} %get-tuple-element.71), channel_id=1, source_target_pairs={{0,14},{1,15},{2,12},{3,13},{4,10},{5,11},{6,8},{7,9},{8,6},{9,7},... | collective-permute-start | bytes 405512 | tf_op jit(solution)/shard_map/ppermute | solution.py:706
  35.4 7.7 %collective-permute-start.9 = (bf16[264,256]{1,0:T(8,128)(2,1)S(1)}, bf16[264,256]{1,0:T(8,128)(2,1)S(1)}, u32[]{:S(2)}, u32[]{:S(2)}) collective-permute-start(bf16[264,256]{1,0:T(8,128)(2,1)S(1)} %get-tuple-element.72), channel_id=1, source_target_pairs={{0,16},{1,17},{2,18},{3,19},{4,20},{5,21},{6,22},{7,23},{8,24},{9,... | collective-permute-start | bytes 405512 | tf_op jit(solution)/shard_map/ppermute | solution.py:725
  43.6 9.2 %collective-permute-start.10 = (bf16[264,256]{1,0:T(8,128)(2,1)S(1)}, bf16[264,256]{1,0:T(8,128)(2,1)S(1)}, u32[]{:S(2)}, u32[]{:S(2)}) collective-permute-start(bf16[264,256]{1,0:T(8,128)(2,1)S(1)} %get-tuple-element.86), channel_id=1, source_target_pairs={{0,2},{1,3},{2,0},{3,1},{4,6},{5,7},{6,4},{7,5},{8,10},{9,11},{10,... | collective-permute-start | bytes 405512 | tf_op jit(solution)/shard_map/ppermute | solution.py:706
  44.2 8.6 %collective-permute-start.11 = (bf16[264,256]{1,0:T(8,128)(2,1)S(1)}, bf16[264,256]{1,0:T(8,128)(2,1)S(1)}, u32[]{:S(2)}, u32[]{:S(2)}) collective-permute-start(bf16[264,256]{1,0:T(8,128)(2,1)S(1)} %get-tuple-element.87), channel_id=1, source_target_pairs={{0,4},{1,5},{2,6},{3,7},{4,0},{5,1},{6,2},{7,3},{8,12},{9,13},{10,... | collective-permute-start | bytes 405512 | tf_op jit(solution)/shard_map/ppermute | solution.py:706
  45.4 15.1 %collective-permute-start.12 = (bf16[264,256]{1,0:T(8,128)(2,1)S(1)}, bf16[264,256]{1,0:T(8,128)(2,1)S(1)}, u32[]{:S(2)}, u32[]{:S(2)}) collective-permute-start(bf16[264,256]{1,0:T(8,128)(2,1)S(1)} %get-tuple-element.88), channel_id=1, source_target_pairs={{0,6},{1,7},{2,4},{3,5},{4,2},{5,3},{6,0},{7,1},{8,14},{9,15},{10,... | collective-permute-start | bytes 405512 | tf_op jit(solution)/shard_map/ppermute | solution.py:706
  47.2 13.3 %collective-permute-start.13 = (bf16[264,256]{1,0:T(8,128)(2,1)S(1)}, bf16[264,256]{1,0:T(8,128)(2,1)S(1)}, u32[]{:S(2)}, u32[]{:S(2)}) collective-permute-start(bf16[264,256]{1,0:T(8,128)(2,1)S(1)} %get-tuple-element.89), channel_id=1, source_target_pairs={{0,8},{1,9},{2,10},{3,11},{4,12},{5,13},{6,14},{7,15},{8,0},{9,1},... | collective-permute-start | bytes 405512 | tf_op jit(solution)/shard_map/ppermute | solution.py:706
  48.6 11.9 %collective-permute-start.14 = (bf16[264,256]{1,0:T(8,128)(2,1)S(1)}, bf16[264,256]{1,0:T(8,128)(2,1)S(1)}, u32[]{:S(2)}, u32[]{:S(2)}) collective-permute-start(bf16[264,256]{1,0:T(8,128)(2,1)S(1)} %get-tuple-element.90), channel_id=1, source_target_pairs={{0,10},{1,11},{2,8},{3,9},{4,14},{5,15},{6,12},{7,13},{8,2},{9,3},... | collective-permute-start | bytes 405512 | tf_op jit(solution)/shard_map/ppermute | solution.py:706
  52.8 7.7 %collective-permute-start.15 = (bf16[264,256]{1,0:T(8,128)(2,1)S(1)}, bf16[264,256]{1,0:T(8,128)(2,1)S(1)}, u32[]{:S(2)}, u32[]{:S(2)}) collective-permute-start(bf16[264,256]{1,0:T(8,128)(2,1)S(1)} %get-tuple-element.91), channel_id=1, source_target_pairs={{0,12},{1,13},{2,14},{3,15},{4,8},{5,9},{6,10},{7,11},{8,4},{9,5},... | collective-permute-start | bytes 405512 | tf_op jit(solution)/shard_map/ppermute | solution.py:706
  52.8 7.7 %collective-permute-start.16 = (bf16[264,256]{1,0:T(8,128)(2,1)S(1)}, bf16[264,256]{1,0:T(8,128)(2,1)S(1)}, u32[]{:S(2)}, u32[]{:S(2)}) collective-permute-start(bf16[264,256]{1,0:T(8,128)(2,1)S(1)} %get-tuple-element.92), channel_id=1, source_target_pairs={{0,14},{1,15},{2,12},{3,13},{4,10},{5,11},{6,8},{7,9},{8,6},{9,7},... | collective-permute-start | bytes 405512 | tf_op jit(solution)/shard_map/ppermute | solution.py:706
  55.7 4.9 %copy-start.2 = (bf16[8,264,256]{2,1,0:T(8,128)(2,1)S(1)}, bf16[8,264,256]{2,1,0:T(8,128)(2,1)}, u32[]{:S(2)}) copy-start(bf16[8,264,256]{2,1,0:T(8,128)(2,1)} %get-tuple-element.84.first_ref) | copy-start | bytes 3244036
  55.7 5.7 %copy-start = (bf16[512,2560]{1,0:T(8,128)(2,1)S(1)}, bf16[512,2560]{1,0:T(8,128)(2,1)}, u32[]{:S(2)}) copy-start(bf16[512,2560]{1,0:T(8,128)(2,1)} %get-tuple-element.62.refs_1_) | copy-start | bytes 7864324
  60.5 1.3 %copy-start.1 = (bf16[512,1280]{1,0:T(8,128)(2,1)S(1)}, bf16[512,1280]{1,0:T(8,128)(2,1)}, u32[]{:S(2)}) copy-start(bf16[512,1280]{1,0:T(8,128)(2,1)} %get-tuple-element.61.refs_0_) | copy-start | bytes 3932164
  61.3 2.9 %collective-permute-start.17 = (bf16[8,264,256]{2,1,0:T(8,128)(2,1)S(1)}, bf16[8,264,256]{2,1,0:T(8,128)(2,1)S(1)}, u32[]{:S(2)}, u32[]{:S(2)}) collective-permute-start(bf16[8,264,256]{2,1,0:T(8,128)(2,1)S(1)} %get-tuple-element.93), channel_id=1, source_target_pairs={{0,1},{1,0},{2,3},{3,2},{4,5},{5,4},{6,7},{7,6},{8,9},{9,8},{10,11... | collective-permute-start | bytes 3244040 | tf_op jit(solution)/shard_map/ppermute | solution.py:738
  61.8 2.3 %copy-start.3 = (bf16[512,1024]{1,0:T(8,128)(2,1)S(1)}, bf16[512,1024]{1,0:T(8,128)(2,1)}, u32[]{:S(2)}) copy-start(bf16[512,1024]{1,0:T(8,128)(2,1)} %get-tuple-element.82.refs_7_) | copy-start | bytes 3145732
  61.8 2.4 %copy-start.4 = (bf16[512,512]{1,0:T(8,128)(2,1)S(1)}, bf16[512,512]{1,0:T(8,128)(2,1)}, u32[]{:S(2)}) copy-start(bf16[512,512]{1,0:T(8,128)(2,1)} %get-tuple-element.75.refs_4_) | copy-start | bytes 1572868
  61.8 2.4 %copy-start.5 = (bf16[512,512]{1,0:T(8,128)(2,1)S(1)}, bf16[512,512]{1,0:T(8,128)(2,1)}, u32[]{:S(2)}) copy-start(bf16[512,512]{1,0:T(8,128)(2,1)} %get-tuple-element.81.refs_6_) | copy-start | bytes 1572868
  61.8 2.4 %copy-start.6 = (bf16[512,256]{1,0:T(8,128)(2,1)S(1)}, bf16[512,256]{1,0:T(8,128)(2,1)}, u32[]{:S(2)}) copy-start(bf16[512,256]{1,0:T(8,128)(2,1)} %get-tuple-element.74.refs_3_) | copy-start | bytes 786436
